TPU v7x, 32 devices: a whole 2x2x4 slice. The times are simulated.
32 devices in a mesh: groups: 2 (over x), seq: 16 (over z, y, core).
Axes of the slice: x: 2, y: 2, z: 4, core: 2. Of those that a mesh axis runs over, the one named last changes fastest.
Arguments:
- values: bfloat16 [16384, 2048], P(('groups', 'seq')), parts along dimension 0, may hold values from -6 to 6
- b_proj: bfloat16 [16384, 64], P(('groups', 'seq')), parts along dimension 0, may hold values from -0.03125 to 0.03125
- c_proj: bfloat16 [16384, 64], P(('groups', 'seq')), parts along dimension 0, may hold values from -6 to 6
- step_sizes: float32 [16384, 32], P(('groups', 'seq')), parts along dimension 0, may hold values from 0.5 to 2
- decay_rates: float32 [32], replicated, may hold values from 3.0517578e-05 to 0.05
- skip_gain: float32 [32], replicated, may hold values from 0.5 to 1.5
- teacher: bfloat16 [16384, 2048], P(('groups', 'seq')), parts along dimension 0, may hold values from -6 to 6
- doc_lengths: int32 [32], P('groups'), parts along dimension 0, may hold values from 1 to 2048, 8192 in all
Outputs:
- loss: float32 [2], P('groups'), parts along dimension 0
- grad_values: float32 [16384, 2048], P(('groups', 'seq')), parts along dimension 0
- grad_b: float32 [16384, 64], P(('groups', 'seq')), parts along dimension 0
- grad_c: float32 [16384, 64], P(('groups', 'seq')), parts along dimension 0
There are 2 independent parts, one for each index of `groups`. A program takes and returns all parts, laid end to end along the dimension named above; an argument that names none is the same for every part. Nothing has to cross between parts.
Inputs may be any that keep to these rules, and one draw needn't show every extreme that they name: `doc_lengths`: the documents' lengths sum to 8192, the longest is exactly 2048.
All inputs are finite; a program needn't handle non-finite values.
Results may differ from a plain program's by a relative error of at most 0.004.
Values sent between devices are 32-bit elements; how exact they have to be, the bound alone decides.
No kernel may reach another device: no remote copies, remote signals or barrier semaphores. Data moves between devices by JAX's collectives and lax.ppermute only.
A program may use at most 128 MiB of HBM per device.

v0:
```python
import jax
import jax.numpy as jnp
from jax import lax
from jax.sharding import PartitionSpec as P

highest = lax.Precision.HIGHEST


def product(form, left, right):
    return jnp.einsum(form, left, right, preferred_element_type=jnp.float32)


def decay_terms(step_sizes, decay_rates, doc_count):
    length = step_sizes.shape[0]
    log_level = jnp.cumsum(-(step_sizes * decay_rates[None, :]), axis=0)
    last_level = log_level[-1]
    positions = jnp.arange(length, dtype=jnp.int32)
    same_doc = (doc_count[:, None] == doc_count[None, :]) & (
        positions[:, None] >= positions[None, :]
    )
    log_gap = log_level.T[:, :, None] - log_level.T[:, None, :]
    banded = jnp.where(same_doc[None], jnp.exp(jnp.minimum(log_gap, 0.0)), 0.0)
    enter_weight = jnp.where((doc_count == 0)[:, None], jnp.exp(log_level), 0.0)
    leave_weight = jnp.where(
        (doc_count == doc_count[-1])[:, None], jnp.exp(last_level[None, :] - log_level), 0.0
    )
    through_decay = jnp.where(doc_count[-1] == 0, jnp.exp(last_level), 0.0)
    return (banded, enter_weight, leave_weight, through_decay)


def forward_local(inputs, b_proj, c_proj, step_sizes, banded, leave_weight):
    scaled = (step_sizes[:, :, None] * inputs.astype(jnp.float32)).astype(jnp.bfloat16)
    scores = jnp.dot(c_proj, b_proj.T, preferred_element_type=jnp.float32)
    mixing = (banded * scores[None]).astype(jnp.bfloat16)
    inner = product("hts,shp->thp", mixing, scaled)
    local_state = jnp.einsum(
        "shp,sn->hpn",
        leave_weight[:, :, None] * scaled.astype(jnp.float32),
        b_proj.astype(jnp.float32),
        precision=highest,
    )
    return (scaled, mixing, inner, local_state)


def backward_local(
    b_proj,
    c_proj,
    step_sizes,
    skip_gain,
    banded,
    mixing,
    scaled,
    enter_weight,
    leave_weight,
    mismatch,
    state_in,
    adjoint_in,
):
    low = mismatch.astype(jnp.bfloat16)
    wide_b = b_proj.astype(jnp.float32)
    wide_c = c_proj.astype(jnp.float32)
    back_inner = product("hts,thp->shp", mixing, low)
    from_later = jnp.einsum("hpn,sn->shp", adjoint_in, wide_b, precision=highest)
    grad_values = skip_gain[None, :, None] * mismatch + step_sizes[:, :, None] * (
        back_inner + leave_weight[:, :, None] * from_later
    )
    pair_terms = product("thp,shp->hts", low, scaled)
    pair_sum = jnp.sum(banded * pair_terms, axis=0)
    grad_c = jnp.dot(pair_sum, wide_b, precision=highest, preferred_element_type=jnp.float32)
    grad_c = grad_c + jnp.einsum(
        "thp,hpn->tn", enter_weight[:, :, None] * mismatch, state_in, precision=highest
    )
    grad_b = jnp.dot(pair_sum.T, wide_c, precision=highest, preferred_element_type=jnp.float32)
    grad_b = grad_b + jnp.einsum(
        "shp,hpn->sn",
        leave_weight[:, :, None] * scaled.astype(jnp.float32),
        adjoint_in,
        precision=highest,
    )
    return (grad_values, grad_b, grad_c)


def pair_combine(earlier, later):
    return (earlier[0] * later[0], later[0][..., None] * earlier[1] + later[1])


def carried(through_decay, state, backward, head_dim):
    heads, _, width = state.shape
    row_decay = jnp.repeat(through_decay, head_dim)
    rows = state.reshape(heads * head_dim, width)
    devices = lax.axis_size("seq")
    piece = rows.shape[0] // devices
    moved = (
        lax.all_to_all(row_decay, "seq", split_axis=0, concat_axis=0, tiled=True),
        lax.all_to_all(rows, "seq", split_axis=0, concat_axis=0, tiled=True),
    )
    decays = moved[0].reshape(devices, piece)
    blocks = moved[1].reshape(devices, piece, width)
    if backward:
        decays = jnp.flip(decays, 0)
        blocks = jnp.flip(blocks, 0)
    inclusive = lax.associative_scan(pair_combine, (decays, blocks), axis=0)
    shifted = jnp.concatenate([jnp.zeros_like(blocks[:1]), inclusive[1][:-1]], axis=0)
    if backward:
        shifted = jnp.flip(shifted, 0)
    prefix = lax.all_to_all(
        shifted.reshape(devices * piece, width), "seq", split_axis=0, concat_axis=0, tiled=True
    )
    return prefix.reshape(heads, head_dim, width)


def local(values, b_proj, c_proj, step_sizes, decay_rates, skip_gain, teacher, doc_lengths):
    length = values.shape[0]
    heads = step_sizes.shape[1]
    head_dim = values.shape[1] // heads
    inputs = values.reshape(length, heads, head_dim)
    first_row = lax.axis_index("seq") * length
    positions = first_row + jnp.arange(length, dtype=jnp.int32)
    doc_starts = jnp.cumsum(doc_lengths) - doc_lengths
    flags = jnp.any(positions[:, None] == doc_starts[None, :], axis=1).astype(jnp.int32)
    doc_count = jnp.cumsum(flags)
    banded, enter_weight, leave_weight, through_decay = decay_terms(
        step_sizes, decay_rates, doc_count
    )
    scaled, mixing, inner, local_state = forward_local(
        inputs, b_proj, c_proj, step_sizes, banded, leave_weight
    )
    state_in = carried(through_decay, local_state, False, head_dim)
    wide_c = c_proj.astype(jnp.float32)
    output = inner + enter_weight[:, :, None] * jnp.einsum(
        "hpn,tn->thp", state_in, wide_c, precision=highest
    )
    output = output + skip_gain[None, :, None] * inputs.astype(jnp.float32)
    mismatch = output - teacher.astype(jnp.float32).reshape(length, heads, head_dim)
    total = lax.psum(jnp.sum(mismatch * mismatch), "seq")
    loss = (total / (lax.axis_size("seq") * length * heads * head_dim)).reshape(1)
    back_local = jnp.einsum(
        "thp,tn->hpn", enter_weight[:, :, None] * mismatch, wide_c, precision=highest
    )
    adjoint_in = carried(through_decay, back_local, True, head_dim)
    grad_values, grad_b, grad_c = backward_local(
        b_proj,
        c_proj,
        step_sizes,
        skip_gain,
        banded,
        mixing,
        scaled,
        enter_weight,
        leave_weight,
        mismatch,
        state_in,
        adjoint_in,
    )
    return (loss, grad_values.reshape(length, heads * head_dim), grad_b, grad_c)


def solution(mesh):
    in_specs = (
        P(("groups", "seq"), None),
        P(("groups", "seq"), None),
        P(("groups", "seq"), None),
        P(("groups", "seq"), None),
        P(),
        P(),
        P(("groups", "seq"), None),
        P("groups"),
    )
    out_specs = (
        P("groups"),
        P(("groups", "seq"), None),
        P(("groups", "seq"), None),
        P(("groups", "seq"), None),
    )
    return jax.shard_map(local, mesh=mesh, in_specs=in_specs, out_specs=out_specs, check_vma=False)
```

profile of v0, /device:TPU:0, one launch (start us, length us, event | category | flops | bytes accessed | tf_op | source)
XLA Modules:
  0.0 218.5 jit_solution(14924940138193530595)
XLA Ops:
  0.7 0.8 copy.74
  1.6 0.7 sub.29
  2.4 0.3 reduce-window.31
  3.0 0.6 slice.222
  4.2 0.9 copy_bitcast_fusion.1
  5.1 1.2 reduce-window.33
  6.5 0.7 copy_bitcast_fusion
  7.6 0.7 broadcast_in_dim.42
  8.3 7.4 %all-to-all-start.1 = ((f32[16,128,1]{1,2,0:T(1,128)}), f32[16,128,1]{1,2,0:T(1,128)S(1)}, u32[]{:S(2)}, u32[]{:S(2)}) async-start(f32[16,128,1]{1,2,0:T(1,128)} %broadcast_in_dim.42), calls=%async_computation.1 | async-start | bytes 16384 | tf_op jit(solution)/shard_map/all_to_all | solution.py:94
  15.7 0.7 broadcast_compare_fusion
  16.3 4.1 %copy.73 = f32[512,2048]{0,1:T(8,128)} copy(bf16[512,2048]{1,0:T(8,128)(2,1)} %param.8) | data formatting | bytes 6291456 | tf_op jit(solution)/shard_map/convert_element_type | solution.py:32
  20.5 0.7 exponential_select_fusion.2
  21.2 3.1 %convert_multiply_fusion = f32[512,32,64]{0,2,1:T(8,128)S(1)} fusion(f32[512,32]{0,1:T(8,128)S(1)} %get-tuple-element.41, f32[512,32]{0,1:T(8,128)S(1)} %copy-done.12, f32[512,2048]{0,1:T(8,128)} %copy.73), kind=kLoop, calls=%fused_computation.18 | loop fusion | flops 4194304 | bytes 8519680 | tf_op jit(solution)/shard_map/mul | solution.py:38
  24.3 3.1 %fusion.37 = f32[16,128,64]{1,2,0:T(8,128)} fusion(f32[16,128,512]{2,1,0:T(8,128)S(1)} %bitcast.101, bf16[512,64]{0,1:T(8,128)(2,1)S(1)} %copy-done), kind=kOutput, calls=%fused_computation.70 | convolution fusion | flops 805306368 | bytes 4784128 | tf_op jit(solution)/shard_map/shp,sn->hpn/dot_general | solution.py:36
  27.4 6.0 %all-to-all-start = ((f32[16,128,64]{1,2,0:T(8,128)}), f32[16,128,64]{1,2,0:T(8,128)S(1)}, u32[]{:S(2)}, u32[]{:S(2)}) async-start(f32[16,128,64]{1,2,0:T(8,128)} %fusion.37), calls=%async_computation | async-start | bytes 1048576 | tf_op jit(solution)/shard_map/all_to_all | solution.py:95
  33.6 0.6 slice.225
  34.2 13.7 %all-to-all-done = f32[16,128,64]{1,2,0:T(8,128)S(1)} async-done(((f32[16,128,64]{1,2,0:T(8,128)}), f32[16,128,64]{1,2,0:T(8,128)S(1)}, u32[]{:S(2)}, u32[]{:S(2)}) %all-to-all-start) | async-done | bytes 524320 | tf_op jit(solution)/shard_map/all_to_all | solution.py:95
  47.9 0.6 slice.287
  48.8 0.9 pad_maximum_fusion.2
  49.8 0.7 fusion.30
  50.9 0.8 concatenate.27
  51.7 4.5 %all-to-all-start.2 = ((f32[16,128,64]{1,2,0:T(8,128)}), f32[16,128,64]{1,2,0:T(8,128)S(1)}, u32[]{:S(2)}, u32[]{:S(2)}) async-start(f32[16,128,64]{1,2,0:T(8,128)} %concatenate.27), calls=%async_computation.2 | async-start | bytes 1048576 | tf_op jit(solution)/shard_map/all_to_all | solution.py:106
  56.2 2.9 %copy.79 = f32[512,2048]{0,1:T(8,128)} copy(bf16[512,2048]{1,0:T(8,128)(2,1)S(1)} %copy-done.7) | data formatting | bytes 6291456 | tf_op jit(solution)/shard_map/reshape | solution.py:134
  59.4 0.3 fusion.53
  59.8 10.9 %all-to-all-done.2 = f32[16,128,64]{1,2,0:T(8,128)S(1)} async-done(((f32[16,128,64]{1,2,0:T(8,128)}), f32[16,128,64]{1,2,0:T(8,128)S(1)}, u32[]{:S(2)}, u32[]{:S(2)}) %all-to-all-start.2) | async-done | bytes 524320 | tf_op jit(solution)/shard_map/all_to_all | solution.py:106
  70.7 0.3 copy.77
  71.2 2.3 %fusion.24 = f32[32,64,512]{2,1,0:T(8,128)S(1)} fusion(f32[32,64,64]{1,0,2:T(8,128)S(1)} %reshape.268, bf16[512,64]{0,1:T(8,128)(2,1)S(1)} %copy-done.10), kind=kOutput, calls=%fused_computation.34 | convolution fusion | flops 805306368 | bytes 4784128 | tf_op jit(solution)/shard_map/hpn,tn->thp/dot_general | solution.py:130
  73.5 13.3 %multiply_reduce_fusion.1 = (f32[]{:T(128)}, f32[512,32,64]{0,2,1:T(8,128)S(1)}) fusion(f32[512,32,64]{0,2,1:T(8,128)} %bitcast.104, f32[512,32,64]{0,2,1:T(8,128)S(1)} %bitcast.100, f32[32]{0:T(128)S(1)} %copy-done.18, f32[32,64,512]{2,1,0:T(8,128)S(1)} %fusion.24, f32[512,32]{0,1:T(8,128)S(1)} %copy-done.11, f32[512,512]{1,0:T(8,128)S(1)} %fusion.53, ...), kind=kOutput, calls=%fused_computation.17 | convolution fusion | flops 1125122048 | bytes 18284676 | tf_op jit(solution)/shard_map/hts,shp->thp/dot_general | solution.py:10
  86.8 2.0 copy-done.2
  88.8 2.1 fusion.13
  90.9 1.1 copy.80
  92.1 14.6 %all-to-all-start.3 = ((f32[16,128,64]{1,2,0:T(8,128)}), f32[16,128,64]{1,2,0:T(8,128)S(1)}, u32[]{:S(2)}, u32[]{:S(2)}) async-start(f32[16,128,64]{1,2,0:T(8,128)} %copy.80), calls=%async_computation.3 | async-start | bytes 1048576 | tf_op jit(solution)/shard_map/all_to_all | solution.py:95
  106.6 2.5 %mul.245 = f32[512,32,64]{0,2,1:T(8,128)} broadcast(f32[512,32]{0,1:T(8,128)S(1)} %get-tuple-element.41), dimensions={0,1} | broadcast | bytes 4259840 | tf_op jit(solution)/shard_map/mul | solution.py:38
  109.2 5.4 %copy.83 = f32[512,2048]{1,0:T(8,128)} copy(f32[512,2048]{0,1:T(8,128)} %bitcast.102) | data formatting | bytes 8388608 | tf_op jit(solution)/shard_map/mul | solution.py:38
  114.6 2.5 %mul.237 = f32[512,32,64]{0,2,1:T(8,128)} broadcast(f32[512,32]{0,1:T(8,128)S(1)} %copy-done.13), dimensions={0,1} | broadcast | bytes 4259840 | tf_op jit(solution)/shard_map/mul | solution.py:32
  117.0 5.4 %copy.82 = f32[512,2048]{1,0:T(8,128)} copy(f32[512,2048]{0,1:T(8,128)} %bitcast.103) | data formatting | bytes 8388608 | tf_op jit(solution)/shard_map/mul | solution.py:32
  123.6 0.8 rev.7
  124.4 6.1 %all-to-all-start.4 = ((f32[16,128,64]{1,2,0:T(8,128)}), f32[16,128,64]{1,2,0:T(8,128)S(1)}, u32[]{:S(2)}, u32[]{:S(2)}) async-start(f32[16,128,64]{1,2,0:T(8,128)} %rev.7), calls=%async_computation.4 | async-start | bytes 1048576 | tf_op jit(solution)/shard_map/all_to_all | solution.py:106
  130.6 15.1 %multiply_reduce_fusion = f32[512,512]{1,0:T(8,128)S(1)} fusion(f32[32,512]{1,0:T(8,128)S(1)} %copy-done.15, pred[512,512]{1,0:T(8,128)(4,1)S(1)} %fusion.23, f32[512,32,64]{0,2,1:T(8,128)} %bitcast.99, f32[512,32]{0,1:T(8,128)S(1)} %copy-done.13, f32[512,32,64]{0,2,1:T(8,128)} %copy-done.2), kind=kOutput, calls=%fused_computation | convolution fusion | flops 1118568448 | bytes 9830400 | tf_op jit(solution)/shard_map/thp,shp->hts/dot_general | solution.py:10
  145.6 34.5 %psum.7 = f32[]{:T(128)} all-reduce(f32[]{:T(128)} %get-tuple-element.46), channel_id=1, replica_groups=mesh['groups'=2,'seq'=16] {'seq'}, use_global_device_ids=true, to_apply=%region_7.8 | all-reduce | flops 1 | bytes 8 | tf_op jit(solution)/shard_map/psum | solution.py:135
  180.8 5.2 %fusion.17 = f32[512,64]{0,1:T(8,128)S(1)} fusion(f32[512,32,64]{0,2,1:T(8,128)} %copy-done.2, f32[512,32]{0,1:T(8,128)S(1)} %copy-done.11, f32[32,64,64]{1,0,2:T(8,128)S(1)} %reshape.268), kind=kOutput, calls=%fused_computation.26 | convolution fusion | flops 806354944 | bytes 4915200 | tf_op jit(solution)/shard_map/thp,hpn->tn/dot_general | solution.py:70
  186.0 1.3 convolution_add_fusion
  187.4 0.3 copy.81
  187.7 1.9 fusion.35
  190.2 12.2 %fusion.4 = f32[512,32,64]{0,2,1:T(8,128)} fusion(f32[32,64,512]{2,1,0:T(8,128)S(1)} %fusion.35, f32[512,32,64]{0,2,1:T(8,128)S(1)} %copy-done.3, f32[512,512]{1,0:T(8,128)S(1)} %copy-done.9, f32[32,512]{1,0:T(8,128)S(1)} %copy-done.15, pred[512,512]{1,0:T(8,128)(4,1)S(1)} %fusion.23, f32[32]{0:T(128)S(1)} %copy-done.19, ...), kind=kOutput, calls=%fused_computation.8 | convolution fusion | flops 1121976320 | bytes 14090368 | tf_op jit(solution)/shard_map/hts,thp->shp/dot_general | solution.py:10
  202.4 5.5 %copy.86 = f32[512,2048]{1,0:T(8,128)} copy(f32[512,2048]{0,1:T(8,128)} %bitcast.105) | data formatting | bytes 8388608
  207.9 8.0 %fusion.8 = f32[512,64]{0,1:T(8,128)S(1)} fusion(f32[512,2048]{1,0:T(8,128)} %copy.83, f32[512,2048]{1,0:T(8,128)} %copy.82, bf16[512,2048]{1,0:T(8,128)(2,1)S(1)} %copy-done.4, f32[16,128,64]{1,2,0:T(8,128)S(1)} %all-to-all-done.4), kind=kOutput, calls=%fused_computation.13 | convolution fusion | flops 810549248 | bytes 11141120 | tf_op jit(solution)/shard_map/shp,hpn->sn/dot_general | solution.py:74
  216.0 1.2 convolution_add_fusion.1
  (129 shorter events, 3.9 us)
Async XLA Ops:
  0.6 23.7 %copy-start = (bf16[512,64]{0,1:T(8,128)(2,1)S(1)}, bf16[512,64]{0,1:T(8,128)(2,1)}, u32[]{:S(2)}) copy-start(bf16[512,64]{0,1:T(8,128)(2,1)} %param.9) | copy-start | bytes 196612
  0.6 20.6 %copy-start.12 = (f32[512,32]{0,1:T(8,128)S(1)}, f32[512,32]{0,1:T(8,128)}, u32[]{:S(2)}) copy-start(f32[512,32]{0,1:T(8,128)} %param.11) | copy-start | bytes 196612
  3.0 21.3 %copy-start.16 = (s32[512]{0:T(512)}, s32[512]{0:T(512)S(1)}, u32[]{:S(2)}) copy-start(s32[512]{0:T(512)S(1)} %get-tuple-element.31) | copy-start | bytes 6148
  8.3 19.1 %all-to-all-start.1 = ((f32[16,128,1]{1,2,0:T(1,128)}), f32[16,128,1]{1,2,0:T(1,128)S(1)}, u32[]{:S(2)}, u32[]{:S(2)}) async-start(f32[16,128,1]{1,2,0:T(1,128)} %broadcast_in_dim.42), calls=%async_computation.1 | async-start | bytes 16384 | tf_op jit(solution)/shard_map/all_to_all | solution.py:94
  27.4 20.5 %all-to-all-start = ((f32[16,128,64]{1,2,0:T(8,128)}), f32[16,128,64]{1,2,0:T(8,128)S(1)}, u32[]{:S(2)}, u32[]{:S(2)}) async-start(f32[16,128,64]{1,2,0:T(8,128)} %fusion.37), calls=%async_computation | async-start | bytes 1048576 | tf_op jit(solution)/shard_map/all_to_all | solution.py:95
  48.7 7.5 %copy-start.7 = (bf16[512,2048]{1,0:T(8,128)(2,1)S(1)}, bf16[512,2048]{1,0:T(8,128)(2,1)}, u32[]{:S(2)}) copy-start(bf16[512,2048]{1,0:T(8,128)(2,1)} %param.14) | copy-start | bytes 6291460
  50.9 8.3 %copy-start.17 = (s32[512]{0:T(512)S(1)}, s32[512]{0:T(512)}, u32[]{:S(2)}) copy-start(s32[512]{0:T(512)} %copy-done.16) | copy-start | bytes 6148
  50.9 8.5 %copy-start.10 = (bf16[512,64]{0,1:T(8,128)(2,1)S(1)}, bf16[512,64]{0,1:T(8,128)(2,1)}, u32[]{:S(2)}) copy-start(bf16[512,64]{0,1:T(8,128)(2,1)} %param.10) | copy-start | bytes 196612
  51.7 18.9 %all-to-all-start.2 = ((f32[16,128,64]{1,2,0:T(8,128)}), f32[16,128,64]{1,2,0:T(8,128)S(1)}, u32[]{:S(2)}, u32[]{:S(2)}) async-start(f32[16,128,64]{1,2,0:T(8,128)} %concatenate.27), calls=%async_computation.2 | async-start | bytes 1048576 | tf_op jit(solution)/shard_map/all_to_all | solution.py:106
  59.7 27.1 %copy-start.8 = (f32[512,512]{1,0:T(8,128)}, f32[512,512]{1,0:T(8,128)S(1)}, u32[]{:S(2)}) copy-start(f32[512,512]{1,0:T(8,128)S(1)} %fusion.53) | copy-start | bytes 3145732
  59.7 13.7 %copy-start.11 = (f32[512,32]{0,1:T(8,128)S(1)}, f32[512,32]{0,1:T(8,128)}, u32[]{:S(2)}) copy-start(f32[512,32]{0,1:T(8,128)} %get-tuple-element.40) | copy-start | bytes 196612
  59.7 13.7 %copy-start.13 = (f32[512,32]{0,1:T(8,128)S(1)}, f32[512,32]{0,1:T(8,128)}, u32[]{:S(2)}) copy-start(f32[512,32]{0,1:T(8,128)} %param.11) | copy-start | bytes 196612
  59.7 13.7 %copy-start.14 = (f32[32,512]{1,0:T(8,128)S(1)}, f32[32,512]{1,0:T(8,128)}, u32[]{:S(2)}) copy-start(f32[32,512]{1,0:T(8,128)} %get-tuple-element.42) | copy-start | bytes 196612
  59.8 13.7 %copy-start.18 = (f32[32]{0:T(128)S(1)}, f32[32]{0:T(128)}, u32[]{:S(2)}) copy-start(f32[32]{0:T(128)} %param.13) | copy-start | bytes 388
  71.2 2.3 %copy-start.1 = (f32[512,2048]{0,1:T(8,128)S(1)}, f32[512,2048]{0,1:T(8,128)}, u32[]{:S(2)}) copy-start(f32[512,2048]{0,1:T(8,128)} %copy.73) | copy-start | bytes 12582916
  86.8 2.0 copy-start.2
  92.1 30.6 %all-to-all-start.3 = ((f32[16,128,64]{1,2,0:T(8,128)}), f32[16,128,64]{1,2,0:T(8,128)S(1)}, u32[]{:S(2)}, u32[]{:S(2)}) async-start(f32[16,128,64]{1,2,0:T(8,128)} %copy.80), calls=%async_computation.3 | async-start | bytes 1048576 | tf_op jit(solution)/shard_map/all_to_all | solution.py:95
  123.2 7.4 %copy-start.15 = (f32[32,512]{1,0:T(8,128)S(1)}, f32[32,512]{1,0:T(8,128)}, u32[]{:S(2)}) copy-start(f32[32,512]{1,0:T(8,128)} %get-tuple-element.42) | copy-start | bytes 196612
  124.4 62.9 %all-to-all-start.4 = ((f32[16,128,64]{1,2,0:T(8,128)}), f32[16,128,64]{1,2,0:T(8,128)S(1)}, u32[]{:S(2)}, u32[]{:S(2)}) async-start(f32[16,128,64]{1,2,0:T(8,128)} %rev.7), calls=%async_computation.4 | async-start | bytes 1048576 | tf_op jit(solution)/shard_map/all_to_all | solution.py:106
  145.6 42.1 %copy-start.5 = (f32[512,512]{1,0:T(8,128)}, f32[512,512]{1,0:T(8,128)S(1)}, u32[]{:S(2)}) copy-start(f32[512,512]{1,0:T(8,128)S(1)} %multiply_reduce_fusion) | copy-start | bytes 3145732
  186.0 3.6 %copy-start.19 = (f32[32]{0:T(128)S(1)}, f32[32]{0:T(128)}, u32[]{:S(2)}) copy-start(f32[32]{0:T(128)} %param.13) | copy-start | bytes 388
  187.7 2.2 %copy-start.3 = (f32[512,32,64]{0,2,1:T(8,128)S(1)}, f32[512,32,64]{0,2,1:T(8,128)}, u32[]{:S(2)}) copy-start(f32[512,32,64]{0,2,1:T(8,128)} %copy-done.2) | copy-start | bytes 12582916
  187.7 2.5 %copy-start.9 = (f32[512,512]{1,0:T(8,128)S(1)}, f32[512,512]{1,0:T(8,128)}, u32[]{:S(2)}) copy-start(f32[512,512]{1,0:T(8,128)} %copy-done.8) | copy-start | bytes 3145732
  202.4 5.5 %copy-start.4 = (bf16[512,2048]{1,0:T(8,128)(2,1)S(1)}, bf16[512,2048]{1,0:T(8,128)(2,1)}, u32[]{:S(2)}) copy-start(bf16[512,2048]{1,0:T(8,128)(2,1)} %param.8) | copy-start | bytes 6291460
  207.9 8.0 %copy-start.6 = (f32[512,512]{1,0:T(8,128)S(1)}, f32[512,512]{1,0:T(8,128)}, u32[]{:S(2)}) copy-start(f32[512,512]{1,0:T(8,128)} %copy-done.5) | copy-start | bytes 3145732
where the time goes:
time: 219 us; the launch traced here: 218 us
  matrix products  65.9 us (30%)
  local copies, waits for them, and re-layouts  39.6 us (18%)
  starting transfers between devices  38.5 us (18%)
  blocking collectives  34.5 us (16%)
  waiting for transfers between devices  24.6 us (11%)
  other arithmetic  11.2 us (5%)
  between operations  4.05 us (2%)
    dot_general x3, matrix products, product(): return jnp.einsum(form, left, right, preferred_element_type=jnp.float32)  40.6 us
    psum x1, blocking collectives, local(): total = lax.psum(jnp.sum(mismatch * mismatch), 'seq')  34.5 us
    all_to_all x2, starting transfers between devices, carried(): lax.all_to_all(rows, 'seq', split_axis=0, concat_axis=0, tiled=True)  20.6 us
    all_to_all x2, waiting for transfers between devices, carried(): lax.all_to_all(rows, 'seq', split_axis=0, concat_axis=0, tiled=True)  13.7 us
    all_to_all x2, waiting for transfers between devices, carried(): lax.all_to_all(shifted.reshape(devices * piece, width), 'seq', split_axis...  10.9 us
    all_to_all x2, starting transfers between devices, carried(): lax.all_to_all(shifted.reshape(devices * piece, width), 'seq', split_axis...  10.6 us
    unnamed x43, local copies, waits for them, and re-layouts  8.38 us
    dot_general x1, matrix products, backward_local(): jnp.einsum('shp,hpn->sn', leave_weight[:, :, None] * scaled.astype(jnp.fl...  8.03 us
  transfers between devices with their start and end apart: 5, of which 2 were waited for; matrix products, arithmetic and copies ran while one was open for 24% of the time, Pallas kernels for 0%

commit v1 on v0

v1 whole, which is shorter than its diff:
```python
import functools
import jax
import jax.numpy as jnp
from jax import lax
from jax.experimental import pallas as pl
from jax.experimental.pallas import tpu as pltpu
from jax.sharding import PartitionSpec as P

F32 = jnp.float32
BF16 = jnp.bfloat16
PAD = 8
CHUNK = 512
LIMIT = 40 << 20


def dot(a, b):
    return jnp.dot(a, b, preferred_element_type=F32)


def dot_nt(a, b):
    return lax.dot_general(a, b, (((1,), (1,)), ((), ())), preferred_element_type=F32)


def iota(shape, axis):
    return lax.broadcasted_iota(jnp.int32, shape, axis)


def split3(x):
    hi = x.astype(BF16)
    rest = x - hi.astype(F32)
    mid = rest.astype(BF16)
    lo = (rest - mid.astype(F32)).astype(BF16)
    return jnp.concatenate([hi, mid, lo], axis=1)


def split2_rows(x):
    hi = x.astype(BF16)
    lo = (x - hi.astype(F32)).astype(BF16)
    return jnp.concatenate([hi, lo], axis=0)


def expander(heads, head_dim, width, chunk):
    rows = lax.rem(iota((3 * heads, width), 0), heads)
    cols = iota((3 * heads, width), 1) // head_dim + chunk * (width // head_dim)
    return (rows == cols).astype(F32).astype(BF16)


def doc_ids(info, docs, length, axis):
    shape = (length, 1) if axis == 0 else (1, length)
    place = iota(shape, axis)
    ids = jnp.zeros(shape, jnp.int32)
    before = jnp.int32(0)
    final = jnp.int32(0)
    start = -info[0]
    for d in range(docs):
        ids = ids + (place >= start).astype(jnp.int32)
        before = before + (start <= -1).astype(jnp.int32)
        final = final + (start <= length - 1).astype(jnp.int32)
        start = start + info[2 + d]
    return ids, before, final


def same_doc(info, docs, length):
    col = doc_ids(info, docs, length, 0)[0]
    row = doc_ids(info, docs, length, 1)[0]
    return (col == row) & (iota((length, length), 0) >= iota((length, length), 1))


def put_half(info, j, per_half, keep_ref, send_ref, state, decay):
    width = state.shape[1]
    rows = state.shape[0]
    place = pl.ds(pl.multiple_of(lax.rem(j, per_half) * width, width), width)
    mine = j // per_half == info[1]

    def put(ref):
        ref[0:rows, place] = state
        ref[rows : rows + PAD, place] = jnp.broadcast_to(decay, (PAD, width))

    pl.when(mine)(lambda: put(keep_ref))
    pl.when(jnp.logical_not(mine))(lambda: put(send_ref))


def get_half(info, j, per_half, mine_ref, other_ref, width):
    place = pl.ds(pl.multiple_of(lax.rem(j, per_half) * width, width), width)
    own = (j // per_half == info[1]).astype(F32)
    return jnp.where(own > 0.5, mine_ref[:, place], other_ref[:, place])


def prepare_kernel(
    docs,
    info,
    v_ref,
    b_ref,
    c_ref,
    step_ref,
    rate_ref,
    gain_ref,
    x_ref,
    keep_ref,
    send_ref,
    enter3_ref,
    sf3_ref,
    rows_ref,
    bm_ref,
    cm_ref,
    f3,
    s3,
    r3,
    bt,
):
    j = pl.program_id(0)
    length, heads = step_ref.shape
    width = v_ref.shape[1]
    head_dim = width * pl.num_programs(0) // heads

    @pl.when(j == 0)
    def _():
        step = step_ref[...]
        lower = (iota((length, length), 0) >= iota((length, length), 1)).astype(F32).astype(BF16)
        sums = dot(lower, split3(-(step * rate_ref[...])))
        level = sums[:, :heads] + sums[:, heads : 2 * heads] + sums[:, 2 * heads :]
        middle = level[length // 2 - 1 : length // 2, :]
        last = level[length - 1 : length, :]
        ids, before, final = doc_ids(info, docs, length, 0)
        leave = jnp.exp(middle - level)
        enter3_ref[...] = split3(jnp.exp(level - middle))
        f3[...] = split3(leave)
        s3[...] = split3(step)
        sf3_ref[...] = split3(step * leave)
        through = jnp.where(before == final, jnp.exp(last), 0.0)
        pick = iota((PAD, heads), 0)
        table = jnp.where(pick == 0, jnp.exp(middle), 0.0)
        table = jnp.where(pick == 1, jnp.exp(last - middle), table)
        table = jnp.where(pick == 2, through, table)
        table = jnp.where(pick == 3, gain_ref[...], table)
        r3[...] = split3(table)
        bm = jnp.where(ids == final, b_ref[...].astype(F32), 0.0)
        bm_ref[...] = bm.astype(BF16)
        bt[...] = bm.T.astype(BF16)
        cm_ref[...] = jnp.where(ids == before, c_ref[...].astype(F32), 0.0).astype(BF16)

    spread = expander(heads, head_dim, width, j)
    rows = dot(r3[...], spread)
    rows_ref[...] = rows
    scaled = (dot(s3[...], spread) * v_ref[...].astype(F32)).astype(BF16).astype(F32)
    x = dot(f3[...], spread) * scaled
    hi = x.astype(BF16)
    lo = (x - hi.astype(F32)).astype(BF16)
    x_ref[...] = hi
    state = (dot(bt[...], hi) + dot(bt[...], lo)) * rows[1:2, :]
    put_half(info, j, pl.num_programs(0) // 2, keep_ref, send_ref, state, rows[2:3, :])


def inner_kernel(docs, info, x_ref, v_ref, teach_ref, b_ref, c_ref, enter3_ref, rows_ref, base_ref, st_ref, s):
    j = pl.program_id(0)
    length = x_ref.shape[0]
    width = x_ref.shape[1]
    heads = enter3_ref.shape[1] // 3
    head_dim = width * pl.num_programs(0) // heads

    @pl.when(j == 0)
    def _():
        scores = jnp.where(same_doc(info, docs, length), dot_nt(c_ref[...], b_ref[...]), 0.0)
        s[...] = scores.astype(BF16)
        st_ref[...] = scores.T.astype(BF16)

    enter = dot(enter3_ref[...], expander(heads, head_dim, width, j))
    base_ref[...] = (
        enter * dot(s[...], x_ref[...])
        + rows_ref[3:4, :] * v_ref[...].astype(F32)
        - teach_ref[...].astype(F32)
    )


def mismatch_kernel(
    info, base_ref, enter3_ref, rows_ref, cm_ref, mine_ref, other_ref, mm_ref, y_ref, keep_ref, send_ref, loss_ref, ct
):
    j = pl.program_id(0)
    length, width = base_ref.shape
    heads = enter3_ref.shape[1] // 3
    head_dim = width * pl.num_programs(0) // heads
    per_half = pl.num_programs(0) // 2

    @pl.when(j == 0)
    def _():
        ct[...] = cm_ref[...].astype(F32).T.astype(BF16)
        loss_ref[...] = jnp.zeros_like(loss_ref)

    enter = dot(enter3_ref[...], expander(heads, head_dim, width, j))
    state = split2_rows(get_half(info, j, per_half, mine_ref, other_ref, width) * rows_ref[0:1, :])
    cm = cm_ref[...]
    mm = base_ref[...] + enter * dot(jnp.concatenate([cm, cm], axis=1), state)
    mm_ref[...] = mm
    y = (enter * mm).astype(BF16)
    y_ref[...] = y
    loss_ref[...] += jnp.sum((mm * mm).reshape(length // 8, 8, width), axis=0)
    put_half(info, j, per_half, keep_ref, send_ref, dot(ct[...], y) * rows_ref[0:1, :], rows_ref[2:3, :])


def pair_kernel(
    docs,
    info,
    mm_ref,
    y_ref,
    x_ref,
    st_ref,
    sf3_ref,
    rows_ref,
    b_ref,
    c_ref,
    mine_ref,
    other_ref,
    g_ref,
    gb_ref,
    gc_ref,
    pair,
    acc,
):
    j = pl.program_id(0)
    length, width = mm_ref.shape
    heads = sf3_ref.shape[1] // 3
    head_dim = width * pl.num_programs(0) // heads
    width_n = b_ref.shape[1]

    @pl.when(j == 0)
    def _():
        pair[...] = jnp.zeros_like(pair)
        acc[...] = jnp.zeros_like(acc)

    y = y_ref[...]
    pair[...] += dot_nt(y, x_ref[...])
    sf = dot(sf3_ref[...], expander(heads, head_dim, width, j))
    g_ref[...] = rows_ref[3:4, :] * mm_ref[...] + sf * dot(st_ref[...], y)
    state = get_half(info, j, pl.num_programs(0) // 2, mine_ref, other_ref, width) * rows_ref[0:1, :]
    acc[...] += dot_nt(y, split2_rows(state))

    @pl.when(j == pl.num_programs(0) - 1)
    def _():
        masked = jnp.where(same_doc(info, docs, length), pair[...], 0.0)
        hi = masked.astype(BF16)
        lo = (masked - hi.astype(F32)).astype(BF16)
        turned = masked.T
        hi_t = turned.astype(BF16)
        lo_t = (turned - hi_t.astype(F32)).astype(BF16)
        ids, before, _final = doc_ids(info, docs, length, 0)
        through = acc[:, :width_n] + acc[:, width_n:]
        gc_ref[...] = dot(hi, b_ref[...]) + dot(lo, b_ref[...]) + jnp.where(ids == before, through, 0.0)
        gb_ref[...] = dot(hi_t, c_ref[...]) + dot(lo_t, c_ref[...])


def finish_kernel(
    docs, info, g_ref, x_ref, sf3_ref, rows_ref, bm_ref, gb_part_ref, mine_ref, other_ref, gv_ref, gb_ref, acc
):
    j = pl.program_id(0)
    length, width = g_ref.shape
    heads = sf3_ref.shape[1] // 3
    head_dim = width * pl.num_programs(0) // heads
    width_n = bm_ref.shape[1]

    @pl.when(j == 0)
    def _():
        acc[...] = jnp.zeros_like(acc)

    sf = dot(sf3_ref[...], expander(heads, head_dim, width, j))
    adjoint = split2_rows(
        get_half(info, j, pl.num_programs(0) // 2, mine_ref, other_ref, width) * rows_ref[1:2, :]
    )
    bm = bm_ref[...]
    gv_ref[...] = g_ref[...] + sf * dot(jnp.concatenate([bm, bm], axis=1), adjoint)
    acc[...] += dot_nt(x_ref[...], adjoint)

    @pl.when(j == pl.num_programs(0) - 1)
    def _():
        ids, _before, final = doc_ids(info, docs, length, 0)
        through = acc[:, :width_n] + acc[:, width_n:]
        gb_ref[...] = gb_part_ref[...] + jnp.where(ids == final, through, 0.0)


def call(kernel, info, ins, in_kinds, outs, out_kinds, scratch, steps, flops):
    def spec(shape, kind):
        if kind == "cols":
            return pl.BlockSpec((shape[0], shape[1] // steps), lambda j, info: (0, j))
        return pl.BlockSpec(shape, lambda j, info: (0, 0))

    size = sum(a.size * a.dtype.itemsize for a in ins) + sum(o.size * o.dtype.itemsize for o in outs)
    return pl.pallas_call(
        kernel,
        out_shape=outs,
        grid_spec=pltpu.PrefetchScalarGridSpec(
            num_scalar_prefetch=1,
            grid=(steps,),
            in_specs=[spec(a.shape, k) for a, k in zip(ins, in_kinds)],
            out_specs=[spec(o.shape, k) for o, k in zip(outs, out_kinds)],
            scratch_shapes=scratch,
        ),
        compiler_params=pltpu.CompilerParams(
            dimension_semantics=("arbitrary",), vmem_limit_bytes=LIMIT
        ),
        cost_estimate=pl.CostEstimate(flops=flops, bytes_accessed=size, transcendentals=0),
    )(info, *ins)


def swap(x, devices):
    return lax.ppermute(x, "seq", [(i, i ^ 1) for i in range(devices)])


def shift(x, by, devices):
    return lax.ppermute(
        x, "seq", [(i, i + by) for i in range(devices) if 0 <= i + by < devices]
    )


def carry(keep, send, odd, devices, way):
    rows = keep.shape[0] - PAD
    got = swap(send, devices)
    near = (odd == 0) if way == 1 else (odd == 1)
    first = jnp.where(near, keep, got)
    second = jnp.where(near, got, keep)
    first_decay = first[rows : rows + 1]
    second_decay = second[rows : rows + 1]
    both = second[:rows] + second_decay * first[:rows]
    decay = jnp.broadcast_to(first_decay * second_decay, (PAD, both.shape[1]))
    packed = jnp.concatenate([both, decay], axis=0)
    reach = max(1, devices // 8)
    one = shift(packed, 2 * way, devices)
    two = shift(packed if reach > 2 else both, 4 * way, devices)
    state = one[:rows] + one[rows : rows + 1] * two[:rows]
    if reach > 2:
        run = one[rows:] * two[rows:]
        span = 2
        while span < reach:
            more = shift(jnp.concatenate([state, run], axis=0), 2 * span * way, devices)
            state = state + run[0:1] * more[:rows]
            run = run * more[rows:]
            span *= 2
    inside = first[:rows] + first_decay * state
    mine = jnp.where(near, state, inside)
    other = swap(jnp.where(near, inside, state), devices)
    return mine, other


def local(values, b_proj, c_proj, step_sizes, decay_rates, skip_gain, teacher, doc_lengths):
    length, total = values.shape
    heads = step_sizes.shape[1]
    state = b_proj.shape[1]
    docs = doc_lengths.shape[0]
    devices = lax.axis_size("seq")
    index = lax.axis_index("seq")
    odd = lax.rem(index, 2)
    info = jnp.concatenate([jnp.stack([index * length, odd]).astype(jnp.int32), doc_lengths])
    steps = total // CHUNK
    rates = decay_rates.reshape(1, heads)
    gains = skip_gain.reshape(1, heads)

    def out(*shape, dtype=F32):
        return jax.ShapeDtypeStruct(shape, dtype)

    half = out(state + PAD, total // 2)
    thirds = out(length, 3 * heads, dtype=BF16)
    square = 2 * length * length * total
    thin = 2 * length * state * total
    x, keep, send, enter3, sf3, rows, bm, cm = call(
        functools.partial(prepare_kernel, docs),
        info,
        [values, b_proj, c_proj, step_sizes, rates, gains],
        ["cols", "all", "all", "all", "all", "all"],
        [
            out(length, total, dtype=BF16),
            half,
            half,
            thirds,
            thirds,
            out(PAD, total),
            out(length, state, dtype=BF16),
            out(length, state, dtype=BF16),
        ],
        ["cols", "all", "all", "all", "all", "cols", "all", "all"],
        [
            pltpu.VMEM((length, 3 * heads), BF16),
            pltpu.VMEM((length, 3 * heads), BF16),
            pltpu.VMEM((PAD, 3 * heads), BF16),
            pltpu.VMEM((state, length), BF16),
        ],
        steps,
        4 * thin,
    )
    base, score_t = call(
        functools.partial(inner_kernel, docs),
        info,
        [x, values, teacher, b_proj, c_proj, enter3, rows],
        ["cols", "cols", "cols", "all", "all", "all", "cols"],
        [out(length, total), out(length, length, dtype=BF16)],
        ["cols", "all"],
        [pltpu.VMEM((length, length), BF16)],
        steps,
        square,
    )
    state_mine, state_other = carry(keep, send, odd, devices, 1)
    mm, y, back_keep, back_send, squares = call(
        mismatch_kernel,
        info,
        [base, enter3, rows, cm, state_mine, state_other],
        ["cols", "all", "cols", "all", "all", "all"],
        [out(length, total), out(length, total, dtype=BF16), half, half, out(8, CHUNK)],
        ["cols", "cols", "all", "all", "all"],
        [pltpu.VMEM((state, length), BF16)],
        steps,
        4 * thin,
    )
    parts = jnp.broadcast_to(jnp.sum(squares), (devices, 128))
    parts = lax.all_to_all(parts, "seq", split_axis=0, concat_axis=0, tiled=True)
    loss = (jnp.sum(parts[:, 0]) / (devices * length * total)).reshape(1)
    g, gb_part, grad_c = call(
        functools.partial(pair_kernel, docs),
        info,
        [mm, y, x, score_t, sf3, rows, b_proj, c_proj, state_mine, state_other],
        ["cols", "cols", "cols", "all", "all", "cols", "all", "all", "all", "all"],
        [out(length, total), out(length, state), out(length, state)],
        ["cols", "all", "all"],
        [pltpu.VMEM((length, length), F32), pltpu.VMEM((length, 2 * state), F32)],
        steps,
        2 * square,
    )
    adj_mine, adj_other = carry(back_keep, back_send, odd, devices, -1)
    grad_values, grad_b = call(
        functools.partial(finish_kernel, docs),
        info,
        [g, x, sf3, rows, bm, gb_part, adj_mine, adj_other],
        ["cols", "cols", "all", "cols", "all", "all", "all", "all"],
        [out(length, total), out(length, state)],
        ["cols", "all"],
        [pltpu.VMEM((length, 2 * state), F32)],
        steps,
        4 * thin,
    )
    return loss, grad_values, grad_b, grad_c


def solution(mesh):
    rows = P(("groups", "seq"), None)
    in_specs = (rows, rows, rows, rows, P(), P(), rows, P("groups"))
    out_specs = (P("groups"), rows, rows, rows)
    return jax.shard_map(local, mesh=mesh, in_specs=in_specs, out_specs=out_specs, check_vma=False)
```

time: 219 us -> 103 us (0.47)
  matrix products: 65.9 us -> 0 us
  blocking collectives: 34.5 us -> 0 us
  Pallas kernels: 0 us -> 29 us
  starting transfers between devices: 38.5 us -> 24.8 us
  local copies, waits for them, and re-layouts: 39.6 us -> 26.7 us
  waiting for transfers between devices: 24.6 us -> 11.9 us
  other arithmetic: 11.2 us -> 6.8 us
    dot_general x12 -> x0, matrix products: 65.9 us -> none  [the longest x3 40.6 us: product(): return jnp.einsum(form, left, right, preferred_element_type=jnp.float32)]
    psum x1 -> x0, blocking collectives: 34.5 us -> none  [local(): total = lax.psum(jnp.sum(mismatch * mismatch), 'seq')]
    pallas_call x0 -> x5, Pallas kernels: none -> 29 us  [call(): pl.pallas_call(kernel, out_shape=outs, grid_spec=pltpu.PrefetchScalarGrid...]
    all_to_all x5 -> x1, starting transfers between devices: 38.5 us -> 12.8 us  [local(): lax.all_to_all(parts, 'seq', split_axis=0, concat_axis=0, tiled=True)]
    all_to_all x5 -> x1, waiting for transfers between devices: 24.6 us -> 0.01 us  [local(): lax.all_to_all(parts, 'seq', split_axis=0, concat_axis=0, tiled=True)]
    unnamed x43 -> x45, local copies, waits for them, and re-layouts: 8.38 us -> 24.6 us
    mul x8 -> x0, local copies, waits for them, and re-layouts: 15.8 us -> none  [the longest x2 7.92 us: forward_local(): step_sizes[:, :, None] * inputs.astype(jnp.float32)]
    ppermute x0 -> x8, starting transfers between devices: none -> 12 us  [the longest x4 11 us: shift(): lax.ppermute(x, 'seq', [(i, i + by) for i in range(devices) if 0 <= i + b...]
  transfers between devices with their start and end apart: 5 -> 9, of which waited for: 2 -> 5; matrix products, arithmetic and copies ran while one was open for 24% -> 7% of each run, Pallas kernels for 0% -> 12%
where the time goes in v1:
time: 103 us; the launch traced here: 102 us
  Pallas kernels  29 us (28%)
  local copies, waits for them, and re-layouts  26.7 us (26%)
  starting transfers between devices  24.8 us (24%)
  waiting for transfers between devices  11.9 us (12%)
  other arithmetic  6.8 us (7%)
  between operations  2.68 us (3%)
    pallas_call x5, Pallas kernels, call(): pl.pallas_call(kernel, out_shape=outs, grid_spec=pltpu.PrefetchScalarGrid...  29 us
    unnamed x45, local copies, waits for them, and re-layouts  24.6 us
    all_to_all x1, starting transfers between devices, local(): lax.all_to_all(parts, 'seq', split_axis=0, concat_axis=0, tiled=True)  12.8 us
    ppermute x4, starting transfers between devices, shift(): lax.ppermute(x, 'seq', [(i, i + by) for i in range(devices) if 0 <= i + b...  11 us
    ppermute x4, waiting for transfers between devices, shift(): lax.ppermute(x, 'seq', [(i, i + by) for i in range(devices) if 0 <= i + b...  8.75 us
    ppermute x4, waiting for transfers between devices, swap(): return lax.ppermute(x, 'seq', [(i, i ^ 1) for i in range(devices)])  3.11 us
    select_n x2, other arithmetic, carry(): second = jnp.where(near, got, keep)  2.07 us
  transfers between devices with their start and end apart: 9, of which 5 were waited for; matrix products, arithmetic and copies ran while one was open for 7% of the time, Pallas kernels for 12%

profile of v1, /device:TPU:0, one launch (start us, length us, event | category | flops | bytes accessed | tf_op | source)
XLA Modules:
  0.0 101.7 jit_solution(13408990321140788617)
XLA Ops:
  0.6 1.0 copy.30.b_ref
  1.6 1.0 copy.31.c_ref
  2.6 1.0 copy.32.step_ref
  3.5 0.7 pad_add_fusion.info
  4.3 1.6 %copy-done = bf16[512,2048]{1,0:T(8,128)(2,1)S(1)} copy-done((bf16[512,2048]{1,0:T(8,128)(2,1)S(1)}, bf16[512,2048]{1,0:T(8,128)(2,1)}, u32[]{:S(2)}) %copy-start) | copy-done | bytes 2097176
  5.9 0.7 copy-done.17
  6.5 0.7 copy-done.18
  7.2 6.0 %shard_map.111 = (bf16[512,2048]{1,0:T(8,128)(2,1)S(1)}, f32[72,1024]{1,0:T(8,128)S(1)}, f32[72,1024]{1,0:T(8,128)}, bf16[512,96]{1,0:T(8,128)(2,1)S(1)}, bf16[5...) custom-call(s32[18]{0:T(128)S(1)} %pad_add_fusion.info, ...), custom_call_target="tpu_custom_call" | custom-call | flops 536870912 | bytes 5374208 | tf_op jit(solution)/shard_map/pallas_call | solution.py:286
  13.2 0.7 copy-done.15
  13.8 0.5 collective-permute-start
  14.3 1.5 %collective-permute-done = f32[72,1024]{1,0:T(8,128)} collective-permute-done((f32[72,1024]{1,0:T(8,128)}, f32[72,1024]{1,0:T(8,128)}, u32[]{:S(2)}, u32[]{:S(2)}) %collective-permute-start) | collective-permute-done | bytes 294944 | tf_op jit(solution)/shard_map/ppermute | solution.py:304
  15.8 1.0 %broadcast_select_fusion.3 = (f32[72,1024]{1,0:T(8,128)S(1)}, f32[72,1024]{1,0:T(8,128)S(1)}) fusion(f32[72,1024]{1,0:T(8,128)} %collective-permute-done, f32[72,1024]{1,0:T(8,128)S(1)} %get-tuple-element.30, pred[]{:T(512)S(6)} %eq.6), kind=kLoop, calls=%fused_computation.15 | loop fusion | flops 147456 | bytes 1179649 | tf_op jit(solution)/shard_map/jit(_where)/select_n | solution.py:318
  17.0 4.9 %collective-permute-start.1 = (f32[72,1024]{1,0:T(8,128)S(1)}, f32[72,1024]{1,0:T(8,128)S(1)}, u32[]{:S(2)}, u32[]{:S(2)}) collective-permute-start(f32[72,1024]{1,0:T(8,128)S(1)} %pad_maximum_fusion), channel_id=1, source_target_pairs={{0,2},{1,3},{2,4},{3,5},{4,6},{5,7},{6,8},{7,9},{8,10},{9,11},{10,... | collective-permute-start | bytes 884744 | tf_op jit(solution)/shard_map/ppermute | solution.py:308
  21.9 3.5 %collective-permute-start.2 = (f32[64,1024]{1,0:T(8,128)S(1)}, f32[64,1024]{1,0:T(8,128)S(1)}, u32[]{:S(2)}, u32[]{:S(2)}) collective-permute-start(f32[64,1024]{1,0:T(8,128)S(1)} %slice_add_fusion.3), channel_id=1, source_target_pairs={{0,4},{1,5},{2,6},{3,7},{4,8},{5,9},{6,10},{7,11},{8,12},{9,13},{1... | collective-permute-start | bytes 786440 | tf_op jit(solution)/shard_map/ppermute | solution.py:308
  25.4 3.0 %collective-permute-done.1 = f32[72,1024]{1,0:T(8,128)S(1)} collective-permute-done((f32[72,1024]{1,0:T(8,128)S(1)}, f32[72,1024]{1,0:T(8,128)S(1)}, u32[]{:S(2)}, u32[]{:S(2)}) %collective-permute-start.1) | collective-permute-done | bytes 294944 | tf_op jit(solution)/shard_map/ppermute | solution.py:308
  28.5 2.5 %collective-permute-done.2 = f32[64,1024]{1,0:T(8,128)S(1)} collective-permute-done((f32[64,1024]{1,0:T(8,128)S(1)}, f32[64,1024]{1,0:T(8,128)S(1)}, u32[]{:S(2)}, u32[]{:S(2)}) %collective-permute-start.2) | collective-permute-done | bytes 262176 | tf_op jit(solution)/shard_map/ppermute | solution.py:308
  31.0 0.1 fusion.2
  31.2 1.6 %copy-done.7 = bf16[512,2048]{1,0:T(8,128)(2,1)S(1)} copy-done((bf16[512,2048]{1,0:T(8,128)(2,1)S(1)}, bf16[512,2048]{1,0:T(8,128)(2,1)}, u32[]{:S(2)}) %copy-start.7) | copy-done | bytes 2097176
  32.8 4.6 %shard_map.112 = (f32[512,2048]{1,0:T(8,128)S(1)}, bf16[512,512]{1,0:T(8,128)(2,1)S(1)}) custom-call(s32[18]{0:T(128)S(1)} %pad_add_fusion.info, bf16[512,2048]{1,0:T(8,128)(2,1)S(1)} %get-tuple-element.24.x_ref, bf16[512,2048]{1,0:T(8,128)(2,1)S(1)} %copy-done.1, bf16[512,2048]{1,0:T(8,128)(2,1)S(1)} %copy-done.7, bf16[512,64]{1,0:T(8,128)(2,1)S(1)} %copy.30.b_ref, ...), custom_call_target="tpu_custom_call" | custom-call | flops 1073741824 | bytes 11304960 | tf_op jit(solution)/shard_map/pallas_call | solution.py:286
  37.3 4.8 %shard_map.113 = (f32[512,2048]{1,0:T(8,128)S(1)}, bf16[512,2048]{1,0:T(8,128)(2,1)S(1)}, f32[72,1024]{1,0:T(8,128)S(1)}, f32[72,1024]{1,0:T(8,128)}, f32[8,512]{1,0:T(8,128)S(1)}) custom-call(s32[18]{0:T(128)S(1)} %pad_add_fusion.info, f32[512,2048]{1,0:T(8,128)S(1)} %get-tuple-element.27.base_ref, bf16[512,96]{1,0:T(8,128)(2,1)S(1)} %get-tuple-element.25.enter3_ref, ...), custom_call_target="tpu_custom_call" | custom-call | flops 536870912 | bytes 11845632 | tf_op jit(solution)/shard_map/pallas_call | solution.py:286
  42.2 2.0 %copy-done.2 = f32[512,2048]{1,0:T(8,128)} copy-done((f32[512,2048]{1,0:T(8,128)}, f32[512,2048]{1,0:T(8,128)S(1)}, u32[]{:S(2)}) %copy-start.2) | copy-done | bytes 4194328
  44.2 1.3 %copy-done.5 = bf16[512,2048]{1,0:T(8,128)(2,1)} copy-done((bf16[512,2048]{1,0:T(8,128)(2,1)}, bf16[512,2048]{1,0:T(8,128)(2,1)S(1)}, u32[]{:S(2)}) %copy-start.5) | copy-done | bytes 2097176
  45.5 0.5 collective-permute-start.4
  46.0 1.6 %collective-permute-done.4 = f32[72,1024]{1,0:T(8,128)} collective-permute-done((f32[72,1024]{1,0:T(8,128)}, f32[72,1024]{1,0:T(8,128)}, u32[]{:S(2)}, u32[]{:S(2)}) %collective-permute-start.4) | collective-permute-done | bytes 294944 | tf_op jit(solution)/shard_map/ppermute | solution.py:304
  47.6 1.0 %broadcast_select_fusion.1 = (f32[72,1024]{1,0:T(8,128)S(1)}, f32[72,1024]{1,0:T(8,128)S(1)}) fusion(f32[72,1024]{1,0:T(8,128)} %collective-permute-done.4, f32[72,1024]{1,0:T(8,128)S(1)} %get-tuple-element.40, pred[]{:T(512)S(6)} %eq.7), kind=kLoop, calls=%fused_computation.13 | loop fusion | flops 147456 | bytes 1179649 | tf_op jit(solution)/shard_map/jit(_where)/select_n | solution.py:318
  48.6 0.7 copy-done.19
  49.4 0.7 pad_maximum_fusion.1
  50.1 1.3 %collective-permute-start.5 = (f32[72,1024]{1,0:T(8,128)}, f32[72,1024]{1,0:T(8,128)}, u32[]{:S(2)}, u32[]{:S(2)}) collective-permute-start(f32[72,1024]{1,0:T(8,128)} %pad_maximum_fusion.1), channel_id=1, source_target_pairs={{2,0},{3,1},{4,2},{5,3},{6,4},{7,5},{8,6},{9,7},{10,8},{11,9},{12,... | collective-permute-start | bytes 884744 | tf_op jit(solution)/shard_map/ppermute | solution.py:308
  51.4 1.3 %collective-permute-start.6 = (f32[64,1024]{1,0:T(8,128)S(1)}, f32[64,1024]{1,0:T(8,128)}, u32[]{:S(2)}, u32[]{:S(2)}) collective-permute-start(f32[64,1024]{1,0:T(8,128)S(1)} %slice_add_fusion.1), channel_id=1, source_target_pairs={{4,0},{5,1},{6,2},{7,3},{8,4},{9,5},{10,6},{11,7},{12,8},{13,9},{1... | collective-permute-start | bytes 786440 | tf_op jit(solution)/shard_map/ppermute | solution.py:308
  52.7 0.6 reduce_sum.18
  53.3 1.2 %broadcast_in_dim.19 = f32[16,1,128]{2,1,0:T(1,128)} broadcast(f32[]{:T(128)} %reduce_sum.18), dimensions={} | broadcast | bytes 8196 | tf_op jit(solution)/shard_map/broadcast_in_dim | solution.py:410
  54.5 12.8 %all-to-all-start = ((f32[16,1,128]{2,1,0:T(1,128)}), f32[16,1,128]{2,1,0:T(1,128)S(1)}, u32[]{:S(2)}, u32[]{:S(2)}) async-start(f32[16,1,128]{2,1,0:T(1,128)} %broadcast_in_dim.19), calls=%async_computation | async-start | bytes 16384 | tf_op jit(solution)/shard_map/all_to_all | solution.py:411
  67.3 0.8 slice.66
  68.1 3.2 %collective-permute-done.6 = f32[64,1024]{1,0:T(8,128)} collective-permute-done((f32[64,1024]{1,0:T(8,128)S(1)}, f32[64,1024]{1,0:T(8,128)}, u32[]{:S(2)}, u32[]{:S(2)}) %collective-permute-start.6) | collective-permute-done | bytes 262176 | tf_op jit(solution)/shard_map/ppermute | solution.py:308
  71.3 1.9 %fusion = (f32[64,1024]{1,0:T(8,128)}, f32[64,1024]{1,0:T(8,128)S(1)}) fusion(f32[72,1024]{1,0:T(8,128)} %copy-done.19, f32[1024]{0:T(1024)S(1)} %bitcast.17, pred[]{:T(512)S(6)} %eq.7, f32[64,1024]{1,0:T(8,128)} %collective-permute-done.6, f32[1024]{0:T(1024)S(1)} %bitcast.22, f32[72,1024]{1,0:T(8,128)} %collective-permute-done.5), kind=kLoop, calls=%fused_computation.7 | loop fusion | flops 393216 | bytes 1318913 | tf_op jit(solution)/shard_map/jit(_where)/select_n | solution.py:338
  73.2 1.6 %copy-done.6 = bf16[512,2048]{1,0:T(8,128)(2,1)S(1)} copy-done((bf16[512,2048]{1,0:T(8,128)(2,1)S(1)}, bf16[512,2048]{1,0:T(8,128)(2,1)}, u32[]{:S(2)}) %copy-start.6) | copy-done | bytes 2097176
  74.7 1.0 %copy-done.9 = bf16[512,512]{1,0:T(8,128)(2,1)S(1)} copy-done((bf16[512,512]{1,0:T(8,128)(2,1)S(1)}, bf16[512,512]{1,0:T(8,128)(2,1)}, u32[]{:S(2)}) %copy-start.9) | copy-done | bytes 524312
  75.8 7.7 %shard_map.114 = (f32[512,2048]{1,0:T(8,128)S(1)}, f32[512,64]{1,0:T(8,128)S(1)}, f32[512,64]{1,0:T(8,128)S(1)}) custom-call(s32[18]{0:T(128)S(1)} %pad_add_fusion.info, f32[512,2048]{1,0:T(8,128)} %copy-done.2, bf16[512,2048]{1,0:T(8,128)(2,1)S(1)} %copy-done.6, bf16[512,2048]{1,0:T(8,128)(2,1)S(1)} %get-tuple-element.24.x_ref, ...), custom_call_target="tpu_custom_call" | custom-call | flops 2147483648 | bytes 14188544 | tf_op jit(solution)/shard_map/pallas_call | solution.py:286
  83.5 2.0 %copy-done.3 = f32[512,2048]{1,0:T(8,128)} copy-done((f32[512,2048]{1,0:T(8,128)}, f32[512,2048]{1,0:T(8,128)S(1)}, u32[]{:S(2)}) %copy-start.3) | copy-done | bytes 4194328
  85.6 0.7 copy-done.10
  86.2 0.7 copy-done.11
  86.9 1.7 %copy.39 = f32[512,64]{0,1:T(8,128)} copy(f32[512,64]{1,0:T(8,128)} %copy-done.10) | data formatting | bytes 262144
  88.7 0.6 slice_reduce_fusion
  89.9 2.2 %copy-done.4 = f32[512,2048]{1,0:T(8,128)S(1)} copy-done((f32[512,2048]{1,0:T(8,128)S(1)}, f32[512,2048]{1,0:T(8,128)}, u32[]{:S(2)}) %copy-start.4) | copy-done | bytes 4194328
  92.1 0.9 copy-done.12
  93.1 0.9 copy-done.14
  94.0 5.9 %shard_map.115 = (f32[512,2048]{1,0:T(8,128)}, f32[512,64]{1,0:T(8,128)S(1)}) custom-call(s32[18]{0:T(128)S(1)} %pad_add_fusion.info, f32[512,2048]{1,0:T(8,128)S(1)} %copy-done.4, bf16[512,2048]{1,0:T(8,128)(2,1)S(1)} %get-tuple-element.24.x_ref, bf16[512,96]{1,0:T(8,128)(2,1)S(1)} %get-tuple-element.35.sf3_ref, f32[8,2048]{1,0:T(8,128)S(1)} %get-tuple-element.26.rows_ref, ...), custom_call_target="tpu_custom_call" | custom-call | flops 536870912 | bytes 11501568 | tf_op jit(solution)/shard_map/pallas_call | solution.py:286
  99.8 0.8 copy.38
  (38 shorter events, 0.3 us)
Async XLA Ops:
  4.3 1.6 %copy-start = (bf16[512,2048]{1,0:T(8,128)(2,1)S(1)}, bf16[512,2048]{1,0:T(8,128)(2,1)}, u32[]{:S(2)}) copy-start(bf16[512,2048]{1,0:T(8,128)(2,1)} %v_ref.3) | copy-start | bytes 6291460
  5.9 0.7 copy-start.17
  6.5 0.7 copy-start.18
  13.2 0.7 copy-start.15
  13.8 17.2 %copy-start.13 = (bf16[512,64]{1,0:T(8,128)(2,1)}, bf16[512,64]{1,0:T(8,128)(2,1)S(1)}, u32[]{:S(2)}) copy-start(bf16[512,64]{1,0:T(8,128)(2,1)S(1)} %get-tuple-element.37.bm_ref) | copy-start | bytes 196612
  13.8 2.0 %collective-permute-start = (f32[72,1024]{1,0:T(8,128)}, f32[72,1024]{1,0:T(8,128)}, u32[]{:S(2)}, u32[]{:S(2)}) collective-permute-start(f32[72,1024]{1,0:T(8,128)} %get-tuple-element.29), channel_id=1, source_target_pairs={{0,1},{1,0},{2,3},{3,2},{4,5},{5,4},{6,7},{7,6},{8,9},{9,8},{10,11... | collective-permute-start | bytes 884744 | tf_op jit(solution)/shard_map/ppermute | solution.py:304
  14.3 16.9 %copy-start.1 = (bf16[512,2048]{1,0:T(8,128)(2,1)S(1)}, bf16[512,2048]{1,0:T(8,128)(2,1)}, u32[]{:S(2)}) copy-start(bf16[512,2048]{1,0:T(8,128)(2,1)} %v_ref.3) | copy-start | bytes 6291460
  17.0 20.4 %copy-start.16 = (bf16[512,64]{1,0:T(8,128)(2,1)S(1)}, bf16[512,64]{1,0:T(8,128)(2,1)}, u32[]{:S(2)}) copy-start(bf16[512,64]{1,0:T(8,128)(2,1)} %copy-done.15) | copy-start | bytes 196612
  17.0 11.5 %collective-permute-start.1 = (f32[72,1024]{1,0:T(8,128)S(1)}, f32[72,1024]{1,0:T(8,128)S(1)}, u32[]{:S(2)}, u32[]{:S(2)}) collective-permute-start(f32[72,1024]{1,0:T(8,128)S(1)} %pad_maximum_fusion), channel_id=1, source_target_pairs={{0,2},{1,3},{2,4},{3,5},{4,6},{5,7},{6,8},{7,9},{8,10},{9,11},{10,... | collective-permute-start | bytes 884744 | tf_op jit(solution)/shard_map/ppermute | solution.py:308
  21.9 9.0 %collective-permute-start.2 = (f32[64,1024]{1,0:T(8,128)S(1)}, f32[64,1024]{1,0:T(8,128)S(1)}, u32[]{:S(2)}, u32[]{:S(2)}) collective-permute-start(f32[64,1024]{1,0:T(8,128)S(1)} %slice_add_fusion.3), channel_id=1, source_target_pairs={{0,4},{1,5},{2,6},{3,7},{4,8},{5,9},{6,10},{7,11},{8,12},{9,13},{1... | collective-permute-start | bytes 786440 | tf_op jit(solution)/shard_map/ppermute | solution.py:308
  31.1 6.3 %collective-permute-start.3 = (f32[64,1024]{1,0:T(8,128)S(1)}, f32[64,1024]{1,0:T(8,128)S(1)}, u32[]{:S(2)}, u32[]{:S(2)}) collective-permute-start(f32[64,1024]{1,0:T(8,128)S(1)} %get-tuple-element.58), channel_id=1, source_target_pairs={{0,1},{1,0},{2,3},{3,2},{4,5},{5,4},{6,7},{7,6},{8,9},{9,8},{10,11... | collective-permute-start | bytes 786440 | tf_op jit(solution)/shard_map/ppermute | solution.py:304
  31.2 1.6 %copy-start.7 = (bf16[512,2048]{1,0:T(8,128)(2,1)S(1)}, bf16[512,2048]{1,0:T(8,128)(2,1)}, u32[]{:S(2)}) copy-start(bf16[512,2048]{1,0:T(8,128)(2,1)} %teach_ref.1) | copy-start | bytes 6291460
  37.3 4.9 %copy-start.8 = (bf16[512,512]{1,0:T(8,128)(2,1)}, bf16[512,512]{1,0:T(8,128)(2,1)S(1)}, u32[]{:S(2)}) copy-start(bf16[512,512]{1,0:T(8,128)(2,1)S(1)} %get-tuple-element.34.st_ref) | copy-start | bytes 1572868
  42.2 2.0 %copy-start.2 = (f32[512,2048]{1,0:T(8,128)}, f32[512,2048]{1,0:T(8,128)S(1)}, u32[]{:S(2)}) copy-start(f32[512,2048]{1,0:T(8,128)S(1)} %get-tuple-element.32.mm_ref) | copy-start | bytes 12582916
  44.2 1.3 %copy-start.5 = (bf16[512,2048]{1,0:T(8,128)(2,1)}, bf16[512,2048]{1,0:T(8,128)(2,1)S(1)}, u32[]{:S(2)}) copy-start(bf16[512,2048]{1,0:T(8,128)(2,1)S(1)} %get-tuple-element.33.y_ref) | copy-start | bytes 6291460
  45.5 2.0 %collective-permute-start.4 = (f32[72,1024]{1,0:T(8,128)}, f32[72,1024]{1,0:T(8,128)}, u32[]{:S(2)}, u32[]{:S(2)}) collective-permute-start(f32[72,1024]{1,0:T(8,128)} %get-tuple-element.39), channel_id=1, source_target_pairs={{0,1},{1,0},{2,3},{3,2},{4,5},{5,4},{6,7},{7,6},{8,9},{9,8},{10,11... | collective-permute-start | bytes 884744 | tf_op jit(solution)/shard_map/ppermute | solution.py:304
  48.6 0.7 copy-start.19
  50.1 17.2 %collective-permute-start.5 = (f32[72,1024]{1,0:T(8,128)}, f32[72,1024]{1,0:T(8,128)}, u32[]{:S(2)}, u32[]{:S(2)}) collective-permute-start(f32[72,1024]{1,0:T(8,128)} %pad_maximum_fusion.1), channel_id=1, source_target_pairs={{2,0},{3,1},{4,2},{5,3},{6,4},{7,5},{8,6},{9,7},{10,8},{11,9},{12,... | collective-permute-start | bytes 884744 | tf_op jit(solution)/shard_map/ppermute | solution.py:308
  51.4 19.9 %collective-permute-start.6 = (f32[64,1024]{1,0:T(8,128)S(1)}, f32[64,1024]{1,0:T(8,128)}, u32[]{:S(2)}, u32[]{:S(2)}) collective-permute-start(f32[64,1024]{1,0:T(8,128)S(1)} %slice_add_fusion.1), channel_id=1, source_target_pairs={{4,0},{5,1},{6,2},{7,3},{8,4},{9,5},{10,6},{11,7},{12,8},{13,9},{1... | collective-permute-start | bytes 786440 | tf_op jit(solution)/shard_map/ppermute | solution.py:308
  54.5 34.1 %all-to-all-start = ((f32[16,1,128]{2,1,0:T(1,128)}), f32[16,1,128]{2,1,0:T(1,128)S(1)}, u32[]{:S(2)}, u32[]{:S(2)}) async-start(f32[16,1,128]{2,1,0:T(1,128)} %broadcast_in_dim.19), calls=%async_computation | async-start | bytes 16384 | tf_op jit(solution)/shard_map/all_to_all | solution.py:411
  73.2 16.8 %collective-permute-start.7 = (f32[64,1024]{1,0:T(8,128)}, f32[64,1024]{1,0:T(8,128)}, u32[]{:S(2)}, u32[]{:S(2)}) collective-permute-start(f32[64,1024]{1,0:T(8,128)} %get-tuple-element.56), channel_id=1, source_target_pairs={{0,1},{1,0},{2,3},{3,2},{4,5},{5,4},{6,7},{7,6},{8,9},{9,8},{10,11... | collective-permute-start | bytes 786440 | tf_op jit(solution)/shard_map/ppermute | solution.py:304
  73.2 1.6 %copy-start.6 = (bf16[512,2048]{1,0:T(8,128)(2,1)S(1)}, bf16[512,2048]{1,0:T(8,128)(2,1)}, u32[]{:S(2)}) copy-start(bf16[512,2048]{1,0:T(8,128)(2,1)} %copy-done.5) | copy-start | bytes 6291460
  74.7 1.0 %copy-start.9 = (bf16[512,512]{1,0:T(8,128)(2,1)S(1)}, bf16[512,512]{1,0:T(8,128)(2,1)}, u32[]{:S(2)}) copy-start(bf16[512,512]{1,0:T(8,128)(2,1)} %copy-done.8) | copy-start | bytes 1572868
  83.5 2.0 %copy-start.3 = (f32[512,2048]{1,0:T(8,128)}, f32[512,2048]{1,0:T(8,128)S(1)}, u32[]{:S(2)}) copy-start(f32[512,2048]{1,0:T(8,128)S(1)} %get-tuple-element.36.g_ref) | copy-start | bytes 12582916
  85.5 0.7 copy-start.10
  86.2 0.7 copy-start.11
  89.9 2.2 %copy-start.4 = (f32[512,2048]{1,0:T(8,128)S(1)}, f32[512,2048]{1,0:T(8,128)}, u32[]{:S(2)}) copy-start(f32[512,2048]{1,0:T(8,128)} %copy-done.3) | copy-start | bytes 12582916
  92.1 0.9 copy-start.12
  93.1 0.9 copy-start.14

commit v2 on v1

v2 whole, which is shorter than its diff:
```python
import functools
import jax
import jax.numpy as jnp
from jax import lax
from jax.experimental import pallas as pl
from jax.experimental.pallas import tpu as pltpu
from jax.sharding import PartitionSpec as P

F32 = jnp.float32
BF16 = jnp.bfloat16
PAD = 8
CHUNK = 512
LIMIT = 60 << 20


def dot(a, b):
    return jnp.dot(a, b, preferred_element_type=F32)


def dot_nt(a, b):
    return lax.dot_general(a, b, (((1,), (1,)), ((), ())), preferred_element_type=F32)


def iota(shape, axis):
    return lax.broadcasted_iota(jnp.int32, shape, axis)


def dot_tn(a, b):
    return lax.dot_general(a, b, (((0,), (0,)), ((), ())), preferred_element_type=F32)


def split3(x):
    hi = x.astype(BF16)
    rest = x - hi.astype(F32)
    mid = rest.astype(BF16)
    lo = (rest - mid.astype(F32)).astype(BF16)
    return jnp.concatenate([hi, mid, lo], axis=0)


def split2(x):
    hi = x.astype(BF16)
    lo = (x - hi.astype(F32)).astype(BF16)
    return jnp.concatenate([hi, lo], axis=0)


def twice(x):
    return jnp.concatenate([x, x], axis=0)


def expander(heads, head_dim, width, chunk):
    rows = lax.rem(iota((3 * heads, width), 0), heads)
    cols = iota((3 * heads, width), 1) // head_dim + chunk * (width // head_dim)
    return (rows == cols).astype(F32).astype(BF16)


def doc_ids(lengths, docs, length, axis):
    shape = (length, 1) if axis == 0 else (1, length)
    place = iota(shape, axis)
    ids = jnp.zeros(shape, jnp.int32)
    before = jnp.int32(0)
    final = jnp.int32(0)
    start = -lax.axis_index("seq") * length
    for d in range(docs):
        ids = ids + (place >= start).astype(jnp.int32)
        before = before + (start <= -1).astype(jnp.int32)
        final = final + (start <= length - 1).astype(jnp.int32)
        start = start + lengths[d]
    return ids, before, final


def own_half(j, per_half):
    return j // per_half == lax.rem(lax.axis_index("seq"), 2)


def put_half(j, per_half, keep_ref, send_ref, state, decay):
    width = state.shape[1]
    rows = state.shape[0]
    place = pl.ds(pl.multiple_of(lax.rem(j, per_half) * width, width), width)
    mine = own_half(j, per_half)

    def put(ref):
        ref[0:rows, place] = state
        ref[rows : rows + 1, place] = decay

    pl.when(mine)(lambda: put(keep_ref))
    pl.when(jnp.logical_not(mine))(lambda: put(send_ref))


def get_half(j, per_half, mine_ref, other_ref, width):
    place = pl.ds(pl.multiple_of(lax.rem(j, per_half) * width, width), width)
    own = own_half(j, per_half).astype(F32)
    return jnp.where(own > 0.5, mine_ref[:, place], other_ref[:, place])


def column(row):
    n = row.shape[1]
    return jnp.sum(jnp.where(iota((n, n), 0) == iota((n, n), 1), row, 0.0), axis=1, keepdims=True)


def prepare_kernel(
    docs,
    lengths,
    v_ref,
    b_ref,
    c_ref,
    step_ref,
    rate_ref,
    gain_ref,
    x_ref,
    keep_ref,
    send_ref,
    enter3_ref,
    sf3_ref,
    rows_ref,
    bm_ref,
    cm_ref,
    f3,
    s3,
    r3,
):
    j = pl.program_id(0)
    heads, length = step_ref.shape
    width = v_ref.shape[1]
    head_dim = width * pl.num_programs(0) // heads

    @pl.when(j == 0)
    def _():
        blank = jnp.zeros((PAD, keep_ref.shape[1]), F32)
        keep_ref[b_ref.shape[0] :, :] = blank
        send_ref[b_ref.shape[0] :, :] = blank
        step = step_ref[...]
        upper = (iota((length, length), 0) <= iota((length, length), 1)).astype(F32).astype(BF16)
        sums = dot(split3(-(step * column(rate_ref[...]))), upper)
        level = sums[:heads] + sums[heads : 2 * heads] + sums[2 * heads :]
        middle = level[:, length // 2 - 1 : length // 2]
        last = level[:, length - 1 : length]
        ids, before, final = doc_ids(lengths, docs, length, 1)
        leave = jnp.exp(middle - level)
        enter3_ref[...] = split3(jnp.exp(level - middle))
        f3[...] = split3(leave)
        s3[...] = split3(step)
        sf3_ref[...] = split3(step * leave)
        through = jnp.where(before == final, jnp.exp(last), 0.0)
        pick = iota((heads, 128), 1)
        table = jnp.where(pick == 0, jnp.exp(middle), 0.0)
        table = jnp.where(pick == 1, jnp.exp(last - middle), table)
        table = jnp.where(pick == 2, through, table)
        table = jnp.where(pick == 3, column(gain_ref[...]), table)
        r3[...] = split3(table)
        bm_ref[...] = jnp.where(ids == final, b_ref[...].astype(F32), 0.0).astype(BF16)
        cm_ref[...] = jnp.where(ids == before, c_ref[...].astype(F32), 0.0).astype(BF16)

    spread = expander(heads, head_dim, width, j)
    rows = dot_tn(r3[...], spread)[:PAD]
    rows_ref[...] = rows
    scaled = (dot_tn(s3[...], spread) * v_ref[...].astype(F32)).astype(BF16).astype(F32)
    x = dot_tn(f3[...], spread) * scaled
    hi = x.astype(BF16)
    lo = (x - hi.astype(F32)).astype(BF16)
    x_ref[...] = hi
    state = (dot(bm_ref[...], hi) + dot(bm_ref[...], lo)) * rows[1:2, :]
    put_half(j, pl.num_programs(0) // 2, keep_ref, send_ref, state, rows[2:3, :])


def inner_kernel(
    docs, lengths, x_ref, v_ref, teach_ref, b_ref, c_ref, enter3_ref, rows_ref, base_ref, st_ref, s
):
    j = pl.program_id(0)
    length = x_ref.shape[0]
    width = x_ref.shape[1]
    heads = enter3_ref.shape[0] // 3
    head_dim = width * pl.num_programs(0) // heads

    @pl.when(j == 0)
    def _():
        col = doc_ids(lengths, docs, length, 0)[0]
        row = doc_ids(lengths, docs, length, 1)[0]
        down = iota((length, length), 0)
        along = iota((length, length), 1)
        scores = dot_tn(c_ref[...], b_ref[...])
        s[...] = jnp.where((col == row) & (down >= along), scores, 0.0).astype(BF16)
        turned = dot_tn(b_ref[...], c_ref[...])
        st_ref[...] = jnp.where((col == row) & (down <= along), turned, 0.0).astype(BF16)

    enter = dot_tn(enter3_ref[...], expander(heads, head_dim, width, j))
    base_ref[...] = (
        enter * dot(s[...], x_ref[...])
        + rows_ref[3:4, :] * v_ref[...].astype(F32)
        - teach_ref[...].astype(F32)
    )


def mismatch_kernel(
    base_ref, enter3_ref, rows_ref, cm_ref, mine_ref, other_ref, mm_ref, y_ref, keep_ref, send_ref
):
    j = pl.program_id(0)
    length, width = base_ref.shape
    heads = enter3_ref.shape[0] // 3
    head_dim = width * pl.num_programs(0) // heads
    per_half = pl.num_programs(0) // 2

    @pl.when(j == 0)
    def _():
        blank = jnp.zeros((PAD, keep_ref.shape[1]), F32)
        keep_ref[cm_ref.shape[0] :, :] = blank
        send_ref[cm_ref.shape[0] :, :] = blank

    enter = dot_tn(enter3_ref[...], expander(heads, head_dim, width, j))
    state = split2(get_half(j, per_half, mine_ref, other_ref, width) * rows_ref[0:1, :])
    cm = cm_ref[...]
    mm = base_ref[...] + enter * dot_tn(twice(cm), state)
    mm_ref[...] = mm
    y = (enter * mm).astype(BF16)
    y_ref[...] = y
    squares = jnp.sum(mm * mm, axis=0, keepdims=True)
    line = slice(cm_ref.shape[0] + 1, cm_ref.shape[0] + 2)
    keep_ref[line, :width] += squares
    send_ref[line, :width] += squares
    put_half(j, per_half, keep_ref, send_ref, dot(cm, y) * rows_ref[0:1, :], rows_ref[2:3, :])


def pair_kernel(
    docs,
    lengths,
    mm_ref,
    y_ref,
    x_ref,
    st_ref,
    sf3_ref,
    rows_ref,
    b_ref,
    c_ref,
    mine_ref,
    other_ref,
    g_ref,
    gb_ref,
    gc_ref,
    pair,
    acc,
):
    j = pl.program_id(0)
    length, width = mm_ref.shape
    heads = sf3_ref.shape[0] // 3
    head_dim = width * pl.num_programs(0) // heads
    width_n = b_ref.shape[0]

    @pl.when(j == 0)
    def _():
        pair[...] = jnp.zeros_like(pair)
        acc[...] = jnp.zeros_like(acc)

    y = y_ref[...]
    pair[...] += dot_nt(y, x_ref[...])
    sf = dot_tn(sf3_ref[...], expander(heads, head_dim, width, j))
    g_ref[...] = rows_ref[3:4, :] * mm_ref[...] + sf * dot(st_ref[...], y)
    state = get_half(j, pl.num_programs(0) // 2, mine_ref, other_ref, width) * rows_ref[0:1, :]
    acc[...] += dot_nt(split2(state), y)

    @pl.when(j == pl.num_programs(0) - 1)
    def _():
        col = doc_ids(lengths, docs, length, 0)[0]
        row, before, _final = doc_ids(lengths, docs, length, 1)
        keep = (col == row) & (iota((length, length), 0) >= iota((length, length), 1))
        masked = jnp.where(keep, pair[...], 0.0)
        hi = masked.astype(BF16)
        lo = (masked - hi.astype(F32)).astype(BF16)
        through = acc[:width_n] + acc[width_n:]
        gc_ref[...] = dot_nt(b_ref[...], hi) + dot_nt(b_ref[...], lo) + jnp.where(row == before, through, 0.0)
        gb_ref[...] = dot(c_ref[...], hi) + dot(c_ref[...], lo)


def finish_kernel(
    docs, lengths, g_ref, x_ref, sf3_ref, rows_ref, bm_ref, gb_part_ref, mine_ref, other_ref, gv_ref, gb_ref, acc
):
    j = pl.program_id(0)
    length, width = g_ref.shape
    heads = sf3_ref.shape[0] // 3
    head_dim = width * pl.num_programs(0) // heads
    width_n = bm_ref.shape[0]

    @pl.when(j == 0)
    def _():
        acc[...] = jnp.zeros_like(acc)

    sf = dot_tn(sf3_ref[...], expander(heads, head_dim, width, j))
    adjoint = split2(
        get_half(j, pl.num_programs(0) // 2, mine_ref, other_ref, width) * rows_ref[1:2, :]
    )
    gv_ref[...] = g_ref[...] + sf * dot_tn(twice(bm_ref[...]), adjoint)
    acc[...] += dot_nt(x_ref[...], adjoint)

    @pl.when(j == pl.num_programs(0) - 1)
    def _():
        ids, _before, final = doc_ids(lengths, docs, length, 1)
        through = (acc[:, :width_n] + acc[:, width_n:]).T
        gb_ref[...] = gb_part_ref[...] + jnp.where(ids == final, through, 0.0)


def call(kernel, scalars, ins, in_kinds, outs, out_kinds, scratch, steps, flops):
    def spec(shape, kind):
        if kind == "cols":
            return pl.BlockSpec((shape[0], shape[1] // steps), lambda j, *_: (0, j))
        return pl.BlockSpec(shape, lambda j, *_: (0, 0))

    size = sum(a.size * a.dtype.itemsize for a in ins) + sum(o.size * o.dtype.itemsize for o in outs)
    return pl.pallas_call(
        kernel,
        out_shape=outs,
        grid_spec=pltpu.PrefetchScalarGridSpec(
            num_scalar_prefetch=len(scalars),
            grid=(steps,),
            in_specs=[spec(a.shape, k) for a, k in zip(ins, in_kinds)],
            out_specs=[spec(o.shape, k) for o, k in zip(outs, out_kinds)],
            scratch_shapes=scratch,
        ),
        compiler_params=pltpu.CompilerParams(
            dimension_semantics=("arbitrary",), vmem_limit_bytes=LIMIT
        ),
        cost_estimate=pl.CostEstimate(flops=flops, bytes_accessed=size, transcendentals=0),
    )(*scalars, *ins)


def swap(x, devices):
    return lax.ppermute(x, "seq", [(i, i ^ 1) for i in range(devices)])


def shift(x, by, devices):
    return lax.ppermute(
        x, "seq", [(i, i + by) for i in range(devices) if 0 <= i + by < devices]
    )


def turn(x, by, devices):
    return lax.ppermute(x, "seq", [(i, (i + by) % devices) for i in range(devices)])


def chip_order(way, mine_ref, got_ref):
    near = lax.rem(lax.axis_index("seq"), 2) == (0 if way == 1 else 1)
    near = near.astype(F32) > 0.5
    mine, got = mine_ref[...], got_ref[...]
    return near, jnp.where(near, mine, got), jnp.where(near, got, mine)


def compose_kernel(way, keep_ref, got_ref, packed_ref, both_ref):
    rows = both_ref.shape[0]
    _near, first, second = chip_order(way, keep_ref, got_ref)
    both = second[:rows] + second[rows : rows + 1] * first[:rows]
    both_ref[...] = both
    packed_ref[:rows] = both
    a, b = first[rows:], second[rows:]
    packed_ref[rows:] = jnp.where(iota(a.shape, 0) == 0, a * b, a + b)


def arrive_kernel(way, keep_ref, got_ref, packed_ref, one_ref, two_ref, mine_ref, theirs_ref, line_ref):
    rows = mine_ref.shape[0]
    near, first, _second = chip_order(way, keep_ref, got_ref)
    state = one_ref[:rows] + one_ref[rows : rows + 1] * two_ref[:rows]
    inside = first[:rows] + first[rows : rows + 1] * state
    mine_ref[...] = jnp.where(near, state, inside)
    theirs_ref[...] = jnp.where(near, inside, state)
    line_ref[...] = packed_ref[rows + 1 : rows + 2] + one_ref[rows + 1 : rows + 2]


def small(kernel, ins, outs):
    size = sum(a.size * a.dtype.itemsize for a in ins) + sum(o.size * o.dtype.itemsize for o in outs)
    return pl.pallas_call(
        kernel,
        out_shape=outs,
        in_specs=[pl.BlockSpec(memory_space=pltpu.VMEM)] * len(ins),
        out_specs=[pl.BlockSpec(memory_space=pltpu.VMEM)] * len(outs),
        compiler_params=pltpu.CompilerParams(vmem_limit_bytes=8 << 20),
        cost_estimate=pl.CostEstimate(flops=0, bytes_accessed=size, transcendentals=0),
    )(*ins)


def carry(keep, send, devices, way, beside):
    rows, width = keep.shape[0] - PAD, keep.shape[1]
    part = jax.ShapeDtypeStruct((rows, width), F32)
    got = swap(send, devices)
    packed, both = small(
        functools.partial(compose_kernel, way), [keep, got], [jax.ShapeDtypeStruct(keep.shape, F32), part]
    )
    reach = max(1, devices // 8)
    one = shift(packed, 2, devices) if way == 1 else turn(packed, -2, devices)
    two = shift(packed if reach > 2 else both, 4 * way, devices)
    if reach > 2:
        state = one[:rows] + one[rows : rows + 1] * two[:rows]
        run = one[rows : rows + 1] * two[rows : rows + 1]
        span = 2
        while span < reach:
            more = shift(jnp.concatenate([state, jnp.broadcast_to(run, (PAD, width))], axis=0), 2 * span * way, devices)
            state = state + run * more[:rows]
            run = run * more[rows : rows + 1]
            span *= 2
        one = jnp.concatenate([state, one[rows:]], axis=0)
        two = jnp.zeros_like(state)
    mine, theirs, line = small(
        functools.partial(arrive_kernel, way),
        [keep, got, packed, one, two],
        [part, part, jax.ShapeDtypeStruct((1, width), F32)],
    )
    theirs, beside = lax.optimization_barrier((theirs, beside))
    return mine, swap(theirs, devices), line, beside


def local(values, b_proj, c_proj, step_sizes, decay_rates, skip_gain, teacher, doc_lengths):
    length, total = values.shape
    heads = step_sizes.shape[1]
    state = b_proj.shape[1]
    docs = doc_lengths.shape[0]
    devices = lax.axis_size("seq")
    steps = total // CHUNK
    rates = decay_rates.reshape(1, heads)
    gains = skip_gain.reshape(1, heads)
    b = b_proj.T
    c = c_proj.T

    def out(*shape, dtype=F32):
        return jax.ShapeDtypeStruct(shape, dtype)

    half = out(state + PAD, total // 2)
    thirds = out(3 * heads, length, dtype=BF16)
    narrow = out(state, length, dtype=BF16)
    square = 2 * length * length * total
    thin = 2 * length * state * total
    x, keep, send, enter3, sf3, rows, bm, cm = call(
        functools.partial(prepare_kernel, docs),
        [doc_lengths],
        [values, b, c, step_sizes.T, rates, gains],
        ["cols", "all", "all", "all", "all", "all"],
        [out(length, total, dtype=BF16), half, half, thirds, thirds, out(PAD, total), narrow, narrow],
        ["cols", "all", "all", "all", "all", "cols", "all", "all"],
        [
            pltpu.VMEM((3 * heads, length), BF16),
            pltpu.VMEM((3 * heads, length), BF16),
            pltpu.VMEM((3 * heads, 128), BF16),
        ],
        steps,
        4 * thin,
    )
    inner = call(
        functools.partial(inner_kernel, docs),
        [doc_lengths],
        [x, values, teacher, b, c, enter3, rows],
        ["cols", "cols", "cols", "all", "all", "all", "cols"],
        [out(length, total), out(length, length, dtype=BF16)],
        ["cols", "all"],
        [pltpu.VMEM((length, length), BF16)],
        steps,
        square,
    )
    state_mine, state_other, _, (base, score_t) = carry(keep, send, devices, 1, inner)
    mm, y, back_keep, back_send = call(
        mismatch_kernel,
        [],
        [base, enter3, rows, cm, state_mine, state_other],
        ["cols", "all", "cols", "all", "all", "all"],
        [out(length, total), out(length, total, dtype=BF16), half, half],
        ["cols", "cols", "all", "all"],
        [],
        steps,
        4 * thin,
    )
    pairs = call(
        functools.partial(pair_kernel, docs),
        [doc_lengths],
        [mm, y, x, score_t, sf3, rows, b, c, state_mine, state_other],
        ["cols", "cols", "cols", "all", "all", "cols", "all", "all", "all", "all"],
        [out(length, total), out(state, length), out(state, length)],
        ["cols", "all", "all"],
        [pltpu.VMEM((length, length), F32), pltpu.VMEM((2 * state, length), F32)],
        steps,
        2 * square,
    )
    adj_mine, adj_other, squares, (g, gb_part, grad_c) = carry(back_keep, back_send, devices, -1, pairs)
    span = 2
    while span < devices // 2:
        squares = squares + turn(squares, -2 * span, devices)
        span *= 2
    grad_values, grad_b = call(
        functools.partial(finish_kernel, docs),
        [doc_lengths],
        [g, x, sf3, rows, bm, gb_part, adj_mine, adj_other],
        ["cols", "cols", "all", "cols", "all", "all", "all", "all"],
        [out(length, total), out(state, length)],
        ["cols", "all"],
        [pltpu.VMEM((length, 2 * state), F32)],
        steps,
        4 * thin,
    )
    loss = (jnp.sum(squares) / (devices * length * total)).reshape(1)
    return loss, grad_values, grad_b.T, grad_c.T


def solution(mesh):
    rows = P(("groups", "seq"), None)
    in_specs = (rows, rows, rows, rows, P(), P(), rows, P("groups"))
    out_specs = (P("groups"), rows, rows, rows)
    return jax.shard_map(local, mesh=mesh, in_specs=in_specs, out_specs=out_specs, check_vma=False)
```

time: 103 us -> 79.5 us (0.77)
  local copies, waits for them, and re-layouts: 26.7 us -> 4.79 us
  Pallas kernels: 29 us -> 41.2 us
  other arithmetic: 6.8 us -> 0.61 us
  starting transfers between devices: 24.8 us -> 19.3 us
  waiting for transfers between devices: 11.9 us -> 10.4 us
    unnamed x45 -> x16, local copies, waits for them, and re-layouts: 24.6 us -> 4.79 us
    all_to_all x1 -> x0, starting transfers between devices: 12.8 us -> none  [local(): lax.all_to_all(parts, 'seq', split_axis=0, concat_axis=0, tiled=True)]
    pallas_call x5, Pallas kernels: 29 us -> 40.3 us  [call(): pl.pallas_call(kernel, out_shape=outs, grid_spec=pltpu.PrefetchScalarGrid...]
    ppermute x0 -> x3, starting transfers between devices: none -> 8.86 us  [turn(): lax.ppermute(x, 'seq', [(i, (i + by) % devices) for i in range(devices)])]
    ppermute x4 -> x3, waiting for transfers between devices: 8.75 us -> 0.01 us  [shift(): lax.ppermute(x, 'seq', [(i, i + by) for i in range(devices) if 0 <= i + b...]
    ppermute x0 -> x3, waiting for transfers between devices: none -> 5.84 us  [turn(): lax.ppermute(x, 'seq', [(i, (i + by) % devices) for i in range(devices)])]
    select_n x4 -> x0, other arithmetic: 4.02 us -> none  [the longest x2 2.07 us: carry(): second = jnp.where(near, got, keep)]
    concatenate x3 -> x0, other arithmetic: 1.49 us -> none  [the longest x2 0.75 us: carry(): packed = jnp.concatenate([both, decay], axis=0)]
  transfers between devices with their start and end apart: 9 -> 10, of which waited for: 5 -> 5; matrix products, arithmetic and copies ran while one was open for 7% -> 1% of each run, Pallas kernels for 12% -> 23%
where the time goes in v2:
time: 79.5 us; the launch traced here: 78.9 us
  Pallas kernels  41.2 us (52%)
  starting transfers between devices  19.3 us (24%)
  waiting for transfers between devices  10.4 us (13%)
  local copies, waits for them, and re-layouts  4.79 us (6%)
  between operations  2.56 us (3%)
    pallas_call x5, Pallas kernels, call(): pl.pallas_call(kernel, out_shape=outs, grid_spec=pltpu.PrefetchScalarGrid...  40.3 us
    ppermute x3, starting transfers between devices, shift(): lax.ppermute(x, 'seq', [(i, i + by) for i in range(devices) if 0 <= i + b...  9.7 us
    ppermute x3, starting transfers between devices, turn(): lax.ppermute(x, 'seq', [(i, (i + by) % devices) for i in range(devices)])  8.86 us
    ppermute x3, waiting for transfers between devices, turn(): lax.ppermute(x, 'seq', [(i, (i + by) % devices) for i in range(devices)])  5.84 us
    unnamed x16, local copies, waits for them, and re-layouts  4.79 us
    ppermute x4, waiting for transfers between devices, swap(): return lax.ppermute(x, 'seq', [(i, i ^ 1) for i in range(devices)])  4.59 us
  transfers between devices with their start and end apart: 10, of which 5 were waited for; matrix products, arithmetic and copies ran while one was open for 1% of the time, Pallas kernels for 23%

profile of v2, /device:TPU:0, one launch (start us, length us, event | category | flops | bytes accessed | tf_op | source)
XLA Modules:
  0.0 78.9 jit_solution(14376504818883978715)
XLA Ops:
  0.6 7.0 %shard_map.111 = (bf16[512,2048]{1,0:T(8,128)(2,1)}, f32[72,1024]{1,0:T(8,128)}, f32[72,1024]{1,0:T(8,128)}, bf16[96,512]{1,0:T(8,128)(2,1)}, bf16[96,512]{1,0:T...) custom-call(s32[16]{0:T(128)} %lengths.7, bf16[512,2048]{1,0:T(8,128)(2,1)} %v_ref.3, ...), custom_call_target="tpu_custom_call" | custom-call | flops 536870912 | bytes 5374208 | tf_op jit(solution)/shard_map/pallas_call | solution.py:306
  7.7 0.5 collective-permute-start
  8.2 1.4 %collective-permute-done.got_ref = f32[72,1024]{1,0:T(8,128)S(1)} collective-permute-done((f32[72,1024]{1,0:T(8,128)}, f32[72,1024]{1,0:T(8,128)S(1)}, u32[]{:S(2)}, u32[]{:S(2)}) %collective-permute-start) | collective-permute-done | bytes 294944 | tf_op jit(solution)/shard_map/ppermute | solution.py:324
  9.6 0.0 copy-start.2
  9.6 1.0 %copy-done.2 = f32[72,1024]{1,0:T(8,128)S(1)} copy-done((f32[72,1024]{1,0:T(8,128)S(1)}, f32[72,1024]{1,0:T(8,128)}, u32[]{:S(2)}) %copy-start.2) | copy-done | bytes 294936
  10.5 0.0 copy-start.3
  10.5 0.1 shard_map.112
  10.6 5.0 %collective-permute-start.1 = (f32[72,1024]{1,0:T(8,128)S(1)}, f32[72,1024]{1,0:T(8,128)S(1)}, u32[]{:S(2)}, u32[]{:S(2)}) collective-permute-start(f32[72,1024]{1,0:T(8,128)S(1)} %get-tuple-element.41.packed_ref), channel_id=1, source_target_pairs={{0,2},{1,3},{2,4},{3,5},{4,6},{5,7},{6,8},{7,9},{8,10},{9,11},{10,... | collective-permute-start | bytes 884744 | tf_op jit(solution)/shard_map/ppermute | solution.py:328
  15.6 3.5 %collective-permute-start.2 = (f32[64,1024]{1,0:T(8,128)S(1)}, f32[64,1024]{1,0:T(8,128)S(1)}, u32[]{:S(2)}, u32[]{:S(2)}) collective-permute-start(f32[64,1024]{1,0:T(8,128)S(1)} %get-tuple-element.42), channel_id=1, source_target_pairs={{0,4},{1,5},{2,6},{3,7},{4,8},{5,9},{6,10},{7,11},{8,12},{9,13},{1... | collective-permute-start | bytes 786440 | tf_op jit(solution)/shard_map/ppermute | solution.py:328
  19.0 8.2 %shard_map.114 = (f32[512,2048]{1,0:T(8,128)}, bf16[512,512]{1,0:T(8,128)(2,1)}) custom-call(s32[16]{0:T(128)} %lengths.7, bf16[512,2048]{1,0:T(8,128)(2,1)} %get-tuple-element.44.x_ref, bf16[512,2048]{1,0:T(8,128)(2,1)} %v_ref.3, bf16[512,2048]{1,0:T(8,128)(2,1)} %teach_ref.1, bf16[64,512]{1,0:T(8,128)(2,1)} %bitcast.9, bf16[64,512]{1,0:T(8,128)(2,1)} %bitcast.12, ...), custom_call_target="tpu_custom_call" | custom-call | flops 1073741824 | bytes 11304960 | tf_op jit(solution)/shard_map/pallas_call | solution.py:306
  27.2 0.0 collective-permute-done.2.two_ref
  27.3 0.0 collective-permute-done.1.one_ref
  27.3 0.0 copy-done.3
  27.3 0.6 shard_map.113
  27.9 0.0 copy-start.4
  27.9 0.7 copy-done.4
  28.6 0.0 collective-permute-start.3
  28.6 1.5 %collective-permute-done.3.other_ref = f32[64,1024]{1,0:T(8,128)S(1)} collective-permute-done((f32[64,1024]{1,0:T(8,128)S(1)}, f32[64,1024]{1,0:T(8,128)S(1)}, u32[]{:S(2)}, u32[]{:S(2)}) %collective-permute-start.3) | collective-permute-done | bytes 262176 | tf_op jit(solution)/shard_map/ppermute | solution.py:324
  30.2 0.0 copy-start.6
  30.2 0.7 copy-done.6
  30.9 7.1 %shard_map.115 = (f32[512,2048]{1,0:T(8,128)}, bf16[512,2048]{1,0:T(8,128)(2,1)}, f32[72,1024]{1,0:T(8,128)}, f32[72,1024]{1,0:T(8,128)}) custom-call(f32[512,2048]{1,0:T(8,128)} %get-tuple-element.49.base_ref, bf16[96,512]{1,0:T(8,128)(2,1)} %get-tuple-element.45.enter3_ref, f32[8,2048]{1,0:T(8,128)} %get-tuple-element.46.rows_ref, ...), custom_call_target="tpu_custom_call" | custom-call | flops 536870912 | bytes 11829248 | tf_op jit(solution)/shard_map/pallas_call | solution.py:306
  38.0 0.2 collective-permute-start.4
  38.2 1.6 %collective-permute-done.4.got_ref = f32[72,1024]{1,0:T(8,128)S(1)} collective-permute-done((f32[72,1024]{1,0:T(8,128)}, f32[72,1024]{1,0:T(8,128)S(1)}, u32[]{:S(2)}, u32[]{:S(2)}) %collective-permute-start.4) | collective-permute-done | bytes 294944 | tf_op jit(solution)/shard_map/ppermute | solution.py:324
  39.8 0.0 copy-start
  39.8 1.0 %copy-done = f32[72,1024]{1,0:T(8,128)S(1)} copy-done((f32[72,1024]{1,0:T(8,128)S(1)}, f32[72,1024]{1,0:T(8,128)}, u32[]{:S(2)}) %copy-start) | copy-done | bytes 294936
  40.8 0.1 shard_map.116
  40.9 6.0 %collective-permute-start.5 = (f32[72,1024]{1,0:T(8,128)S(1)}, f32[72,1024]{1,0:T(8,128)S(1)}, u32[]{:S(2)}, u32[]{:S(2)}) collective-permute-start(f32[72,1024]{1,0:T(8,128)S(1)} %get-tuple-element.55.packed_ref), channel_id=1, source_target_pairs={{0,14},{1,15},{2,0},{3,1},{4,2},{5,3},{6,4},{7,5},{8,6},{9,7},{10,... | collective-permute-start | bytes 884744 | tf_op jit(solution)/shard_map/ppermute | solution.py:334
  46.8 1.3 %collective-permute-start.6 = (f32[64,1024]{1,0:T(8,128)S(1)}, f32[64,1024]{1,0:T(8,128)S(1)}, u32[]{:S(2)}, u32[]{:S(2)}) collective-permute-start(f32[64,1024]{1,0:T(8,128)S(1)} %get-tuple-element.56), channel_id=1, source_target_pairs={{4,0},{5,1},{6,2},{7,3},{8,4},{9,5},{10,6},{11,7},{12,8},{13,9},{1... | collective-permute-start | bytes 786440 | tf_op jit(solution)/shard_map/ppermute | solution.py:328
  48.1 0.0 copy-start.1
  48.1 10.3 %shard_map.118 = (f32[512,2048]{1,0:T(8,128)}, f32[64,512]{1,0:T(8,128)}, f32[64,512]{1,0:T(8,128)}) custom-call(s32[16]{0:T(128)} %lengths.7, f32[512,2048]{1,0:T(8,128)} %get-tuple-element.59.mm_ref, bf16[512,2048]{1,0:T(8,128)(2,1)} %get-tuple-element.60.y_ref, bf16[512,2048]{1,0:T(8,128)(2,1)} %get-tuple-element.44.x_ref, ...), custom_call_target="tpu_custom_call" | custom-call | flops 2147483648 | bytes 14188544 | tf_op jit(solution)/shard_map/pallas_call | solution.py:306
  58.5 0.0 collective-permute-done.6.two_ref
  58.5 0.0 collective-permute-done.5.one_ref
  58.5 0.0 copy-done.1
  58.5 0.1 shard_map.117
  58.6 0.0 copy-start.5
  58.6 0.7 copy-done.5
  59.3 0.0 collective-permute-start.9
  59.3 1.5 %collective-permute-start.7 = (f32[1,1024]{1,0:T(1,128)S(1)}, f32[1,1024]{1,0:T(1,128)S(1)}, u32[]{:S(2)}, u32[]{:S(2)}) collective-permute-start(f32[1,1024]{1,0:T(1,128)S(1)} %get-tuple-element.57), channel_id=1, source_target_pairs={{0,12},{1,13},{2,14},{3,15},{4,0},{5,1},{6,2},{7,3},{8,4},{9,5},{1... | collective-permute-start | bytes 12296 | tf_op jit(solution)/shard_map/ppermute | solution.py:334
  60.8 2.7 %collective-permute-done.7 = f32[1,1024]{1,0:T(1,128)S(1)} collective-permute-done((f32[1,1024]{1,0:T(1,128)S(1)}, f32[1,1024]{1,0:T(1,128)S(1)}, u32[]{:S(2)}, u32[]{:S(2)}) %collective-permute-start.7) | collective-permute-done | bytes 4128 | tf_op jit(solution)/shard_map/ppermute | solution.py:334
  63.5 1.4 %collective-permute-start.8 = (f32[1,1024]{1,0:T(1,128)S(1)}, f32[1,1024]{1,0:T(1,128)S(1)}, u32[]{:S(2)}, u32[]{:S(2)}) collective-permute-start(f32[1,1024]{1,0:T(1,128)S(1)} %add.6), channel_id=1, source_target_pairs={{0,8},{1,9},{2,10},{3,11},{4,12},{5,13},{6,14},{7,15},{8,0},{9,1},... | collective-permute-start | bytes 12296 | tf_op jit(solution)/shard_map/ppermute | solution.py:334
  64.9 3.1 %collective-permute-done.8 = f32[1,1024]{1,0:T(1,128)S(1)} collective-permute-done((f32[1,1024]{1,0:T(1,128)S(1)}, f32[1,1024]{1,0:T(1,128)S(1)}, u32[]{:S(2)}, u32[]{:S(2)}) %collective-permute-start.8) | collective-permute-done | bytes 4128 | tf_op jit(solution)/shard_map/ppermute | solution.py:334
  68.1 0.6 add_reduce_fusion
  69.3 0.0 collective-permute-done.9.other_ref
  69.3 0.0 copy-start.7
  69.3 0.7 copy-done.7
  70.0 7.7 %shard_map.119 = (f32[512,2048]{1,0:T(8,128)}, f32[64,512]{1,0:T(8,128)}) custom-call(s32[16]{0:T(128)} %lengths.7, f32[512,2048]{1,0:T(8,128)} %get-tuple-element.66.g_ref, bf16[512,2048]{1,0:T(8,128)(2,1)} %get-tuple-element.44.x_ref, bf16[96,512]{1,0:T(8,128)(2,1)} %get-tuple-element.62.sf3_ref, f32[8,2048]{1,0:T(8,128)} %get-tuple-element.46.rows_ref, ...), custom_call_target="tpu_custom_call" | custom-call | flops 536870912 | bytes 11501568 | tf_op jit(solution)/shard_map/pallas_call | solution.py:306
  (1 shorter events, 0.0 us)
Async XLA Ops:
  7.7 1.9 %collective-permute-start = (f32[72,1024]{1,0:T(8,128)}, f32[72,1024]{1,0:T(8,128)S(1)}, u32[]{:S(2)}, u32[]{:S(2)}) collective-permute-start(f32[72,1024]{1,0:T(8,128)} %get-tuple-element.40), channel_id=1, source_target_pairs={{0,1},{1,0},{2,3},{3,2},{4,5},{5,4},{6,7},{7,6},{8,9},{9,8},{10,11... | collective-permute-start | bytes 884744 | tf_op jit(solution)/shard_map/ppermute | solution.py:324
  9.6 1.0 %copy-start.2 = (f32[72,1024]{1,0:T(8,128)S(1)}, f32[72,1024]{1,0:T(8,128)}, u32[]{:S(2)}) copy-start(f32[72,1024]{1,0:T(8,128)} %get-tuple-element.39.keep_ref) | copy-start | bytes 884740
  10.5 16.7 %copy-start.3 = (f32[72,1024]{1,0:T(8,128)S(1)}, f32[72,1024]{1,0:T(8,128)}, u32[]{:S(2)}) copy-start(f32[72,1024]{1,0:T(8,128)} %get-tuple-element.39.keep_ref) | copy-start | bytes 884740
  10.6 16.7 %collective-permute-start.1 = (f32[72,1024]{1,0:T(8,128)S(1)}, f32[72,1024]{1,0:T(8,128)S(1)}, u32[]{:S(2)}, u32[]{:S(2)}) collective-permute-start(f32[72,1024]{1,0:T(8,128)S(1)} %get-tuple-element.41.packed_ref), channel_id=1, source_target_pairs={{0,2},{1,3},{2,4},{3,5},{4,6},{5,7},{6,8},{7,9},{8,10},{9,11},{10,... | collective-permute-start | bytes 884744 | tf_op jit(solution)/shard_map/ppermute | solution.py:328
  15.6 11.7 %collective-permute-start.2 = (f32[64,1024]{1,0:T(8,128)S(1)}, f32[64,1024]{1,0:T(8,128)S(1)}, u32[]{:S(2)}, u32[]{:S(2)}) collective-permute-start(f32[64,1024]{1,0:T(8,128)S(1)} %get-tuple-element.42), channel_id=1, source_target_pairs={{0,4},{1,5},{2,6},{3,7},{4,8},{5,9},{6,10},{7,11},{8,12},{9,13},{1... | collective-permute-start | bytes 786440 | tf_op jit(solution)/shard_map/ppermute | solution.py:328
  27.9 0.7 copy-start.4
  28.6 1.5 %collective-permute-start.3 = (f32[64,1024]{1,0:T(8,128)S(1)}, f32[64,1024]{1,0:T(8,128)S(1)}, u32[]{:S(2)}, u32[]{:S(2)}) collective-permute-start(f32[64,1024]{1,0:T(8,128)S(1)} %get-tuple-element.52), channel_id=1, source_target_pairs={{0,1},{1,0},{2,3},{3,2},{4,5},{5,4},{6,7},{7,6},{8,9},{9,8},{10,11... | collective-permute-start | bytes 786440 | tf_op jit(solution)/shard_map/ppermute | solution.py:324
  30.2 0.7 copy-start.6
  38.0 1.9 %collective-permute-start.4 = (f32[72,1024]{1,0:T(8,128)}, f32[72,1024]{1,0:T(8,128)S(1)}, u32[]{:S(2)}, u32[]{:S(2)}) collective-permute-start(f32[72,1024]{1,0:T(8,128)} %get-tuple-element.54), channel_id=1, source_target_pairs={{0,1},{1,0},{2,3},{3,2},{4,5},{5,4},{6,7},{7,6},{8,9},{9,8},{10,11... | collective-permute-start | bytes 884744 | tf_op jit(solution)/shard_map/ppermute | solution.py:324
  39.8 1.0 %copy-start = (f32[72,1024]{1,0:T(8,128)S(1)}, f32[72,1024]{1,0:T(8,128)}, u32[]{:S(2)}) copy-start(f32[72,1024]{1,0:T(8,128)} %get-tuple-element.53.keep_ref) | copy-start | bytes 884740
  40.9 17.6 %collective-permute-start.5 = (f32[72,1024]{1,0:T(8,128)S(1)}, f32[72,1024]{1,0:T(8,128)S(1)}, u32[]{:S(2)}, u32[]{:S(2)}) collective-permute-start(f32[72,1024]{1,0:T(8,128)S(1)} %get-tuple-element.55.packed_ref), channel_id=1, source_target_pairs={{0,14},{1,15},{2,0},{3,1},{4,2},{5,3},{6,4},{7,5},{8,6},{9,7},{10,... | collective-permute-start | bytes 884744 | tf_op jit(solution)/shard_map/ppermute | solution.py:334
  46.8 11.6 %collective-permute-start.6 = (f32[64,1024]{1,0:T(8,128)S(1)}, f32[64,1024]{1,0:T(8,128)S(1)}, u32[]{:S(2)}, u32[]{:S(2)}) collective-permute-start(f32[64,1024]{1,0:T(8,128)S(1)} %get-tuple-element.56), channel_id=1, source_target_pairs={{4,0},{5,1},{6,2},{7,3},{8,4},{9,5},{10,6},{11,7},{12,8},{13,9},{1... | collective-permute-start | bytes 786440 | tf_op jit(solution)/shard_map/ppermute | solution.py:328
  48.1 10.4 %copy-start.1 = (f32[72,1024]{1,0:T(8,128)S(1)}, f32[72,1024]{1,0:T(8,128)}, u32[]{:S(2)}) copy-start(f32[72,1024]{1,0:T(8,128)} %get-tuple-element.53.keep_ref) | copy-start | bytes 884740
  58.6 0.7 copy-start.5
  59.3 10.0 %collective-permute-start.9 = (f32[64,1024]{1,0:T(8,128)S(1)}, f32[64,1024]{1,0:T(8,128)S(1)}, u32[]{:S(2)}, u32[]{:S(2)}) collective-permute-start(f32[64,1024]{1,0:T(8,128)S(1)} %get-tuple-element.70), channel_id=1, source_target_pairs={{0,1},{1,0},{2,3},{3,2},{4,5},{5,4},{6,7},{7,6},{8,9},{9,8},{10,11... | collective-permute-start | bytes 786440 | tf_op jit(solution)/shard_map/ppermute | solution.py:324
  59.3 4.2 %collective-permute-start.7 = (f32[1,1024]{1,0:T(1,128)S(1)}, f32[1,1024]{1,0:T(1,128)S(1)}, u32[]{:S(2)}, u32[]{:S(2)}) collective-permute-start(f32[1,1024]{1,0:T(1,128)S(1)} %get-tuple-element.57), channel_id=1, source_target_pairs={{0,12},{1,13},{2,14},{3,15},{4,0},{5,1},{6,2},{7,3},{8,4},{9,5},{1... | collective-permute-start | bytes 12296 | tf_op jit(solution)/shard_map/ppermute | solution.py:334
  63.5 4.5 %collective-permute-start.8 = (f32[1,1024]{1,0:T(1,128)S(1)}, f32[1,1024]{1,0:T(1,128)S(1)}, u32[]{:S(2)}, u32[]{:S(2)}) collective-permute-start(f32[1,1024]{1,0:T(1,128)S(1)} %add.6), channel_id=1, source_target_pairs={{0,8},{1,9},{2,10},{3,11},{4,12},{5,13},{6,14},{7,15},{8,0},{9,1},... | collective-permute-start | bytes 12296 | tf_op jit(solution)/shard_map/ppermute | solution.py:334
  69.3 0.7 copy-start.7

commit v3 on v2

v3 whole, which is shorter than its diff:
```python
import functools
import jax
import jax.numpy as jnp
from jax import lax
from jax.experimental import pallas as pl
from jax.experimental.pallas import tpu as pltpu
from jax.sharding import PartitionSpec as P

F32 = jnp.float32
BF16 = jnp.bfloat16
PAD = 8
STEPS = 4
LIMIT = 24 << 20
HBM = pl.BlockSpec(memory_space=pltpu.MemorySpace.HBM)
VMEM = pl.BlockSpec(memory_space=pltpu.MemorySpace.VMEM)


def dot(a, b):
    return jnp.dot(a, b, preferred_element_type=F32)


def dot_nt(a, b):
    return lax.dot_general(a, b, (((1,), (1,)), ((), ())), preferred_element_type=F32)


def dot_tn(a, b):
    return lax.dot_general(a, b, (((0,), (0,)), ((), ())), preferred_element_type=F32)


def iota(shape, axis):
    return lax.broadcasted_iota(jnp.int32, shape, axis)


def split3(x):
    hi = x.astype(BF16)
    rest = x - hi.astype(F32)
    mid = rest.astype(BF16)
    lo = (rest - mid.astype(F32)).astype(BF16)
    return jnp.concatenate([hi, mid, lo], axis=0)


def split2(x):
    hi = x.astype(BF16)
    lo = (x - hi.astype(F32)).astype(BF16)
    return jnp.concatenate([hi, lo], axis=0)


def twice(x):
    return jnp.concatenate([x, x], axis=0)


def expander(heads, head_dim, width, chunk):
    rows = lax.rem(iota((3 * heads, width), 0), heads)
    cols = iota((3 * heads, width), 1) // head_dim + chunk * (width // head_dim)
    return (rows == cols).astype(F32).astype(BF16)


def column(row):
    n = row.shape[1]
    return jnp.sum(jnp.where(iota((n, n), 0) == iota((n, n), 1), row, 0.0), axis=1, keepdims=True)


def tall(row):
    return jnp.broadcast_to(row, (128, row.shape[1])).T


def same_doc(ids_ref):
    ids = ids_ref[0:1, :]
    return tall(ids)[:, 0:1] == ids


def odd_core():
    return lax.rem(lax.axis_index("seq"), 2)


def put_half(j, keep_ref, send_ref, state, decay):
    width = state.shape[1]
    rows = state.shape[0]
    half = STEPS // 2
    place = slice((j % half) * width, (j % half + 1) * width)
    mine = odd_core() == j // half

    def put(ref):
        ref[0:rows, place] = state
        ref[rows : rows + 1, place] = decay

    pl.when(mine)(lambda: put(keep_ref))
    pl.when(jnp.logical_not(mine))(lambda: put(send_ref))


def get_half(j, mine_ref, other_ref, width):
    half = STEPS // 2
    place = slice((j % half) * width, (j % half + 1) * width)
    own = (odd_core() == j // half).astype(F32)
    return jnp.where(own > 0.5, mine_ref[:, place], other_ref[:, place])


def prepare_kernel(
    lengths_hbm,
    v_hbm,
    b_hbm,
    c_hbm,
    step_hbm,
    rate_hbm,
    gain_hbm,
    x_ref,
    keep_ref,
    send_ref,
    enter3_ref,
    sf3_ref,
    rows_ref,
    bm_ref,
    cm_ref,
    ids_ref,
    lengths,
    v,
    b,
    c,
    step,
    rate,
    gain,
    sems,
    v_sems,
):
    heads, length = step.shape
    total = v.shape[1]
    width = total // STEPS
    head_dim = total // heads
    small = [(step_hbm, step), (rate_hbm, rate), (gain_hbm, gain), (lengths_hbm, lengths), (b_hbm, b), (c_hbm, c)]
    small = [pltpu.make_async_copy(src, dst, sems.at[i]) for i, (src, dst) in enumerate(small)]
    parts = [slice(j * width, (j + 1) * width) for j in range(STEPS)]
    large = [pltpu.make_async_copy(v_hbm.at[:, p], v.at[:, p], v_sems.at[j]) for j, p in enumerate(parts)]
    for copy in small + large:
        copy.start()
    blank = jnp.zeros((PAD, keep_ref.shape[1]), F32)
    keep_ref[b.shape[0] :, :] = blank
    send_ref[b.shape[0] :, :] = blank
    upper = (iota((length, length), 0) <= iota((length, length), 1)).astype(F32).astype(BF16)
    for copy in small:
        copy.wait()
    sums = dot(split3(-(step[...] * column(rate[...]))), upper)
    level = sums[:heads] + sums[heads : 2 * heads] + sums[2 * heads :]
    middle = level[:, length // 2 - 1 : length // 2]
    last = level[:, length - 1 : length]
    place = iota((1, length), 1)
    ids = jnp.zeros((1, length), jnp.int32)
    before = jnp.int32(0)
    final = jnp.int32(0)
    start = -lax.axis_index("seq") * length
    for d in range(lengths.shape[0]):
        ids = ids + (place >= start).astype(jnp.int32)
        before = before + (start <= -1).astype(jnp.int32)
        final = final + (start <= length - 1).astype(jnp.int32)
        start = start + lengths[d]
    first_doc = (ids == before).astype(F32)
    last_doc = (ids == final).astype(F32)
    ids_ref[0:1, :] = ids.astype(F32)
    ids_ref[1:2, :] = first_doc
    ids_ref[2:3, :] = last_doc
    leave = jnp.exp(middle - level)
    enter3_ref[...] = split3(jnp.exp(level - middle))
    f3 = split3(leave)
    s3 = split3(step[...])
    sf3_ref[...] = split3(step[...] * leave)
    through = jnp.where(before == final, jnp.exp(last), 0.0)
    pick = iota((heads, 128), 1)
    table = jnp.where(pick == 0, jnp.exp(middle), 0.0)
    table = jnp.where(pick == 1, jnp.exp(last - middle), table)
    table = jnp.where(pick == 2, through, table)
    table = jnp.where(pick == 3, column(gain[...]), table)
    r3 = split3(table)
    bm = (b[...].astype(F32) * last_doc).astype(BF16)
    bm_ref[...] = bm
    cm_ref[...] = (c[...].astype(F32) * first_doc).astype(BF16)
    for j, part in enumerate(parts):
        spread = expander(heads, head_dim, width, j)
        rows = dot_tn(r3, spread)[:PAD]
        rows_ref[:, part] = rows
        steps = dot_tn(s3, spread)
        leaves = dot_tn(f3, spread)
        large[j].wait()
        scaled = (steps * v[:, part].astype(F32)).astype(BF16).astype(F32)
        x = leaves * scaled
        hi = x.astype(BF16)
        lo = (x - hi.astype(F32)).astype(BF16)
        x_ref[:, part] = hi
        state = (dot(bm, hi) + dot(bm, lo)) * rows[1:2, :]
        put_half(j, keep_ref, send_ref, state, rows[2:3, :])


def inner_kernel(x_ref, v_ref, teach_ref, b_ref, c_ref, enter3_ref, rows_ref, ids_ref, base_ref, st_ref):
    length, total = x_ref.shape
    width = total // STEPS
    heads = enter3_ref.shape[0] // 3
    same = same_doc(ids_ref)
    down = iota((length, length), 0)
    along = iota((length, length), 1)
    s = jnp.where(same & (down >= along), dot_tn(c_ref[...], b_ref[...]), 0.0).astype(BF16)
    st_ref[...] = jnp.where(same & (down <= along), dot_tn(b_ref[...], c_ref[...]), 0.0).astype(BF16)
    for j in range(STEPS):
        part = slice(j * width, (j + 1) * width)
        enter = dot_tn(enter3_ref[...], expander(heads, total // heads, width, j))
        base_ref[:, part] = (
            enter * dot(s, x_ref[:, part])
            + rows_ref[3:4, part] * v_ref[:, part].astype(F32)
            - teach_ref[:, part].astype(F32)
        )


def mismatch_kernel(
    base_ref, enter3_ref, rows_ref, cm_ref, mine_ref, other_ref, mm_ref, y_ref, keep_ref, send_ref
):
    length, total = base_ref.shape
    width = total // STEPS
    heads = enter3_ref.shape[0] // 3
    n = cm_ref.shape[0]
    blank = jnp.zeros((PAD, keep_ref.shape[1]), F32)
    keep_ref[n:, :] = blank
    send_ref[n:, :] = blank
    cm = cm_ref[...]
    sums = jnp.zeros((1, width), F32)
    for j in range(STEPS):
        part = slice(j * width, (j + 1) * width)
        enter = dot_tn(enter3_ref[...], expander(heads, total // heads, width, j))
        state = split2(get_half(j, mine_ref, other_ref, width) * rows_ref[0:1, part])
        mm = base_ref[:, part] + enter * dot_tn(twice(cm), state)
        mm_ref[:, part] = mm
        y = (enter * mm).astype(BF16)
        y_ref[:, part] = y
        sums = sums + jnp.sum(mm * mm, axis=0, keepdims=True)
        put_half(j, keep_ref, send_ref, dot(cm, y) * rows_ref[0:1, part], rows_ref[2:3, part])
    keep_ref[n + 1 : n + 2, :width] = sums
    send_ref[n + 1 : n + 2, :width] = sums


def pair_kernel(
    mm_ref,
    y_ref,
    x_ref,
    st_ref,
    sf3_ref,
    rows_ref,
    b_ref,
    c_ref,
    ids_ref,
    mine_ref,
    other_ref,
    g_ref,
    gb_ref,
    gc_hbm,
    pair,
    gc,
    sem,
):
    length, total = mm_ref.shape
    width = total // STEPS
    heads = sf3_ref.shape[0] // 3
    n = b_ref.shape[0]
    acc = jnp.zeros((2 * n, length), F32)
    for j in range(STEPS):
        part = slice(j * width, (j + 1) * width)
        y = y_ref[:, part]
        sf = dot_tn(sf3_ref[...], expander(heads, total // heads, width, j))
        g_ref[:, part] = rows_ref[3:4, part] * mm_ref[:, part] + sf * dot(st_ref[...], y)
        state = get_half(j, mine_ref, other_ref, width) * rows_ref[0:1, part]
        acc = acc + dot_nt(split2(state), y)
    pair[...] = dot_nt(y_ref[...], x_ref[...])
    keep = same_doc(ids_ref) & (iota((length, length), 0) >= iota((length, length), 1))
    masked = jnp.where(keep, pair[...], 0.0)
    hi = masked.astype(BF16)
    lo = (masked - hi.astype(F32)).astype(BF16)
    through = (acc[:n] + acc[n:]) * ids_ref[1:2, :]
    gc[...] = dot_nt(b_ref[...], hi) + dot_nt(b_ref[...], lo) + through
    copy = pltpu.make_async_copy(gc, gc_hbm, sem)
    copy.start()
    gb_ref[...] = dot(c_ref[...], hi) + dot(c_ref[...], lo)
    copy.wait()


def finish_kernel(
    g_ref, x_ref, sf3_ref, rows_ref, bm_ref, ids_ref, gb_part_ref, mine_ref, other_ref, gv_hbm, gb_hbm, gv, gb, sems
):
    length, total = g_ref.shape
    width = total // STEPS
    heads = sf3_ref.shape[0] // 3
    n = bm_ref.shape[0]
    acc = jnp.zeros((length, 2 * n), F32)
    copies = []
    for j in range(STEPS):
        part = slice(j * width, (j + 1) * width)
        sf = dot_tn(sf3_ref[...], expander(heads, total // heads, width, j))
        adjoint = split2(get_half(j, mine_ref, other_ref, width) * rows_ref[1:2, part])
        gv[:, part] = g_ref[:, part] + sf * dot_tn(twice(bm_ref[...]), adjoint)
        copies.append(pltpu.make_async_copy(gv.at[:, part], gv_hbm.at[:, part], sems.at[j]))
        copies[j].start()
        acc = acc + dot_nt(x_ref[:, part], adjoint)
    through = (acc[:, :n] + acc[:, n:]).T
    gb[...] = gb_part_ref[...] + through * ids_ref[2:3, :]
    copies.append(pltpu.make_async_copy(gb, gb_hbm, sems.at[STEPS]))
    copies[STEPS].start()
    for copy in copies:
        copy.wait()


def call(kernel, ins, outs, flops=0, in_specs=None, out_specs=None, scratch=()):
    size = sum(a.size * a.dtype.itemsize for a in ins) + sum(o.size * o.dtype.itemsize for o in outs)
    return pl.pallas_call(
        kernel,
        out_shape=outs,
        in_specs=in_specs or [VMEM] * len(ins),
        out_specs=out_specs or [VMEM] * len(outs),
        scratch_shapes=scratch,
        compiler_params=pltpu.CompilerParams(vmem_limit_bytes=LIMIT),
        cost_estimate=pl.CostEstimate(flops=flops, bytes_accessed=size, transcendentals=0),
    )(*ins)


def out(*shape, dtype=F32):
    return jax.ShapeDtypeStruct(shape, dtype)


def swap(x, devices):
    return lax.ppermute(x, "seq", [(i, i ^ 1) for i in range(devices)])


def shift(x, by, devices):
    return lax.ppermute(
        x, "seq", [(i, i + by) for i in range(devices) if 0 <= i + by < devices]
    )


def turn(x, by, devices):
    return lax.ppermute(x, "seq", [(i, (i + by) % devices) for i in range(devices)])


def chip_order(way, mine_ref, got_ref):
    near = odd_core() == (0 if way == 1 else 1)
    near = near.astype(F32) > 0.5
    mine, got = mine_ref[...], got_ref[...]
    return near, jnp.where(near, mine, got), jnp.where(near, got, mine)


def compose_kernel(way, keep_ref, got_ref, packed_ref):
    rows = keep_ref.shape[0] - PAD
    _near, first, second = chip_order(way, keep_ref, got_ref)
    packed_ref[:rows] = second[:rows] + second[rows : rows + 1] * first[:rows]
    a, b = first[rows:], second[rows:]
    packed_ref[rows:] = jnp.where(iota(a.shape, 0) == 0, a * b, a + b)


def arrive_kernel(way, keep_ref, got_ref, packed_ref, one_ref, two_ref, mine_ref, theirs_ref, line2_ref, line3_ref):
    rows = mine_ref.shape[0]
    near, first, _second = chip_order(way, keep_ref, got_ref)
    state = one_ref[:rows] + one_ref[rows : rows + 1] * two_ref[:rows]
    inside = first[:rows] + first[rows : rows + 1] * state
    mine_ref[...] = jnp.where(near, state, inside)
    theirs_ref[...] = jnp.where(near, inside, state)
    line = slice(rows + 1, rows + 2)
    line2_ref[...] = packed_ref[line] + one_ref[line]
    line3_ref[...] = packed_ref[line] + one_ref[line] + two_ref[line]


def loss_kernel(scale, *refs):
    total = refs[0][...]
    for ref in refs[1:-1]:
        total = total + ref[...]
    refs[-1][...] = jnp.broadcast_to(jnp.sum(total) * scale, (1, 1))


def carry(keep, send, devices, way, beside):
    rows, width = keep.shape[0] - PAD, keep.shape[1]
    got = swap(send, devices)
    [packed] = call(functools.partial(compose_kernel, way), [keep, got], [out(rows + PAD, width)])
    reach = max(1, devices // 8)
    move = shift if way == 1 else turn
    one = move(packed, 2 * way, devices)
    two = move(packed, 4 * way, devices)
    if reach > 2:
        state = one[:rows] + one[rows : rows + 1] * two[:rows]
        run = one[rows : rows + 1] * two[rows : rows + 1]
        span = 2
        while span < reach:
            more = shift(jnp.concatenate([state, jnp.broadcast_to(run, (PAD, width))], axis=0), 2 * span * way, devices)
            state = state + run * more[:rows]
            run = run * more[rows : rows + 1]
            span *= 2
        one = jnp.concatenate([state, one[rows:]], axis=0)
        two = jnp.concatenate([jnp.zeros_like(state), two[rows:]], axis=0)
    mine, theirs, line2, line3 = call(
        functools.partial(arrive_kernel, way),
        [keep, got, packed, one, two],
        [out(rows, width), out(rows, width), out(1, width), out(1, width)],
    )
    theirs, beside = lax.optimization_barrier((theirs, beside))
    return mine, swap(theirs, devices), line2, line3, beside


def loss_lines(line2, line3, devices):
    chips = devices // 2
    if chips == 8:
        return [line3, turn(line3, -6, devices), turn(line2, -12, devices)]
    span = 2
    while span < chips:
        line2 = line2 + turn(line2, -2 * span, devices)
        span *= 2
    return [line2]


def local(values, b_proj, c_proj, step_sizes, decay_rates, skip_gain, teacher, doc_lengths):
    length, total = values.shape
    heads = step_sizes.shape[1]
    state = b_proj.shape[1]
    devices = lax.axis_size("seq")
    b = b_proj.T
    c = c_proj.T
    half = out(state + PAD, total // 2)
    thirds = out(3 * heads, length, dtype=BF16)
    narrow = out(state, length, dtype=BF16)
    square = 2 * length * length * total
    dma = pltpu.SemaphoreType.DMA
    x, keep, send, enter3, sf3, rows, bm, cm, ids = call(
        prepare_kernel,
        [
            pltpu.with_memory_space_constraint(a, pltpu.MemorySpace.HBM)
            for a in (
                doc_lengths,
                values,
                b,
                c,
                step_sizes.T,
                decay_rates.reshape(1, heads),
                skip_gain.reshape(1, heads),
            )
        ],
        [
            out(length, total, dtype=BF16),
            half,
            half,
            thirds,
            thirds,
            out(PAD, total),
            narrow,
            narrow,
            out(PAD, length),
        ],
        in_specs=[HBM] * 7,
        scratch=[
            pltpu.SMEM(doc_lengths.shape, jnp.int32),
            pltpu.VMEM((length, total), BF16),
            pltpu.VMEM((state, length), BF16),
            pltpu.VMEM((state, length), BF16),
            pltpu.VMEM((heads, length), F32),
            pltpu.VMEM((1, heads), F32),
            pltpu.VMEM((1, heads), F32),
            dma((6,)),
            dma((STEPS,)),
        ],
    )
    inner = call(
        inner_kernel,
        [x, values, teacher, b, c, enter3, rows, ids],
        [out(length, total), out(length, length, dtype=BF16)],
        square,
    )
    state_mine, state_other, _, _, (base, score_t) = carry(keep, send, devices, 1, inner)
    mm, y, back_keep, back_send = call(
        mismatch_kernel,
        [base, enter3, rows, cm, state_mine, state_other],
        [out(length, total), out(length, total, dtype=BF16), half, half],
    )
    pairs = call(
        pair_kernel,
        [mm, y, x, score_t, sf3, rows, b, c, ids, state_mine, state_other],
        [out(length, total), out(state, length), out(state, length)],
        2 * square,
        out_specs=[VMEM, VMEM, HBM],
        scratch=[pltpu.VMEM((length, length), F32), pltpu.VMEM((state, length), F32), dma],
    )
    adj_mine, adj_other, line2, line3, (g, gb_part, grad_c) = carry(back_keep, back_send, devices, -1, pairs)
    lines = loss_lines(line2, line3, devices)
    grad_values, grad_b = call(
        finish_kernel,
        [g, x, sf3, rows, bm, ids, gb_part, adj_mine, adj_other],
        [out(length, total), out(state, length)],
        out_specs=[HBM, HBM],
        scratch=[pltpu.VMEM((length, total), F32), pltpu.VMEM((state, length), F32), dma((STEPS + 1,))],
    )
    lines, grad_values = lax.optimization_barrier((lines, grad_values))
    scale = 1.0 / (devices * length * total)
    [loss] = call(functools.partial(loss_kernel, scale), lines, [out(1, 1)])
    return loss.reshape(1), grad_values, grad_b.T, grad_c.T


def solution(mesh):
    rows = P(("groups", "seq"), None)
    in_specs = (rows, rows, rows, rows, P(), P(), rows, P("groups"))
    out_specs = (P("groups"), rows, rows, rows)
    return jax.shard_map(local, mesh=mesh, in_specs=in_specs, out_specs=out_specs, check_vma=False)
```

time: 79.5 us -> 61.2 us (0.77)
  Pallas kernels: 41.2 us -> 20.1 us
  starting transfers between devices: 19.3 us -> 23.6 us
  waiting for transfers between devices: 10.4 us -> 13.2 us
  between operations: 2.56 us -> 0.77 us
  local copies, waits for them, and re-layouts: 4.79 us -> 3.27 us
    pallas_call x9 -> x10, Pallas kernels: 41.2 us -> 20.1 us  [call(): pl.pallas_call(kernel, out_shape=outs, in_specs=in_specs or [VMEM] * len(...]
    ppermute x3 -> x4, starting transfers between devices: 8.86 us -> 14.5 us  [turn(): lax.ppermute(x, 'seq', [(i, (i + by) % devices) for i in range(devices)])]
    ppermute x3 -> x4, waiting for transfers between devices: 5.84 us -> 8.36 us  [turn(): lax.ppermute(x, 'seq', [(i, (i + by) % devices) for i in range(devices)])]
    unnamed x16 -> x8, local copies, waits for them, and re-layouts: 4.79 us -> 3.27 us
    ppermute x3 -> x2, starting transfers between devices: 9.7 us -> 8.31 us  [shift(): lax.ppermute(x, 'seq', [(i, i + by) for i in range(devices) if 0 <= i + b...]
  transfers between devices with their start and end apart: 10 -> 10, of which waited for: 5 -> 6; matrix products, arithmetic and copies ran while one was open for 1% -> 0% of each run, Pallas kernels for 23% -> 16%
where the time goes in v3:
time: 61.2 us; the launch traced here: 61 us
  starting transfers between devices  23.6 us (39%)
  Pallas kernels  20.1 us (33%)
  waiting for transfers between devices  13.2 us (22%)
  local copies, waits for them, and re-layouts  3.27 us (5%)
  between operations  0.77 us (1%)
    pallas_call x10, Pallas kernels, call(): pl.pallas_call(kernel, out_shape=outs, in_specs=in_specs or [VMEM] * len(...  20.1 us
    ppermute x4, starting transfers between devices, turn(): lax.ppermute(x, 'seq', [(i, (i + by) % devices) for i in range(devices)])  14.5 us
    ppermute x4, waiting for transfers between devices, turn(): lax.ppermute(x, 'seq', [(i, (i + by) % devices) for i in range(devices)])  8.36 us
    ppermute x2, starting transfers between devices, shift(): lax.ppermute(x, 'seq', [(i, i + by) for i in range(devices) if 0 <= i + b...  8.31 us
    ppermute x4, waiting for transfers between devices, swap(): return lax.ppermute(x, 'seq', [(i, i ^ 1) for i in range(devices)])  4.2 us
    unnamed x8, local copies, waits for them, and re-layouts  3.27 us
  transfers between devices with their start and end apart: 10, of which 6 were waited for; matrix products, arithmetic and copies ran while one was open for 0% of the time, Pallas kernels for 16%

profile of v3, /device:TPU:0, one launch (start us, length us, event | category | flops | bytes accessed | tf_op | source)
XLA Modules:
  0.0 61.0 jit_solution(18038291620826659477)
XLA Ops:
  0.6 0.0 copy-start
  0.6 5.9 %shard_map.111 = (bf16[512,2048]{1,0:T(8,128)(2,1)S(1)}, f32[72,1024]{1,0:T(8,128)S(1)}, f32[72,1024]{1,0:T(8,128)S(1)}, bf16[96,512]{1,0:T(8,128)(2,1)S(1)}, bf...) custom-call(s32[16]{0:T(128)} %lengths_hbm.1, ...), custom_call_target="tpu_custom_call" | custom-call | bytes 5390656 | tf_op jit(solution)/shard_map/pallas_call | solution.py:307
  6.6 0.5 collective-permute-start
  7.1 1.2 %collective-permute-done.got_ref = f32[72,1024]{1,0:T(8,128)S(1)} collective-permute-done((f32[72,1024]{1,0:T(8,128)S(1)}, f32[72,1024]{1,0:T(8,128)S(1)}, u32[]{:S(2)}, u32[]{:S(2)}) %collective-permute-start) | collective-permute-done | bytes 294944 | tf_op jit(solution)/shard_map/ppermute | solution.py:323
  8.3 0.1 shard_map.112.packed_ref
  8.4 4.9 %collective-permute-start.2 = (f32[72,1024]{1,0:T(8,128)S(1)}, f32[72,1024]{1,0:T(8,128)S(1)}, u32[]{:S(2)}, u32[]{:S(2)}) collective-permute-start(f32[72,1024]{1,0:T(8,128)S(1)} %shard_map.112.packed_ref), channel_id=1, source_target_pairs={{0,4},{1,5},{2,6},{3,7},{4,8},{5,9},{6,10},{7,11},{8,12},{9,13},{1... | collective-permute-start | bytes 884744 | tf_op jit(solution)/shard_map/ppermute | solution.py:327
  13.2 3.4 %collective-permute-start.1 = (f32[72,1024]{1,0:T(8,128)S(1)}, f32[72,1024]{1,0:T(8,128)S(1)}, u32[]{:S(2)}, u32[]{:S(2)}) collective-permute-start(f32[72,1024]{1,0:T(8,128)S(1)} %shard_map.112.packed_ref), channel_id=1, source_target_pairs={{0,2},{1,3},{2,4},{3,5},{4,6},{5,7},{6,8},{7,9},{8,10},{9,11},{10,... | collective-permute-start | bytes 884744 | tf_op jit(solution)/shard_map/ppermute | solution.py:327
  16.7 0.0 copy-done
  16.7 0.0 copy-start.1
  16.7 1.6 %copy-done.1 = bf16[512,2048]{1,0:T(8,128)(2,1)S(1)} copy-done((bf16[512,2048]{1,0:T(8,128)(2,1)S(1)}, bf16[512,2048]{1,0:T(8,128)(2,1)}, u32[]{:S(2)}) %copy-start.1) | copy-done | bytes 2097176
  18.3 0.0 copy-start.2
  18.3 0.8 %copy-done.2 = bf16[512,64]{0,1:T(8,128)(2,1)S(1)} copy-done((bf16[512,64]{0,1:T(8,128)(2,1)S(1)}, bf16[512,64]{0,1:T(8,128)(2,1)}, u32[]{:S(2)}) %copy-start.2) | copy-done | bytes 65560
  19.1 0.0 copy-start.3
  19.1 0.8 %copy-done.3 = bf16[512,64]{0,1:T(8,128)(2,1)S(1)} copy-done((bf16[512,64]{0,1:T(8,128)(2,1)S(1)}, bf16[512,64]{0,1:T(8,128)(2,1)}, u32[]{:S(2)}) %copy-start.3) | copy-done | bytes 65560
  20.0 2.3 %shard_map.114 = (f32[512,2048]{1,0:T(8,128)S(1)}, bf16[512,512]{1,0:T(8,128)(2,1)S(1)}) custom-call(bf16[512,2048]{1,0:T(8,128)(2,1)S(1)} %get-tuple-element.44.x_ref, bf16[512,2048]{1,0:T(8,128)(2,1)S(1)} %copy-done, bf16[512,2048]{1,0:T(8,128)(2,1)S(1)} %copy-done.1, bf16[64,512]{1,0:T(8,128)(2,1)S(1)} %bitcast.9, bf16[64,512]{1,0:T(8,128)(2,1)S(1)} %bitcast.12, ...), custom_call_target="tpu_custom_call" | custom-call | flops 1073741824 | bytes 11321344 | tf_op jit(solution)/shard_map/pallas_call | solution.py:307
  22.3 0.0 collective-permute-done.2.two_ref
  22.3 0.7 %collective-permute-done.1.one_ref = f32[72,1024]{1,0:T(8,128)S(1)} collective-permute-done((f32[72,1024]{1,0:T(8,128)S(1)}, f32[72,1024]{1,0:T(8,128)S(1)}, u32[]{:S(2)}, u32[]{:S(2)}) %collective-permute-start.1) | collective-permute-done | bytes 294944 | tf_op jit(solution)/shard_map/ppermute | solution.py:327
  22.9 0.6 %shard_map.113 = (f32[64,1024]{1,0:T(8,128)S(1)}, f32[64,1024]{1,0:T(8,128)S(1)}, f32[1,1024]{1,0:T(1,128)}, f32[1,1024]{1,0:T(1,128)}) custom-call(f32[72,1024]{1,0:T(8,128)S(1)} %get-tuple-element.41.keep_ref, f32[72,1024]{1,0:T(8,128)S(1)} %collective-permute-done.got_ref, f32[72,1024]{1,0:T(8,128)S(1)} %shard_map.112.packed_ref, ...), custom_call_target="tpu_custom_call" | custom-call | bytes 2007040 | tf_op jit(solution)/shard_map/pallas_call | solution.py:307
  23.6 0.0 collective-permute-start.3
  23.6 1.5 %collective-permute-done.3.other_ref = f32[64,1024]{1,0:T(8,128)S(1)} collective-permute-done((f32[64,1024]{1,0:T(8,128)S(1)}, f32[64,1024]{1,0:T(8,128)S(1)}, u32[]{:S(2)}, u32[]{:S(2)}) %collective-permute-start.3) | collective-permute-done | bytes 262176 | tf_op jit(solution)/shard_map/ppermute | solution.py:323
  25.1 2.9 %shard_map.115 = (f32[512,2048]{1,0:T(8,128)S(1)}, bf16[512,2048]{1,0:T(8,128)(2,1)S(1)}, f32[72,1024]{1,0:T(8,128)S(1)}, f32[72,1024]{1,0:T(8,128)S(1)}) custom-call(f32[512,2048]{1,0:T(8,128)S(1)} %get-tuple-element.50.base_ref, bf16[96,512]{1,0:T(8,128)(2,1)S(1)} %get-tuple-element.45.enter3_ref, f32[8,2048]{1,0:T(8,128)S(1)} %get-tuple-element.46.rows_ref, ...), custom_call_target="tpu_custom_call" | custom-call | bytes 11829248 | tf_op jit(solution)/shard_map/pallas_call | solution.py:307
  28.0 0.2 collective-permute-start.4
  28.2 1.5 %collective-permute-done.4.got_ref = f32[72,1024]{1,0:T(8,128)S(1)} collective-permute-done((f32[72,1024]{1,0:T(8,128)S(1)}, f32[72,1024]{1,0:T(8,128)S(1)}, u32[]{:S(2)}, u32[]{:S(2)}) %collective-permute-start.4) | collective-permute-done | bytes 294944 | tf_op jit(solution)/shard_map/ppermute | solution.py:323
  29.7 0.1 shard_map.116.packed_ref
  29.7 8.7 %collective-permute-start.6 = (f32[72,1024]{1,0:T(8,128)S(1)}, f32[72,1024]{1,0:T(8,128)S(1)}, u32[]{:S(2)}, u32[]{:S(2)}) collective-permute-start(f32[72,1024]{1,0:T(8,128)S(1)} %shard_map.116.packed_ref), channel_id=1, source_target_pairs={{0,12},{1,13},{2,14},{3,15},{4,0},{5,1},{6,2},{7,3},{8,4},{9,5},{1... | collective-permute-start | bytes 884744 | tf_op jit(solution)/shard_map/ppermute | solution.py:333
  38.4 0.0 collective-permute-start.5
  38.4 4.5 %shard_map.118 = (f32[512,2048]{1,0:T(8,128)S(1)}, f32[64,512]{1,0:T(8,128)S(1)}, f32[64,512]{1,0:T(8,128)}) custom-call(f32[512,2048]{1,0:T(8,128)S(1)} %get-tuple-element.59.mm_ref, bf16[512,2048]{1,0:T(8,128)(2,1)S(1)} %get-tuple-element.60.y_ref, bf16[512,2048]{1,0:T(8,128)(2,1)S(1)} %get-tuple-element.44.x_ref, ...), custom_call_target="tpu_custom_call" | custom-call | flops 2147483648 | bytes 14204928 | tf_op jit(solution)/shard_map/pallas_call | solution.py:307
  42.9 2.8 %collective-permute-done.6.two_ref = f32[72,1024]{1,0:T(8,128)S(1)} collective-permute-done((f32[72,1024]{1,0:T(8,128)S(1)}, f32[72,1024]{1,0:T(8,128)S(1)}, u32[]{:S(2)}, u32[]{:S(2)}) %collective-permute-start.6) | collective-permute-done | bytes 294944 | tf_op jit(solution)/shard_map/ppermute | solution.py:333
  45.8 5.5 %collective-permute-done.5.one_ref = f32[72,1024]{1,0:T(8,128)S(1)} collective-permute-done((f32[72,1024]{1,0:T(8,128)S(1)}, f32[72,1024]{1,0:T(8,128)S(1)}, u32[]{:S(2)}, u32[]{:S(2)}) %collective-permute-start.5) | collective-permute-done | bytes 294944 | tf_op jit(solution)/shard_map/ppermute | solution.py:333
  51.3 0.1 shard_map.117
  51.4 0.1 collective-permute-start.9
  51.5 0.1 collective-permute-start.8
  51.5 5.8 %collective-permute-start.7 = (f32[1,1024]{1,0:T(1,128)S(1)}, f32[1,1024]{1,0:T(1,128)S(1)}, u32[]{:S(2)}, u32[]{:S(2)}) collective-permute-start(f32[1,1024]{1,0:T(1,128)S(1)} %get-tuple-element.72.refs_0_), channel_id=1, source_target_pairs={{0,10},{1,11},{2,12},{3,13},{4,14},{5,15},{6,0},{7,1},{8,2},{9,3},... | collective-permute-start | bytes 12296 | tf_op jit(solution)/shard_map/ppermute | solution.py:333
  57.3 0.0 collective-permute-done.9.other_ref
  57.3 2.9 %shard_map.119 = (f32[512,2048]{1,0:T(8,128)}, f32[64,512]{1,0:T(8,128)}) custom-call(f32[512,2048]{1,0:T(8,128)S(1)} %get-tuple-element.66.g_ref, bf16[512,2048]{1,0:T(8,128)(2,1)S(1)} %get-tuple-element.44.x_ref, bf16[96,512]{1,0:T(8,128)(2,1)S(1)} %get-tuple-element.62.sf3_ref, f32[8,2048]{1,0:T(8,128)S(1)} %get-tuple-element.46.rows_ref, ...), custom_call_target="tpu_custom_call" | custom-call | bytes 11517952 | tf_op jit(solution)/shard_map/pallas_call | solution.py:307
  60.3 0.0 collective-permute-done.8.refs_2_
  60.3 0.0 collective-permute-done.7.refs_1_
  60.3 0.6 %shard_map.120 = f32[1,1]{1,0:T(1,128)} custom-call(f32[1,1024]{1,0:T(1,128)S(1)} %get-tuple-element.72.refs_0_, f32[1,1024]{1,0:T(1,128)S(1)} %collective-permute-done.7.refs_1_, f32[1,1024]{1,0:T(1,128)S(1)} %collective-permute-done.8.refs_2_), custom_call_target="tpu_custom_call" | custom-call | bytes 12292 | tf_op jit(solution)/shard_map/pallas_call | solution.py:307
Async XLA Ops:
  0.6 16.1 %copy-start = (bf16[512,2048]{1,0:T(8,128)(2,1)S(1)}, bf16[512,2048]{1,0:T(8,128)(2,1)}, u32[]{:S(2)}) copy-start(bf16[512,2048]{1,0:T(8,128)(2,1)} %v_ref.1) | copy-start | bytes 6291460
  6.6 1.7 %collective-permute-start = (f32[72,1024]{1,0:T(8,128)S(1)}, f32[72,1024]{1,0:T(8,128)S(1)}, u32[]{:S(2)}, u32[]{:S(2)}) collective-permute-start(f32[72,1024]{1,0:T(8,128)S(1)} %get-tuple-element.42), channel_id=1, source_target_pairs={{0,1},{1,0},{2,3},{3,2},{4,5},{5,4},{6,7},{7,6},{8,9},{9,8},{10,11... | collective-permute-start | bytes 884744 | tf_op jit(solution)/shard_map/ppermute | solution.py:323
  8.4 13.9 %collective-permute-start.2 = (f32[72,1024]{1,0:T(8,128)S(1)}, f32[72,1024]{1,0:T(8,128)S(1)}, u32[]{:S(2)}, u32[]{:S(2)}) collective-permute-start(f32[72,1024]{1,0:T(8,128)S(1)} %shard_map.112.packed_ref), channel_id=1, source_target_pairs={{0,4},{1,5},{2,6},{3,7},{4,8},{5,9},{6,10},{7,11},{8,12},{9,13},{1... | collective-permute-start | bytes 884744 | tf_op jit(solution)/shard_map/ppermute | solution.py:327
  13.2 9.7 %collective-permute-start.1 = (f32[72,1024]{1,0:T(8,128)S(1)}, f32[72,1024]{1,0:T(8,128)S(1)}, u32[]{:S(2)}, u32[]{:S(2)}) collective-permute-start(f32[72,1024]{1,0:T(8,128)S(1)} %shard_map.112.packed_ref), channel_id=1, source_target_pairs={{0,2},{1,3},{2,4},{3,5},{4,6},{5,7},{6,8},{7,9},{8,10},{9,11},{10,... | collective-permute-start | bytes 884744 | tf_op jit(solution)/shard_map/ppermute | solution.py:327
  16.7 1.6 %copy-start.1 = (bf16[512,2048]{1,0:T(8,128)(2,1)S(1)}, bf16[512,2048]{1,0:T(8,128)(2,1)}, u32[]{:S(2)}) copy-start(bf16[512,2048]{1,0:T(8,128)(2,1)} %teach_ref.1) | copy-start | bytes 6291460
  18.3 0.8 %copy-start.2 = (bf16[512,64]{0,1:T(8,128)(2,1)S(1)}, bf16[512,64]{0,1:T(8,128)(2,1)}, u32[]{:S(2)}) copy-start(bf16[512,64]{0,1:T(8,128)(2,1)} %param.9) | copy-start | bytes 196612
  19.1 0.8 %copy-start.3 = (bf16[512,64]{0,1:T(8,128)(2,1)S(1)}, bf16[512,64]{0,1:T(8,128)(2,1)}, u32[]{:S(2)}) copy-start(bf16[512,64]{0,1:T(8,128)(2,1)} %param.10) | copy-start | bytes 196612
  23.6 1.5 %collective-permute-start.3 = (f32[64,1024]{1,0:T(8,128)S(1)}, f32[64,1024]{1,0:T(8,128)S(1)}, u32[]{:S(2)}, u32[]{:S(2)}) collective-permute-start(f32[64,1024]{1,0:T(8,128)S(1)} %get-tuple-element.53), channel_id=1, source_target_pairs={{0,1},{1,0},{2,3},{3,2},{4,5},{5,4},{6,7},{7,6},{8,9},{9,8},{10,11... | collective-permute-start | bytes 786440 | tf_op jit(solution)/shard_map/ppermute | solution.py:323
  28.0 1.6 %collective-permute-start.4 = (f32[72,1024]{1,0:T(8,128)S(1)}, f32[72,1024]{1,0:T(8,128)S(1)}, u32[]{:S(2)}, u32[]{:S(2)}) collective-permute-start(f32[72,1024]{1,0:T(8,128)S(1)} %get-tuple-element.55), channel_id=1, source_target_pairs={{0,1},{1,0},{2,3},{3,2},{4,5},{5,4},{6,7},{7,6},{8,9},{9,8},{10,11... | collective-permute-start | bytes 884744 | tf_op jit(solution)/shard_map/ppermute | solution.py:323
  29.7 16.0 %collective-permute-start.6 = (f32[72,1024]{1,0:T(8,128)S(1)}, f32[72,1024]{1,0:T(8,128)S(1)}, u32[]{:S(2)}, u32[]{:S(2)}) collective-permute-start(f32[72,1024]{1,0:T(8,128)S(1)} %shard_map.116.packed_ref), channel_id=1, source_target_pairs={{0,12},{1,13},{2,14},{3,15},{4,0},{5,1},{6,2},{7,3},{8,4},{9,5},{1... | collective-permute-start | bytes 884744 | tf_op jit(solution)/shard_map/ppermute | solution.py:333
  38.4 12.9 %collective-permute-start.5 = (f32[72,1024]{1,0:T(8,128)S(1)}, f32[72,1024]{1,0:T(8,128)S(1)}, u32[]{:S(2)}, u32[]{:S(2)}) collective-permute-start(f32[72,1024]{1,0:T(8,128)S(1)} %shard_map.116.packed_ref), channel_id=1, source_target_pairs={{0,14},{1,15},{2,0},{3,1},{4,2},{5,3},{6,4},{7,5},{8,6},{9,7},{10,... | collective-permute-start | bytes 884744 | tf_op jit(solution)/shard_map/ppermute | solution.py:333
  51.4 5.9 %collective-permute-start.9 = (f32[64,1024]{1,0:T(8,128)S(1)}, f32[64,1024]{1,0:T(8,128)S(1)}, u32[]{:S(2)}, u32[]{:S(2)}) collective-permute-start(f32[64,1024]{1,0:T(8,128)S(1)} %get-tuple-element.70), channel_id=1, source_target_pairs={{0,1},{1,0},{2,3},{3,2},{4,5},{5,4},{6,7},{7,6},{8,9},{9,8},{10,11... | collective-permute-start | bytes 786440 | tf_op jit(solution)/shard_map/ppermute | solution.py:323
  51.5 8.8 %collective-permute-start.8 = (f32[1,1024]{1,0:T(1,128)S(1)}, f32[1,1024]{1,0:T(1,128)S(1)}, u32[]{:S(2)}, u32[]{:S(2)}) collective-permute-start(f32[1,1024]{1,0:T(1,128)S(1)} %get-tuple-element.57), channel_id=1, source_target_pairs={{0,4},{1,5},{2,6},{3,7},{4,8},{5,9},{6,10},{7,11},{8,12},{9,13},{1... | collective-permute-start | bytes 12296 | tf_op jit(solution)/shard_map/ppermute | solution.py:333
  51.5 8.8 %collective-permute-start.7 = (f32[1,1024]{1,0:T(1,128)S(1)}, f32[1,1024]{1,0:T(1,128)S(1)}, u32[]{:S(2)}, u32[]{:S(2)}) collective-permute-start(f32[1,1024]{1,0:T(1,128)S(1)} %get-tuple-element.72.refs_0_), channel_id=1, source_target_pairs={{0,10},{1,11},{2,12},{3,13},{4,14},{5,15},{6,0},{7,1},{8,2},{9,3},... | collective-permute-start | bytes 12296 | tf_op jit(solution)/shard_map/ppermute | solution.py:333

commit v4 on v3

--- a/solution.py
+++ b/solution.py
@@ -73,26 +73,36 @@
     return lax.rem(lax.axis_index("seq"), 2)
 
 
+def tiles(j, rows, width, ref):
+    groups = ref.shape[0] // (rows // 8)
+    inside = width // 128
+    return [
+        (r * groups + (j % (STEPS // 2)) * inside + q, r, q) for r in range(rows // 8) for q in range(inside)
+    ]
+
+
 def put_half(j, keep_ref, send_ref, state, decay):
-    width = state.shape[1]
-    rows = state.shape[0]
-    half = STEPS // 2
-    place = slice((j % half) * width, (j % half + 1) * width)
-    mine = odd_core() == j // half
+    rows, width = state.shape
+    groups = keep_ref.shape[0] // (rows // 8)
+    last = groups * (rows // 8)
+    mine = odd_core() == j // (STEPS // 2)
 
     def put(ref):
-        ref[0:rows, place] = state
-        ref[rows : rows + 1, place] = decay
+        for t, r, q in tiles(j, rows, width, ref):
+            ref[t] = state[r * 8 : (r + 1) * 8, q * 128 : (q + 1) * 128]
+            if r == 0:
+                ref[last, t % groups : t % groups + 1, :] = decay[:, q * 128 : (q + 1) * 128]
 
     pl.when(mine)(lambda: put(keep_ref))
     pl.when(jnp.logical_not(mine))(lambda: put(send_ref))
 
 
-def get_half(j, mine_ref, other_ref, width):
-    half = STEPS // 2
-    place = slice((j % half) * width, (j % half + 1) * width)
-    own = (odd_core() == j // half).astype(F32)
-    return jnp.where(own > 0.5, mine_ref[:, place], other_ref[:, place])
+def get_half(j, rows, mine_ref, other_ref, width):
+    own = (odd_core() == j // (STEPS // 2)).astype(F32) > 0.5
+    lines = [[] for _ in range(rows // 8)]
+    for t, r, _q in tiles(j, rows, width, mine_ref):
+        lines[r].append(jnp.where(own, mine_ref[t], other_ref[t]))
+    return jnp.concatenate([jnp.concatenate(line, axis=1) for line in lines], axis=0)
 
 
 def prepare_kernel(
@@ -132,9 +142,9 @@
     large = [pltpu.make_async_copy(v_hbm.at[:, p], v.at[:, p], v_sems.at[j]) for j, p in enumerate(parts)]
     for copy in small + large:
         copy.start()
-    blank = jnp.zeros((PAD, keep_ref.shape[1]), F32)
-    keep_ref[b.shape[0] :, :] = blank
-    send_ref[b.shape[0] :, :] = blank
+    last_tile = keep_ref.shape[0] - 1
+    keep_ref[last_tile] = jnp.zeros((8, 128), F32)
+    send_ref[last_tile] = jnp.zeros((8, 128), F32)
     upper = (iota((length, length), 0) <= iota((length, length), 1)).astype(F32).astype(BF16)
     for copy in small:
         copy.wait()
@@ -207,30 +217,28 @@
         )
 
 
-def mismatch_kernel(
-    base_ref, enter3_ref, rows_ref, cm_ref, mine_ref, other_ref, mm_ref, y_ref, keep_ref, send_ref
-):
+def mismatch_kernel(base_ref, enter3_ref, rows_ref, cm_ref, mine_ref, other_ref, mm_ref, y_ref, keep_ref, send_ref):
     length, total = base_ref.shape
     width = total // STEPS
     heads = enter3_ref.shape[0] // 3
-    n = cm_ref.shape[0]
-    blank = jnp.zeros((PAD, keep_ref.shape[1]), F32)
-    keep_ref[n:, :] = blank
-    send_ref[n:, :] = blank
     cm = cm_ref[...]
-    sums = jnp.zeros((1, width), F32)
+    sums = jnp.zeros((8, width), F32)
     for j in range(STEPS):
         part = slice(j * width, (j + 1) * width)
         enter = dot_tn(enter3_ref[...], expander(heads, total // heads, width, j))
-        state = split2(get_half(j, mine_ref, other_ref, width) * rows_ref[0:1, part])
+        state = split2(get_half(j, cm.shape[0], mine_ref, other_ref, width) * rows_ref[0:1, part])
         mm = base_ref[:, part] + enter * dot_tn(twice(cm), state)
         mm_ref[:, part] = mm
         y = (enter * mm).astype(BF16)
         y_ref[:, part] = y
-        sums = sums + jnp.sum(mm * mm, axis=0, keepdims=True)
+        sums = sums + jnp.sum((mm * mm).reshape(length // 8, 8, width), axis=0)
         put_half(j, keep_ref, send_ref, dot(cm, y) * rows_ref[0:1, part], rows_ref[2:3, part])
-    keep_ref[n + 1 : n + 2, :width] = sums
-    send_ref[n + 1 : n + 2, :width] = sums
+    line = sums[:, :128]
+    for q in range(1, width // 128):
+        line = line + sums[:, q * 128 : (q + 1) * 128]
+    last_tile = keep_ref.shape[0] - 1
+    keep_ref[last_tile] = line
+    send_ref[last_tile] = line
 
 
 def pair_kernel(
@@ -262,7 +270,7 @@
         y = y_ref[:, part]
         sf = dot_tn(sf3_ref[...], expander(heads, total // heads, width, j))
         g_ref[:, part] = rows_ref[3:4, part] * mm_ref[:, part] + sf * dot(st_ref[...], y)
-        state = get_half(j, mine_ref, other_ref, width) * rows_ref[0:1, part]
+        state = get_half(j, n, mine_ref, other_ref, width) * rows_ref[0:1, part]
         acc = acc + dot_nt(split2(state), y)
     pair[...] = dot_nt(y_ref[...], x_ref[...])
     keep = same_doc(ids_ref) & (iota((length, length), 0) >= iota((length, length), 1))
@@ -278,7 +286,22 @@
 
 
 def finish_kernel(
-    g_ref, x_ref, sf3_ref, rows_ref, bm_ref, ids_ref, gb_part_ref, mine_ref, other_ref, gv_hbm, gb_hbm, gv, gb, sems
+    scale,
+    g_ref,
+    x_ref,
+    sf3_ref,
+    rows_ref,
+    bm_ref,
+    ids_ref,
+    gb_part_ref,
+    mine_ref,
+    other_ref,
+    gv_hbm,
+    gb_hbm,
+    loss_ref,
+    gv,
+    gb,
+    sems,
 ):
     length, total = g_ref.shape
     width = total // STEPS
@@ -289,11 +312,13 @@
     for j in range(STEPS):
         part = slice(j * width, (j + 1) * width)
         sf = dot_tn(sf3_ref[...], expander(heads, total // heads, width, j))
-        adjoint = split2(get_half(j, mine_ref, other_ref, width) * rows_ref[1:2, part])
+        adjoint = split2(get_half(j, n, mine_ref, other_ref, width) * rows_ref[1:2, part])
         gv[:, part] = g_ref[:, part] + sf * dot_tn(twice(bm_ref[...]), adjoint)
         copies.append(pltpu.make_async_copy(gv.at[:, part], gv_hbm.at[:, part], sems.at[j]))
         copies[j].start()
         acc = acc + dot_nt(x_ref[:, part], adjoint)
+    last_tile = mine_ref.shape[0] - 1
+    loss_ref[...] = jnp.broadcast_to(jnp.sum(mine_ref[last_tile] + other_ref[last_tile]) * scale, (1, 1))
     through = (acc[:, :n] + acc[:, n:]).T
     gb[...] = gb_part_ref[...] + through * ids_ref[2:3, :]
     copies.append(pltpu.make_async_copy(gb, gb_hbm, sems.at[STEPS]))
@@ -333,77 +358,104 @@
     return lax.ppermute(x, "seq", [(i, (i + by) % devices) for i in range(devices)])
 
 
-def chip_order(way, mine_ref, got_ref):
+def in_order(way, keep_ref, got_ref, body):
     near = odd_core() == (0 if way == 1 else 1)
-    near = near.astype(F32) > 0.5
-    mine, got = mine_ref[...], got_ref[...]
-    return near, jnp.where(near, mine, got), jnp.where(near, got, mine)
-
-
-def compose_kernel(way, keep_ref, got_ref, packed_ref):
-    rows = keep_ref.shape[0] - PAD
-    _near, first, second = chip_order(way, keep_ref, got_ref)
-    packed_ref[:rows] = second[:rows] + second[rows : rows + 1] * first[:rows]
-    a, b = first[rows:], second[rows:]
-    packed_ref[rows:] = jnp.where(iota(a.shape, 0) == 0, a * b, a + b)
-
-
-def arrive_kernel(way, keep_ref, got_ref, packed_ref, one_ref, two_ref, mine_ref, theirs_ref, line2_ref, line3_ref):
-    rows = mine_ref.shape[0]
-    near, first, _second = chip_order(way, keep_ref, got_ref)
-    state = one_ref[:rows] + one_ref[rows : rows + 1] * two_ref[:rows]
-    inside = first[:rows] + first[rows : rows + 1] * state
-    mine_ref[...] = jnp.where(near, state, inside)
-    theirs_ref[...] = jnp.where(near, inside, state)
-    line = slice(rows + 1, rows + 2)
-    line2_ref[...] = packed_ref[line] + one_ref[line]
-    line3_ref[...] = packed_ref[line] + one_ref[line] + two_ref[line]
-
-
-def loss_kernel(scale, *refs):
-    total = refs[0][...]
-    for ref in refs[1:-1]:
-        total = total + ref[...]
-    refs[-1][...] = jnp.broadcast_to(jnp.sum(total) * scale, (1, 1))
-
-
-def carry(keep, send, devices, way, beside):
-    rows, width = keep.shape[0] - PAD, keep.shape[1]
+    pl.when(near)(lambda: body(keep_ref, got_ref, True))
+    pl.when(jnp.logical_not(near))(lambda: body(got_ref, keep_ref, False))
+
+
+def columns(groups, count):
+    return [(q, range(q, count, groups)) for q in range(groups)]
+
+
+def compose_kernel(way, groups, keep_ref, got_ref, packed_ref, both_ref, line_ref):
+    count = both_ref.shape[0] - 1
+
+    def body(first_ref, second_ref, _near):
+        packed_ref[count] = first_ref[count] * second_ref[count]
+        for q, places in columns(groups, count):
+            decay = second_ref[count, q : q + 1, :]
+            for t in places:
+                both = second_ref[t] + decay * first_ref[t]
+                packed_ref[t] = both
+                both_ref[t] = both
+
+    in_order(way, keep_ref, got_ref, body)
+    line = keep_ref[count + 1] + got_ref[count + 1]
+    packed_ref[count + 1] = line
+    both_ref[count] = line
+    line_ref[...] = line
+
+
+def arrive_kernel(way, groups, near_chips, keep_ref, got_ref, line_ref, one_ref, two_ref, *refs):
+    more_refs, mine_ref, theirs_ref = refs[:-2], refs[-2], refs[-1]
+    count = mine_ref.shape[0] - 1
+
+    def body(first_ref, _second_ref, near):
+        outer_ref, inner_ref = (mine_ref, theirs_ref) if near else (theirs_ref, mine_ref)
+        for q, places in columns(groups, count):
+            far_decay = one_ref[count, q : q + 1, :]
+            decay = first_ref[count, q : q + 1, :]
+            for t in places:
+                state = one_ref[t] + far_decay * two_ref[t]
+                outer_ref[t] = state
+                inner_ref[t] = first_ref[t] + decay * state
+
+    in_order(way, keep_ref, got_ref, body)
+    line = jnp.zeros((8, 128), F32)
+    if near_chips:
+        line = line_ref[...] + one_ref[count + 1] + two_ref[count]
+        line = jnp.where((odd_core() == 0).astype(F32) > 0.5, line, 0.0)
+    for ref in more_refs:
+        line = line + ref[...]
+    mine_ref[count] = line
+    theirs_ref[count] = line
+
+
+def far_squares(line, devices):
+    chips = devices // 2
+    if chips != 8:
+        return [lax.psum(line, "seq") * 0.25], False
+    lines = []
+    for far in range(3, chips, 2):
+        pairs = [(i, (i - 2 * (far + i % 2)) % devices) for i in range(devices) if far + i % 2 < chips]
+        lines.append(lax.ppermute(line, "seq", pairs))
+    return lines, True
+
+
+def carry(keep, send, groups, devices, way, beside):
+    count = keep.shape[0] - 2
     got = swap(send, devices)
-    [packed] = call(functools.partial(compose_kernel, way), [keep, got], [out(rows + PAD, width)])
+    packed, both, line = call(
+        functools.partial(compose_kernel, way, groups),
+        [keep, got],
+        [out(*keep.shape), out(count + 1, 8, 128), out(8, 128)],
+    )
     reach = max(1, devices // 8)
     move = shift if way == 1 else turn
     one = move(packed, 2 * way, devices)
-    two = move(packed, 4 * way, devices)
+    two = move(packed if reach > 2 else both, 4 * way, devices)
+    lines, near_chips = far_squares(line, devices) if way == -1 else ([], False)
     if reach > 2:
-        state = one[:rows] + one[rows : rows + 1] * two[:rows]
-        run = one[rows : rows + 1] * two[rows : rows + 1]
+
+        def join(near, far):
+            decay = near[count, :groups]
+            state = near[:count].reshape(-1, groups, 8, 128) + decay[:, None, :] * far[:count].reshape(-1, groups, 8, 128)
+            return jnp.concatenate([state.reshape(count, 8, 128), (near[count:] * far[count:])], axis=0)
+
+        one = join(one, two)
         span = 2
         while span < reach:
-            more = shift(jnp.concatenate([state, jnp.broadcast_to(run, (PAD, width))], axis=0), 2 * span * way, devices)
-            state = state + run * more[:rows]
-            run = run * more[rows : rows + 1]
+            one = join(one, shift(one, 2 * span * way, devices))
             span *= 2
-        one = jnp.concatenate([state, one[rows:]], axis=0)
-        two = jnp.concatenate([jnp.zeros_like(state), two[rows:]], axis=0)
-    mine, theirs, line2, line3 = call(
-        functools.partial(arrive_kernel, way),
-        [keep, got, packed, one, two],
-        [out(rows, width), out(rows, width), out(1, width), out(1, width)],
+        two = jnp.zeros_like(both)
+    mine, theirs = call(
+        functools.partial(arrive_kernel, way, groups, near_chips),
+        [keep, got, line, one, two, *lines],
+        [out(count + 1, 8, 128), out(count + 1, 8, 128)],
     )
     theirs, beside = lax.optimization_barrier((theirs, beside))
-    return mine, swap(theirs, devices), line2, line3, beside
-
-
-def loss_lines(line2, line3, devices):
-    chips = devices // 2
-    if chips == 8:
-        return [line3, turn(line3, -6, devices), turn(line2, -12, devices)]
-    span = 2
-    while span < chips:
-        line2 = line2 + turn(line2, -2 * span, devices)
-        span *= 2
-    return [line2]
+    return mine, swap(theirs, devices), beside
 
 
 def local(values, b_proj, c_proj, step_sizes, decay_rates, skip_gain, teacher, doc_lengths):
@@ -413,7 +465,8 @@
     devices = lax.axis_size("seq")
     b = b_proj.T
     c = c_proj.T
-    half = out(state + PAD, total // 2)
+    groups = total // 2 // 128
+    half = out(state // 8 * groups + 2, 8, 128)
     thirds = out(3 * heads, length, dtype=BF16)
     narrow = out(state, length, dtype=BF16)
     square = 2 * length * length * total
@@ -462,7 +515,7 @@
         [out(length, total), out(length, length, dtype=BF16)],
         square,
     )
-    state_mine, state_other, _, _, (base, score_t) = carry(keep, send, devices, 1, inner)
+    state_mine, state_other, (base, score_t) = carry(keep, send, groups, devices, 1, inner)
     mm, y, back_keep, back_send = call(
         mismatch_kernel,
         [base, enter3, rows, cm, state_mine, state_other],
@@ -476,18 +529,15 @@
         out_specs=[VMEM, VMEM, HBM],
         scratch=[pltpu.VMEM((length, length), F32), pltpu.VMEM((state, length), F32), dma],
     )
-    adj_mine, adj_other, line2, line3, (g, gb_part, grad_c) = carry(back_keep, back_send, devices, -1, pairs)
-    lines = loss_lines(line2, line3, devices)
-    grad_values, grad_b = call(
-        finish_kernel,
+    adj_mine, adj_other, (g, gb_part, grad_c) = carry(back_keep, back_send, groups, devices, -1, pairs)
+    scale = 1.0 / (devices * length * total)
+    grad_values, grad_b, loss = call(
+        functools.partial(finish_kernel, scale),
         [g, x, sf3, rows, bm, ids, gb_part, adj_mine, adj_other],
-        [out(length, total), out(state, length)],
-        out_specs=[HBM, HBM],
+        [out(length, total), out(state, length), out(1, 1)],
+        out_specs=[HBM, HBM, VMEM],
         scratch=[pltpu.VMEM((length, total), F32), pltpu.VMEM((state, length), F32), dma((STEPS + 1,))],
     )
-    lines, grad_values = lax.optimization_barrier((lines, grad_values))
-    scale = 1.0 / (devices * length * total)
-    [loss] = call(functools.partial(loss_kernel, scale), lines, [out(1, 1)])
     return loss.reshape(1), grad_values, grad_b.T, grad_c.T
 
 

time: 61.2 us -> 54.7 us (0.89)
  waiting for transfers between devices: 13.2 us -> 6.53 us
    ppermute x4 -> x2, waiting for transfers between devices: 8.36 us -> 0.01 us  [turn(): lax.ppermute(x, 'seq', [(i, (i + by) % devices) for i in range(devices)])]
    ppermute x4 -> x2, starting transfers between devices: 14.5 us -> 8.5 us  [turn(): lax.ppermute(x, 'seq', [(i, (i + by) % devices) for i in range(devices)])]
    ppermute x0 -> x3, starting transfers between devices: none -> 5.95 us  [far_squares(): lines.append(lax.ppermute(line, 'seq', pairs))]
    ppermute x4, waiting for transfers between devices: 4.2 us -> 5.65 us  [swap(): return lax.ppermute(x, 'seq', [(i, i ^ 1) for i in range(devices)])]
    ppermute x0 -> x3, waiting for transfers between devices: none -> 0.87 us  [far_squares(): lines.append(lax.ppermute(line, 'seq', pairs))]
    ppermute x2, waiting for transfers between devices: 0.66 us -> 0.01 us  [shift(): lax.ppermute(x, 'seq', [(i, i + by) for i in range(devices) if 0 <= i + b...]
    pallas_call x10 -> x9, Pallas kernels: 20.1 us -> 19.8 us  [call(): pl.pallas_call(kernel, out_shape=outs, in_specs=in_specs or [VMEM] * len(...]
    unnamed x8 -> x12, local copies, waits for them, and re-layouts: 3.27 us -> 3.28 us
  transfers between devices with their start and end apart: 10 -> 11, of which waited for: 6 -> 5; matrix products, arithmetic and copies ran while one was open for 0% -> 0% of each run, Pallas kernels for 16% -> 13%
where the time goes in v4:
time: 54.7 us; the launch traced here: 54.1 us
  starting transfers between devices  23.6 us (43%)
  Pallas kernels  19.8 us (36%)
  waiting for transfers between devices  6.53 us (12%)
  local copies, waits for them, and re-layouts  3.28 us (6%)
  between operations  0.96 us (2%)
    pallas_call x9, Pallas kernels, call(): pl.pallas_call(kernel, out_shape=outs, in_specs=in_specs or [VMEM] * len(...  19.8 us
    ppermute x2, starting transfers between devices, turn(): lax.ppermute(x, 'seq', [(i, (i + by) % devices) for i in range(devices)])  8.5 us
    ppermute x2, starting transfers between devices, shift(): lax.ppermute(x, 'seq', [(i, i + by) for i in range(devices) if 0 <= i + b...  8.3 us
    ppermute x3, starting transfers between devices, far_squares(): lines.append(lax.ppermute(line, 'seq', pairs))  5.95 us
    ppermute x4, waiting for transfers between devices, swap(): return lax.ppermute(x, 'seq', [(i, i ^ 1) for i in range(devices)])  5.65 us
    unnamed x12, local copies, waits for them, and re-layouts  3.28 us
  transfers between devices with their start and end apart: 11, of which 5 were waited for; matrix products, arithmetic and copies ran while one was open for 0% of the time, Pallas kernels for 13%

profile of v4, /device:TPU:0, one launch (start us, length us, event | category | flops | bytes accessed | tf_op | source)
XLA Modules:
  0.0 54.1 jit_solution(5282061970015206687)
XLA Ops:
  0.6 0.0 copy-start
  0.6 5.9 %shard_map.111 = (bf16[512,2048]{1,0:T(8,128)(2,1)S(1)}, f32[66,8,128]{2,1,0:T(8,128)S(1)}, f32[66,8,128]{2,1,0:T(8,128)S(1)}, bf16[96,512]{1,0:T(8,128)(2,1)S(1...) custom-call(s32[16]{0:T(128)} %lengths_hbm.1, ...), custom_call_target="tpu_custom_call" | custom-call | bytes 5341504 | tf_op jit(solution)/shard_map/pallas_call | solution.py:332
  6.6 0.5 collective-permute-start
  7.1 1.2 %collective-permute-done.got_ref = f32[66,8,128]{2,1,0:T(8,128)S(1)} collective-permute-done((f32[66,8,128]{2,1,0:T(8,128)S(1)}, f32[66,8,128]{2,1,0:T(8,128)S(1)}, u32[]{:S(2)}, u32[]{:S(2)}) %collective-permute-start) | collective-permute-done | bytes 270368 | tf_op jit(solution)/shard_map/ppermute | solution.py:348
  8.3 4.8 %collective-permute-start.1 = (f32[66,8,128]{2,1,0:T(8,128)S(1)}, f32[66,8,128]{2,1,0:T(8,128)S(1)}, u32[]{:S(2)}, u32[]{:S(2)}) collective-permute-start(f32[66,8,128]{2,1,0:T(8,128)S(1)} %get-tuple-element.45), channel_id=1, source_target_pairs={{0,2},{1,3},{2,4},{3,5},{4,6},{5,7},{6,8},{7,9},{8,10},{9,11},{10,... | collective-permute-start | bytes 811016 | tf_op jit(solution)/shard_map/ppermute | solution.py:352
  13.2 3.5 %collective-permute-start.2 = (f32[65,8,128]{2,1,0:T(8,128)S(1)}, f32[65,8,128]{2,1,0:T(8,128)S(1)}, u32[]{:S(2)}, u32[]{:S(2)}) collective-permute-start(f32[65,8,128]{2,1,0:T(8,128)S(1)} %get-tuple-element.46), channel_id=1, source_target_pairs={{0,4},{1,5},{2,6},{3,7},{4,8},{5,9},{6,10},{7,11},{8,12},{9,13},{1... | collective-permute-start | bytes 798728 | tf_op jit(solution)/shard_map/ppermute | solution.py:352
  16.6 0.0 copy-done
  16.7 0.0 copy-start.1
  16.7 1.6 %copy-done.1 = bf16[512,2048]{1,0:T(8,128)(2,1)S(1)} copy-done((bf16[512,2048]{1,0:T(8,128)(2,1)S(1)}, bf16[512,2048]{1,0:T(8,128)(2,1)}, u32[]{:S(2)}) %copy-start.1) | copy-done | bytes 2097176
  18.2 0.0 copy-start.2
  18.3 0.8 %copy-done.2 = bf16[512,64]{0,1:T(8,128)(2,1)S(1)} copy-done((bf16[512,64]{0,1:T(8,128)(2,1)S(1)}, bf16[512,64]{0,1:T(8,128)(2,1)}, u32[]{:S(2)}) %copy-start.2) | copy-done | bytes 65560
  19.1 0.0 copy-start.4
  19.1 0.8 %copy-done.4 = bf16[512,64]{0,1:T(8,128)(2,1)S(1)} copy-done((bf16[512,64]{0,1:T(8,128)(2,1)S(1)}, bf16[512,64]{0,1:T(8,128)(2,1)}, u32[]{:S(2)}) %copy-start.4) | copy-done | bytes 65560
  19.9 2.3 %shard_map.114 = (f32[512,2048]{1,0:T(8,128)S(1)}, bf16[512,512]{1,0:T(8,128)(2,1)S(1)}) custom-call(bf16[512,2048]{1,0:T(8,128)(2,1)S(1)} %get-tuple-element.48.x_ref, bf16[512,2048]{1,0:T(8,128)(2,1)S(1)} %copy-done, bf16[512,2048]{1,0:T(8,128)(2,1)S(1)} %copy-done.1, bf16[64,512]{1,0:T(8,128)(2,1)S(1)} %bitcast.9, bf16[64,512]{1,0:T(8,128)(2,1)S(1)} %bitcast.12, ...), custom_call_target="tpu_custom_call" | custom-call | flops 1073741824 | bytes 11321344 | tf_op jit(solution)/shard_map/pallas_call | solution.py:332
  22.3 0.0 copy-start.3
  22.3 0.0 copy-start.5
  22.3 0.0 collective-permute-done.2.two_ref
  22.3 0.0 collective-permute-done.1.one_ref
  22.3 0.1 shard_map.113
  22.4 0.1 collective-permute-start.3
  22.5 1.5 %collective-permute-done.3.other_ref = f32[65,8,128]{2,1,0:T(8,128)S(1)} collective-permute-done((f32[65,8,128]{2,1,0:T(8,128)S(1)}, f32[65,8,128]{2,1,0:T(8,128)S(1)}, u32[]{:S(2)}, u32[]{:S(2)}) %collective-permute-start.3) | collective-permute-done | bytes 266272 | tf_op jit(solution)/shard_map/ppermute | solution.py:348
  24.0 3.0 %shard_map.115 = (f32[512,2048]{1,0:T(8,128)S(1)}, bf16[512,2048]{1,0:T(8,128)(2,1)S(1)}, f32[66,8,128]{2,1,0:T(8,128)S(1)}, f32[66,8,128]{2,1,0:T(8,128)S(1)}) custom-call(f32[512,2048]{1,0:T(8,128)S(1)} %get-tuple-element.54.base_ref, bf16[96,512]{1,0:T(8,128)(2,1)S(1)} %get-tuple-element.49.enter3_ref, f32[8,2048]{1,0:T(8,128)S(1)} %get-tuple-element.50.rows_ref, ...), custom_call_target="tpu_custom_call" | custom-call | bytes 11788288 | tf_op jit(solution)/shard_map/pallas_call | solution.py:332
  27.0 0.2 collective-permute-start.4
  27.2 1.4 %collective-permute-done.4.got_ref = f32[66,8,128]{2,1,0:T(8,128)S(1)} collective-permute-done((f32[66,8,128]{2,1,0:T(8,128)S(1)}, f32[66,8,128]{2,1,0:T(8,128)S(1)}, u32[]{:S(2)}, u32[]{:S(2)}) %collective-permute-start.4) | collective-permute-done | bytes 270368 | tf_op jit(solution)/shard_map/ppermute | solution.py:348
  28.7 8.0 %collective-permute-start.5 = (f32[66,8,128]{2,1,0:T(8,128)S(1)}, f32[66,8,128]{2,1,0:T(8,128)S(1)}, u32[]{:S(2)}, u32[]{:S(2)}) collective-permute-start(f32[66,8,128]{2,1,0:T(8,128)S(1)} %get-tuple-element.61), channel_id=1, source_target_pairs={{0,14},{1,15},{2,0},{3,1},{4,2},{5,3},{6,4},{7,5},{8,6},{9,7},{10,... | collective-permute-start | bytes 811016 | tf_op jit(solution)/shard_map/ppermute | solution.py:358
  36.7 0.4 collective-permute-start.6
  37.2 2.1 %collective-permute-start.9 = (f32[8,128]{1,0:T(8,128)S(1)}, f32[8,128]{1,0:T(8,128)S(1)}, u32[]{:S(2)}, u32[]{:S(2)}) collective-permute-start(f32[8,128]{1,0:T(8,128)S(1)} %get-tuple-element.60.line_ref), channel_id=1, source_target_pairs={{0,2},{2,4},{4,6},{6,8},{8,10},{10,12},{12,14},{14,0},{16,18},{18,... | collective-permute-start | bytes 12296 | tf_op jit(solution)/shard_map/ppermute | solution.py:422
  39.2 0.3 collective-permute-start.8
  39.6 3.6 %collective-permute-start.7 = (f32[8,128]{1,0:T(8,128)S(1)}, f32[8,128]{1,0:T(8,128)S(1)}, u32[]{:S(2)}, u32[]{:S(2)}) collective-permute-start(f32[8,128]{1,0:T(8,128)S(1)} %get-tuple-element.60.line_ref), channel_id=1, source_target_pairs={{0,10},{1,9},{2,12},{3,11},{4,14},{5,13},{6,0},{7,15},{8,2},{9,1},... | collective-permute-start | bytes 12296 | tf_op jit(solution)/shard_map/ppermute | solution.py:422
  43.1 0.0 copy-done.3
  43.1 0.0 copy-done.5
  43.1 4.7 %shard_map.118 = (f32[512,2048]{1,0:T(8,128)S(1)}, f32[64,512]{1,0:T(8,128)S(1)}, f32[64,512]{1,0:T(8,128)}) custom-call(f32[512,2048]{1,0:T(8,128)S(1)} %get-tuple-element.64.mm_ref, bf16[512,2048]{1,0:T(8,128)(2,1)S(1)} %get-tuple-element.65.y_ref, bf16[512,2048]{1,0:T(8,128)(2,1)S(1)} %get-tuple-element.48.x_ref, ...), custom_call_target="tpu_custom_call" | custom-call | flops 2147483648 | bytes 14213120 | tf_op jit(solution)/shard_map/pallas_call | solution.py:332
  47.8 0.0 collective-permute-done.9.refs_2_
  47.8 0.8 %collective-permute-done.8.refs_1_ = f32[8,128]{1,0:T(8,128)S(1)} collective-permute-done((f32[8,128]{1,0:T(8,128)S(1)}, f32[8,128]{1,0:T(8,128)S(1)}, u32[]{:S(2)}, u32[]{:S(2)}) %collective-permute-start.8) | collective-permute-done | bytes 4128 | tf_op jit(solution)/shard_map/ppermute | solution.py:422
  48.6 0.0 collective-permute-done.7.refs_0_
  48.7 0.0 collective-permute-done.6.two_ref
  48.7 0.0 collective-permute-done.5.one_ref
  48.7 0.1 shard_map.117
  48.8 0.1 collective-permute-start.10
  48.8 1.5 %collective-permute-done.10.other_ref = f32[65,8,128]{2,1,0:T(8,128)S(1)} collective-permute-done((f32[65,8,128]{2,1,0:T(8,128)S(1)}, f32[65,8,128]{2,1,0:T(8,128)S(1)}, u32[]{:S(2)}, u32[]{:S(2)}) %collective-permute-start.10) | collective-permute-done | bytes 266272 | tf_op jit(solution)/shard_map/ppermute | solution.py:348
  50.4 3.6 %shard_map.119 = (f32[512,2048]{1,0:T(8,128)}, f32[64,512]{1,0:T(8,128)}, f32[1,1]{1,0:T(1,128)}) custom-call(f32[512,2048]{1,0:T(8,128)S(1)} %get-tuple-element.71.g_ref, bf16[512,2048]{1,0:T(8,128)(2,1)S(1)} %get-tuple-element.48.x_ref, bf16[96,512]{1,0:T(8,128)(2,1)S(1)} %get-tuple-element.67.sf3_ref, f32[8,2048]{1,0:T(8,128)S(1)} %get-tuple-element.50.rows_ref, ...), custom_call_target="tpu_custom_call" | custom-call | bytes 11526148 | tf_op jit(solution)/shard_map/pallas_call | solution.py:332
  (2 shorter events, 0.1 us)
Async XLA Ops:
  0.6 16.0 %copy-start = (bf16[512,2048]{1,0:T(8,128)(2,1)S(1)}, bf16[512,2048]{1,0:T(8,128)(2,1)}, u32[]{:S(2)}) copy-start(bf16[512,2048]{1,0:T(8,128)(2,1)} %v_ref.1) | copy-start | bytes 6291460
  6.6 1.7 %collective-permute-start = (f32[66,8,128]{2,1,0:T(8,128)S(1)}, f32[66,8,128]{2,1,0:T(8,128)S(1)}, u32[]{:S(2)}, u32[]{:S(2)}) collective-permute-start(f32[66,8,128]{2,1,0:T(8,128)S(1)} %get-tuple-element.43), channel_id=1, source_target_pairs={{0,1},{1,0},{2,3},{3,2},{4,5},{5,4},{6,7},{7,6},{8,9},{9,8},{10,11... | collective-permute-start | bytes 811016 | tf_op jit(solution)/shard_map/ppermute | solution.py:348
  8.3 14.0 %collective-permute-start.1 = (f32[66,8,128]{2,1,0:T(8,128)S(1)}, f32[66,8,128]{2,1,0:T(8,128)S(1)}, u32[]{:S(2)}, u32[]{:S(2)}) collective-permute-start(f32[66,8,128]{2,1,0:T(8,128)S(1)} %get-tuple-element.45), channel_id=1, source_target_pairs={{0,2},{1,3},{2,4},{3,5},{4,6},{5,7},{6,8},{7,9},{8,10},{9,11},{10,... | collective-permute-start | bytes 811016 | tf_op jit(solution)/shard_map/ppermute | solution.py:352
  13.2 9.2 %collective-permute-start.2 = (f32[65,8,128]{2,1,0:T(8,128)S(1)}, f32[65,8,128]{2,1,0:T(8,128)S(1)}, u32[]{:S(2)}, u32[]{:S(2)}) collective-permute-start(f32[65,8,128]{2,1,0:T(8,128)S(1)} %get-tuple-element.46), channel_id=1, source_target_pairs={{0,4},{1,5},{2,6},{3,7},{4,8},{5,9},{6,10},{7,11},{8,12},{9,13},{1... | collective-permute-start | bytes 798728 | tf_op jit(solution)/shard_map/ppermute | solution.py:352
  16.7 1.6 %copy-start.1 = (bf16[512,2048]{1,0:T(8,128)(2,1)S(1)}, bf16[512,2048]{1,0:T(8,128)(2,1)}, u32[]{:S(2)}) copy-start(bf16[512,2048]{1,0:T(8,128)(2,1)} %teach_ref.1) | copy-start | bytes 6291460
  18.2 0.8 %copy-start.2 = (bf16[512,64]{0,1:T(8,128)(2,1)S(1)}, bf16[512,64]{0,1:T(8,128)(2,1)}, u32[]{:S(2)}) copy-start(bf16[512,64]{0,1:T(8,128)(2,1)} %param.9) | copy-start | bytes 196612
  19.1 0.8 %copy-start.4 = (bf16[512,64]{0,1:T(8,128)(2,1)S(1)}, bf16[512,64]{0,1:T(8,128)(2,1)}, u32[]{:S(2)}) copy-start(bf16[512,64]{0,1:T(8,128)(2,1)} %param.10) | copy-start | bytes 196612
  22.3 20.8 %copy-start.3 = (bf16[512,64]{0,1:T(8,128)(2,1)S(1)}, bf16[512,64]{0,1:T(8,128)(2,1)}, u32[]{:S(2)}) copy-start(bf16[512,64]{0,1:T(8,128)(2,1)} %param.9) | copy-start | bytes 196612
  22.3 20.8 %copy-start.5 = (bf16[512,64]{0,1:T(8,128)(2,1)S(1)}, bf16[512,64]{0,1:T(8,128)(2,1)}, u32[]{:S(2)}) copy-start(bf16[512,64]{0,1:T(8,128)(2,1)} %param.10) | copy-start | bytes 196612
  22.4 1.6 %collective-permute-start.3 = (f32[65,8,128]{2,1,0:T(8,128)S(1)}, f32[65,8,128]{2,1,0:T(8,128)S(1)}, u32[]{:S(2)}, u32[]{:S(2)}) collective-permute-start(f32[65,8,128]{2,1,0:T(8,128)S(1)} %get-tuple-element.57), channel_id=1, source_target_pairs={{0,1},{1,0},{2,3},{3,2},{4,5},{5,4},{6,7},{7,6},{8,9},{9,8},{10,11... | collective-permute-start | bytes 798728 | tf_op jit(solution)/shard_map/ppermute | solution.py:348
  27.0 1.6 %collective-permute-start.4 = (f32[66,8,128]{2,1,0:T(8,128)S(1)}, f32[66,8,128]{2,1,0:T(8,128)S(1)}, u32[]{:S(2)}, u32[]{:S(2)}) collective-permute-start(f32[66,8,128]{2,1,0:T(8,128)S(1)} %get-tuple-element.59), channel_id=1, source_target_pairs={{0,1},{1,0},{2,3},{3,2},{4,5},{5,4},{6,7},{7,6},{8,9},{9,8},{10,11... | collective-permute-start | bytes 811016 | tf_op jit(solution)/shard_map/ppermute | solution.py:348
  28.7 20.0 %collective-permute-start.5 = (f32[66,8,128]{2,1,0:T(8,128)S(1)}, f32[66,8,128]{2,1,0:T(8,128)S(1)}, u32[]{:S(2)}, u32[]{:S(2)}) collective-permute-start(f32[66,8,128]{2,1,0:T(8,128)S(1)} %get-tuple-element.61), channel_id=1, source_target_pairs={{0,14},{1,15},{2,0},{3,1},{4,2},{5,3},{6,4},{7,5},{8,6},{9,7},{10,... | collective-permute-start | bytes 811016 | tf_op jit(solution)/shard_map/ppermute | solution.py:358
  36.7 12.0 %collective-permute-start.6 = (f32[65,8,128]{2,1,0:T(8,128)S(1)}, f32[65,8,128]{2,1,0:T(8,128)S(1)}, u32[]{:S(2)}, u32[]{:S(2)}) collective-permute-start(f32[65,8,128]{2,1,0:T(8,128)S(1)} %get-tuple-element.62), channel_id=1, source_target_pairs={{0,12},{1,13},{2,14},{3,15},{4,0},{5,1},{6,2},{7,3},{8,4},{9,5},{1... | collective-permute-start | bytes 798728 | tf_op jit(solution)/shard_map/ppermute | solution.py:358
  37.2 10.6 %collective-permute-start.9 = (f32[8,128]{1,0:T(8,128)S(1)}, f32[8,128]{1,0:T(8,128)S(1)}, u32[]{:S(2)}, u32[]{:S(2)}) collective-permute-start(f32[8,128]{1,0:T(8,128)S(1)} %get-tuple-element.60.line_ref), channel_id=1, source_target_pairs={{0,2},{2,4},{4,6},{6,8},{8,10},{10,12},{12,14},{14,0},{16,18},{18,... | collective-permute-start | bytes 12296 | tf_op jit(solution)/shard_map/ppermute | solution.py:422
  39.2 9.4 %collective-permute-start.8 = (f32[8,128]{1,0:T(8,128)S(1)}, f32[8,128]{1,0:T(8,128)S(1)}, u32[]{:S(2)}, u32[]{:S(2)}) collective-permute-start(f32[8,128]{1,0:T(8,128)S(1)} %get-tuple-element.60.line_ref), channel_id=1, source_target_pairs={{0,6},{1,5},{2,8},{3,7},{4,10},{5,9},{6,12},{7,11},{8,14},{9,13},{... | collective-permute-start | bytes 12296 | tf_op jit(solution)/shard_map/ppermute | solution.py:422
  39.6 9.1 %collective-permute-start.7 = (f32[8,128]{1,0:T(8,128)S(1)}, f32[8,128]{1,0:T(8,128)S(1)}, u32[]{:S(2)}, u32[]{:S(2)}) collective-permute-start(f32[8,128]{1,0:T(8,128)S(1)} %get-tuple-element.60.line_ref), channel_id=1, source_target_pairs={{0,10},{1,9},{2,12},{3,11},{4,14},{5,13},{6,0},{7,15},{8,2},{9,1},... | collective-permute-start | bytes 12296 | tf_op jit(solution)/shard_map/ppermute | solution.py:422
  48.8 1.6 %collective-permute-start.10 = (f32[65,8,128]{2,1,0:T(8,128)S(1)}, f32[65,8,128]{2,1,0:T(8,128)S(1)}, u32[]{:S(2)}, u32[]{:S(2)}) collective-permute-start(f32[65,8,128]{2,1,0:T(8,128)S(1)} %get-tuple-element.75), channel_id=1, source_target_pairs={{0,1},{1,0},{2,3},{3,2},{4,5},{5,4},{6,7},{7,6},{8,9},{9,8},{10,11... | collective-permute-start | bytes 798728 | tf_op jit(solution)/shard_map/ppermute | solution.py:348

commit v5 on v4

v5 whole, which is shorter than its diff:
```python
import functools
import jax
import jax.numpy as jnp
from jax import lax
from jax.experimental import pallas as pl
from jax.experimental.pallas import tpu as pltpu
from jax.sharding import PartitionSpec as P

F32 = jnp.float32
BF16 = jnp.bfloat16
PAD = 8
STEPS = 4
LIMIT = 24 << 20
HBM = pl.BlockSpec(memory_space=pltpu.MemorySpace.HBM)
VMEM = pl.BlockSpec(memory_space=pltpu.MemorySpace.VMEM)


def dot(a, b):
    return jnp.dot(a, b, preferred_element_type=F32)


def dot_nt(a, b):
    return lax.dot_general(a, b, (((1,), (1,)), ((), ())), preferred_element_type=F32)


def dot_tn(a, b):
    return lax.dot_general(a, b, (((0,), (0,)), ((), ())), preferred_element_type=F32)


def iota(shape, axis):
    return lax.broadcasted_iota(jnp.int32, shape, axis)


def split3(x):
    hi = x.astype(BF16)
    rest = x - hi.astype(F32)
    mid = rest.astype(BF16)
    lo = (rest - mid.astype(F32)).astype(BF16)
    return jnp.concatenate([hi, mid, lo], axis=0)


def split2(x):
    hi = x.astype(BF16)
    lo = (x - hi.astype(F32)).astype(BF16)
    return jnp.concatenate([hi, lo], axis=0)


def twice(x):
    return jnp.concatenate([x, x], axis=0)


def chunk_of(j):
    half = STEPS // 2
    return jnp.where(odd_core() == 0, (j + half) % STEPS, j)


def span_of(j, width):
    return pl.ds(pl.multiple_of(chunk_of(j) * width, width), width)


def expander(heads, head_dim, width, j):
    rows = lax.rem(iota((3 * heads, width), 0), heads)
    cols = iota((3 * heads, width), 1) // head_dim + chunk_of(j) * (width // head_dim)
    return (rows == cols).astype(F32).astype(BF16)


def column(row):
    n = row.shape[1]
    return jnp.sum(jnp.where(iota((n, n), 0) == iota((n, n), 1), row, 0.0), axis=1, keepdims=True)


def tall(row):
    return jnp.broadcast_to(row, (128, row.shape[1])).T


def same_doc(ids_ref):
    ids = ids_ref[0:1, :]
    return tall(ids)[:, 0:1] == ids


def odd_core():
    return lax.rem(lax.axis_index("seq"), 2)


def put_half(a, ref, state, decay):
    rows, width = state.shape
    groups = ref.shape[0] // (rows // 8)
    for q in range(width // 128):
        g = a * (width // 128) + q
        cols = slice(q * 128, (q + 1) * 128)
        for r in range(rows // 8):
            ref[r * groups + g] = state[r * 8 : (r + 1) * 8, cols]
        ref[groups * (rows // 8), g : g + 1, :] = decay[:, cols]


def get_half(a, rows, ref, width):
    groups = ref.shape[0] // (rows // 8)
    inside = range(a * (width // 128), (a + 1) * (width // 128))
    return jnp.concatenate(
        [jnp.concatenate([ref[r * groups + g] for g in inside], axis=1) for r in range(rows // 8)], axis=0
    )


def state_half(first, f3, s3, bm, rows_ref, v_ref, x_ref, message_ref, heads):
    total = v_ref.shape[1]
    width = total // STEPS
    for a in range(STEPS // 2):
        j = first + a
        rel = slice(j * width, (j + 1) * width)
        spread = expander(heads, total // heads, width, j)
        scaled = (dot_tn(s3, spread) * v_ref[:, rel].astype(F32)).astype(BF16).astype(F32)
        x = dot_tn(f3, spread) * scaled
        hi = x.astype(BF16)
        lo = (x - hi.astype(F32)).astype(BF16)
        x_ref[:, a * width : (a + 1) * width] = hi
        state = (dot(bm, hi) + dot(bm, lo)) * rows_ref[1:2, rel]
        put_half(a, message_ref, state, rows_ref[2:3, rel])
    message_ref[message_ref.shape[0] - 1] = jnp.zeros((8, 128), F32)


def prepare_kernel(
    lengths_hbm,
    v_hbm,
    teach_hbm,
    b_hbm,
    c_hbm,
    step_hbm,
    rate_hbm,
    gain_hbm,
    x_ref,
    send_ref,
    enter3_ref,
    sf3_ref,
    f3_ref,
    s3_ref,
    rows_ref,
    bm_ref,
    cm_ref,
    ids_ref,
    v,
    teach,
    b,
    c,
    lengths,
    step,
    rate,
    gain,
    sems,
    v_sems,
    t_sems,
):
    heads, length = step.shape
    total = v.shape[1]
    width = total // STEPS
    small = [(step_hbm, step), (rate_hbm, rate), (gain_hbm, gain), (lengths_hbm, lengths), (b_hbm, b), (c_hbm, c)]
    small = [pltpu.make_async_copy(src, dst, sems.at[i]) for i, (src, dst) in enumerate(small)]
    large = []
    for src, dst, sem in ((v_hbm, v, v_sems), (teach_hbm, teach, t_sems)):
        for j in range(STEPS):
            rel = slice(j * width, (j + 1) * width)
            large.append(pltpu.make_async_copy(src.at[:, span_of(j, width)], dst.at[:, rel], sem.at[j]))
    for copy in small + large:
        copy.start()
    upper = (iota((length, length), 0) <= iota((length, length), 1)).astype(F32).astype(BF16)
    for copy in small:
        copy.wait()
    sums = dot(split3(-(step[...] * column(rate[...]))), upper)
    level = sums[:heads] + sums[heads : 2 * heads] + sums[2 * heads :]
    middle = level[:, length // 2 - 1 : length // 2]
    last = level[:, length - 1 : length]
    place = iota((1, length), 1)
    ids = jnp.zeros((1, length), jnp.int32)
    before = jnp.int32(0)
    final = jnp.int32(0)
    start = -lax.axis_index("seq") * length
    for d in range(lengths.shape[0]):
        ids = ids + (place >= start).astype(jnp.int32)
        before = before + (start <= -1).astype(jnp.int32)
        final = final + (start <= length - 1).astype(jnp.int32)
        start = start + lengths[d]
    first_doc = (ids == before).astype(F32)
    last_doc = (ids == final).astype(F32)
    ids_ref[0:1, :] = ids.astype(F32)
    ids_ref[1:2, :] = first_doc
    ids_ref[2:3, :] = last_doc
    leave = jnp.exp(middle - level)
    enter3_ref[...] = split3(jnp.exp(level - middle))
    f3 = split3(leave)
    s3 = split3(step[...])
    f3_ref[...] = f3
    s3_ref[...] = s3
    sf3_ref[...] = split3(step[...] * leave)
    through = jnp.where(before == final, jnp.exp(last), 0.0)
    pick = iota((heads, 128), 1)
    table = jnp.where(pick == 0, jnp.exp(middle), 0.0)
    table = jnp.where(pick == 1, jnp.exp(last - middle), table)
    table = jnp.where(pick == 2, through, table)
    table = jnp.where(pick == 3, column(gain[...]), table)
    r3 = split3(table)
    for j in range(STEPS):
        spread = expander(heads, total // heads, width, j)
        rows_ref[:, j * width : (j + 1) * width] = dot_tn(r3, spread)[:PAD]
    bm = (b[...].astype(F32) * last_doc).astype(BF16)
    bm_ref[...] = bm
    cm_ref[...] = (c[...].astype(F32) * first_doc).astype(BF16)
    for copy in large[: STEPS // 2]:
        copy.wait()
    state_half(0, f3, s3, bm, rows_ref, v, x_ref, send_ref, heads)
    for copy in large[STEPS // 2 :]:
        copy.wait()


def prepare_own_kernel(f3_ref, s3_ref, bm_ref, rows_ref, v_ref, x_ref, keep_ref):
    state_half(
        STEPS // 2, f3_ref[...], s3_ref[...], bm_ref[...], rows_ref, v_ref, x_ref, keep_ref, f3_ref.shape[0] // 3
    )


def inner_kernel(xf_ref, xo_ref, v_ref, teach_ref, b_ref, c_ref, enter3_ref, rows_ref, ids_ref, base_ref, st_ref):
    length, total = base_ref.shape
    width = total // STEPS
    heads = enter3_ref.shape[0] // 3
    same = same_doc(ids_ref)
    down = iota((length, length), 0)
    along = iota((length, length), 1)
    s = jnp.where(same & (down >= along), dot_tn(c_ref[...], b_ref[...]), 0.0).astype(BF16)
    st_ref[...] = jnp.where(same & (down <= along), dot_tn(b_ref[...], c_ref[...]), 0.0).astype(BF16)
    for j in range(STEPS):
        rel = slice(j * width, (j + 1) * width)
        a = j % (STEPS // 2)
        x_ref = xf_ref if j < STEPS // 2 else xo_ref
        enter = dot_tn(enter3_ref[...], expander(heads, total // heads, width, j))
        base_ref[:, rel] = (
            enter * dot(s, x_ref[:, a * width : (a + 1) * width])
            + rows_ref[3:4, rel] * v_ref[:, rel].astype(F32)
            - teach_ref[:, rel].astype(F32)
        )


def mismatch_kernel(first, base_ref, enter3_ref, rows_ref, cm_ref, state_ref, *refs):
    more, (mm_ref, y_ref, message_ref) = refs[:-3], refs[-3:]
    length, total = base_ref.shape
    width = total // STEPS
    heads = enter3_ref.shape[0] // 3
    cm = cm_ref[...]
    sums = jnp.zeros((8, width), F32)
    for a in range(STEPS // 2):
        j = first + a
        rel = slice(j * width, (j + 1) * width)
        part = slice(a * width, (a + 1) * width)
        enter = dot_tn(enter3_ref[...], expander(heads, total // heads, width, j))
        state = split2(get_half(a, cm.shape[0], state_ref, width) * rows_ref[0:1, rel])
        mm = base_ref[:, rel] + enter * dot_tn(twice(cm), state)
        mm_ref[:, part] = mm
        y = (enter * mm).astype(BF16)
        y_ref[:, part] = y
        sums = sums + jnp.sum((mm * mm).reshape(length // 8, 8, width), axis=0)
        put_half(a, message_ref, dot(cm, y) * rows_ref[0:1, rel], rows_ref[2:3, rel])
    line = sums[:, :128]
    for q in range(1, width // 128):
        line = line + sums[:, q * 128 : (q + 1) * 128]
    for ref in more:
        line = line + ref[ref.shape[0] - 1]
    message_ref[message_ref.shape[0] - 1] = line


def pair_kernel(
    mmf_ref,
    mmo_ref,
    yf_ref,
    yo_ref,
    xf_ref,
    xo_ref,
    st_ref,
    sf3_ref,
    rows_ref,
    b_ref,
    c_ref,
    ids_ref,
    other_ref,
    mine_ref,
    gf_ref,
    go_ref,
    gb_ref,
    gc_hbm,
    pair,
    gc,
    sem,
):
    length, half = mmf_ref.shape
    width = 2 * half // STEPS
    heads = sf3_ref.shape[0] // 3
    n = b_ref.shape[0]
    acc = jnp.zeros((2 * n, length), F32)
    for j in range(STEPS):
        a = j % (STEPS // 2)
        rel = slice(j * width, (j + 1) * width)
        part = slice(a * width, (a + 1) * width)
        far = j < STEPS // 2
        mm_ref, y_ref, state_ref, g_ref = (
            (mmf_ref, yf_ref, other_ref, gf_ref) if far else (mmo_ref, yo_ref, mine_ref, go_ref)
        )
        y = y_ref[:, part]
        sf = dot_tn(sf3_ref[...], expander(heads, 2 * half // heads, width, j))
        g_ref[:, part] = rows_ref[3:4, rel] * mm_ref[:, part] + sf * dot(st_ref[...], y)
        acc = acc + dot_nt(split2(get_half(a, n, state_ref, width) * rows_ref[0:1, rel]), y)
    pair[...] = dot_nt(yf_ref[...], xf_ref[...])
    pair[...] += dot_nt(yo_ref[...], xo_ref[...])
    keep = same_doc(ids_ref) & (iota((length, length), 0) >= iota((length, length), 1))
    masked = jnp.where(keep, pair[...], 0.0)
    hi = masked.astype(BF16)
    lo = (masked - hi.astype(F32)).astype(BF16)
    through = (acc[:n] + acc[n:]) * ids_ref[1:2, :]
    gc[...] = dot_nt(b_ref[...], hi) + dot_nt(b_ref[...], lo) + through
    copy = pltpu.make_async_copy(gc, gc_hbm, sem)
    copy.start()
    gb_ref[...] = dot(c_ref[...], hi) + dot(c_ref[...], lo)
    copy.wait()


def finish_half(first, g_ref, x_ref, sf3_ref, rows_ref, bm_ref, state_ref, gv_hbm, gv, sems):
    half = g_ref.shape[1]
    width = 2 * half // STEPS
    heads = sf3_ref.shape[0] // 3
    bm2 = twice(bm_ref[...])
    copies = []
    acc = jnp.zeros((g_ref.shape[0], bm2.shape[0]), F32)
    for a in range(STEPS // 2):
        j = first + a
        rel = slice(j * width, (j + 1) * width)
        part = slice(a * width, (a + 1) * width)
        sf = dot_tn(sf3_ref[...], expander(heads, 2 * half // heads, width, j))
        adjoint = split2(get_half(a, bm_ref.shape[0], state_ref, width) * rows_ref[1:2, rel])
        gv[:, part] = g_ref[:, part] + sf * dot_tn(bm2, adjoint)
        copies.append(pltpu.make_async_copy(gv.at[:, part], gv_hbm.at[:, span_of(j, width)], sems.at[a]))
        copies[a].start()
        acc = acc + dot_nt(x_ref[:, part], adjoint)
    return acc, copies


def finish_own_kernel(g_ref, x_ref, sf3_ref, rows_ref, bm_ref, mine_ref, gv_hbm, acc_ref, gv, sems):
    acc, copies = finish_half(STEPS // 2, g_ref, x_ref, sf3_ref, rows_ref, bm_ref, mine_ref, gv_hbm, gv, sems)
    acc_ref[...] = acc
    for copy in copies:
        copy.wait()


def finish_kernel(
    scale,
    _gv_in,
    g_ref,
    x_ref,
    sf3_ref,
    rows_ref,
    bm_ref,
    ids_ref,
    gb_part_ref,
    acc_ref,
    mine_ref,
    other_ref,
    gv_hbm,
    gb_hbm,
    loss_hbm,
    gv,
    gb,
    loss,
    sems,
):
    n = bm_ref.shape[0]
    last = mine_ref.shape[0] - 1
    loss[...] = jnp.broadcast_to(jnp.sum(mine_ref[last] + other_ref[last]) * scale, (1, 128))
    half = STEPS // 2
    out_loss = pltpu.make_async_copy(loss, loss_hbm, sems.at[half])
    out_loss.start()
    acc, copies = finish_half(0, g_ref, x_ref, sf3_ref, rows_ref, bm_ref, other_ref, gv_hbm, gv, sems)
    acc = acc + acc_ref[...]
    gb[...] = gb_part_ref[...] + (acc[:, :n] + acc[:, n:]).T * ids_ref[2:3, :]
    out_gb = pltpu.make_async_copy(gb, gb_hbm, sems.at[half + 1])
    out_gb.start()
    for copy in (*copies, out_loss, out_gb):
        copy.wait()


def call(kernel, ins, outs, flops=0, in_specs=None, out_specs=None, scratch=(), aliases=None):
    size = sum(a.size * a.dtype.itemsize for a in ins) + sum(o.size * o.dtype.itemsize for o in outs)
    return pl.pallas_call(
        kernel,
        out_shape=outs,
        in_specs=in_specs or [VMEM] * len(ins),
        out_specs=out_specs or [VMEM] * len(outs),
        scratch_shapes=scratch,
        input_output_aliases=aliases or {},
        compiler_params=pltpu.CompilerParams(vmem_limit_bytes=LIMIT),
        cost_estimate=pl.CostEstimate(flops=flops, bytes_accessed=size, transcendentals=0),
    )(*ins)


def out(*shape, dtype=F32):
    return jax.ShapeDtypeStruct(shape, dtype)


def swap(x, devices):
    return lax.ppermute(x, "seq", [(i, i ^ 1) for i in range(devices)])


def shift(x, by, devices):
    return lax.ppermute(
        x, "seq", [(i, i + by) for i in range(devices) if 0 <= i + by < devices]
    )


def turn(x, by, devices):
    return lax.ppermute(x, "seq", [(i, (i + by) % devices) for i in range(devices)])


def in_order(way, keep_ref, got_ref, body):
    near = odd_core() == (0 if way == 1 else 1)
    pl.when(near)(lambda: body(keep_ref, got_ref, True))
    pl.when(jnp.logical_not(near))(lambda: body(got_ref, keep_ref, False))


def columns(groups, count):
    return [(q, range(q, count, groups)) for q in range(groups)]


def compose_kernel(way, groups, keep_ref, send_ref, got_ref, packed_ref, both_ref, line_ref):
    count = both_ref.shape[0] - 1

    def body(first_ref, second_ref, _near):
        packed_ref[count] = first_ref[count] * second_ref[count]
        for q, places in columns(groups, count):
            decay = second_ref[count, q : q + 1, :]
            for t in places:
                both = second_ref[t] + decay * first_ref[t]
                packed_ref[t] = both
                both_ref[t] = both

    in_order(way, keep_ref, got_ref, body)
    line = send_ref[count + 1] + got_ref[count + 1]
    packed_ref[count + 1] = line
    both_ref[count] = line
    line_ref[...] = line


def arrive_kernel(way, groups, near_chips, keep_ref, got_ref, line_ref, one_ref, two_ref, *refs):
    more_refs, mine_ref, theirs_ref = refs[:-2], refs[-2], refs[-1]
    count = mine_ref.shape[0] - 1

    def body(first_ref, _second_ref, near):
        outer_ref, inner_ref = (mine_ref, theirs_ref) if near else (theirs_ref, mine_ref)
        for q, places in columns(groups, count):
            far_decay = one_ref[count, q : q + 1, :]
            decay = first_ref[count, q : q + 1, :]
            for t in places:
                state = one_ref[t] + far_decay * two_ref[t]
                outer_ref[t] = state
                inner_ref[t] = first_ref[t] + decay * state

    in_order(way, keep_ref, got_ref, body)
    line = jnp.zeros((8, 128), F32)
    if near_chips:
        line = line_ref[...] + one_ref[count + 1] + two_ref[count]
        line = jnp.where((odd_core() == 0).astype(F32) > 0.5, line, 0.0)
    for ref in more_refs:
        line = line + ref[...]
    mine_ref[count] = line
    theirs_ref[count] = line


def far_squares(line, devices):
    chips = devices // 2
    if chips != 8:
        return [lax.psum(line, "seq") * 0.25], False
    lines = []
    for far in range(3, chips, 2):
        pairs = [(i, (i - 2 * (far + i % 2)) % devices) for i in range(devices) if far + i % 2 < chips]
        lines.append(lax.ppermute(line, "seq", pairs))
    return lines, True


def carry(keep, send, groups, devices, way, beside):
    count = keep.shape[0] - 2
    got = swap(send, devices)
    packed, both, line = call(
        functools.partial(compose_kernel, way, groups),
        [keep, send, got],
        [out(*keep.shape), out(count + 1, 8, 128), out(8, 128)],
    )
    reach = max(1, devices // 8)
    move = shift if way == 1 else turn
    one = move(packed, 2 * way, devices)
    two = move(packed if reach > 2 else both, 4 * way, devices)
    lines, near_chips = [], False
    if way == -1:
        lines, near_chips = far_squares(line, devices)
    if reach > 2:

        def join(near, far):
            decay = near[count, :groups]
            state = near[:count].reshape(-1, groups, 8, 128) + decay[:, None, :] * far[:count].reshape(-1, groups, 8, 128)
            return jnp.concatenate([state.reshape(count, 8, 128), (near[count:] * far[count:])], axis=0)

        one = join(one, two)
        span = 2
        while span < reach:
            one = join(one, shift(one, 2 * span * way, devices))
            span *= 2
        two = jnp.zeros_like(both)
    mine, theirs = call(
        functools.partial(arrive_kernel, way, groups, near_chips),
        [keep, got, line, one, two, *lines],
        [out(count + 1, 8, 128), out(count + 1, 8, 128)],
    )
    theirs, beside = lax.optimization_barrier((theirs, beside))
    return mine, swap(theirs, devices), beside


def local(values, b_proj, c_proj, step_sizes, decay_rates, skip_gain, teacher, doc_lengths):
    length, total = values.shape
    heads = step_sizes.shape[1]
    state = b_proj.shape[1]
    devices = lax.axis_size("seq")
    b = b_proj.T
    c = c_proj.T
    groups = total // 2 // 128
    half = out(state // 8 * groups + 2, 8, 128)
    thirds = out(3 * heads, length, dtype=BF16)
    narrow = out(state, length, dtype=BF16)
    square = 2 * length * length * total
    dma = pltpu.SemaphoreType.DMA
    wide = out(length, total, dtype=BF16)
    part = out(length, total // 2)
    part16 = out(length, total // 2, dtype=BF16)
    x_far, send, enter3, sf3, f3, s3, rows, bm, cm, ids, v, teach, b, c = call(
        prepare_kernel,
        [
            pltpu.with_memory_space_constraint(a, pltpu.MemorySpace.HBM)
            for a in (
                doc_lengths,
                values,
                teacher,
                b,
                c,
                step_sizes.T,
                decay_rates.reshape(1, heads),
                skip_gain.reshape(1, heads),
            )
        ],
        [
            part16,
            half,
            thirds,
            thirds,
            thirds,
            thirds,
            out(PAD, total),
            narrow,
            narrow,
            out(PAD, length),
            wide,
            wide,
            narrow,
            narrow,
        ],
        in_specs=[HBM] * 8,
        scratch=[
            pltpu.SMEM(doc_lengths.shape, jnp.int32),
            pltpu.VMEM((heads, length), F32),
            pltpu.VMEM((1, heads), F32),
            pltpu.VMEM((1, heads), F32),
            dma((6,)),
            dma((STEPS,)),
            dma((STEPS,)),
        ],
    )
    x_own, keep = call(prepare_own_kernel, [f3, s3, bm, rows, v], [part16, half])
    inner = call(
        inner_kernel,
        [x_far, x_own, v, teach, b, c, enter3, rows, ids],
        [out(length, total), out(length, length, dtype=BF16)],
        square,
    )
    mine, other, (base, score_t) = carry(keep, send, groups, devices, 1, inner)
    mm_own, y_own, keep = call(
        functools.partial(mismatch_kernel, STEPS // 2), [base, enter3, rows, cm, mine], [part, part16, half]
    )
    mm_far, y_far, send = call(
        functools.partial(mismatch_kernel, 0), [base, enter3, rows, cm, other, keep], [part, part16, half]
    )
    pairs = call(
        pair_kernel,
        [mm_far, mm_own, y_far, y_own, x_far, x_own, score_t, sf3, rows, b, c, ids, other, mine],
        [part, part, out(state, length), out(state, length)],
        2 * square,
        out_specs=[VMEM, VMEM, VMEM, HBM],
        scratch=[pltpu.VMEM((length, length), F32), pltpu.VMEM((state, length), F32), dma],
    )
    mine, other, (g_far, g_own, gb_part, grad_c) = carry(keep, send, groups, devices, -1, pairs)
    grad_values, acc = call(
        finish_own_kernel,
        [g_own, x_own, sf3, rows, bm, mine],
        [out(length, total), out(length, 2 * state)],
        out_specs=[HBM, VMEM],
        scratch=[pltpu.VMEM((length, total // 2), F32), dma((STEPS // 2,))],
    )
    scale = 1.0 / (devices * length * total)
    grad_values, grad_b, loss = call(
        functools.partial(finish_kernel, scale),
        [grad_values, g_far, x_far, sf3, rows, bm, ids, gb_part, acc, mine, other],
        [out(length, total), out(state, length), out(1, 128)],
        in_specs=[HBM] + [VMEM] * 10,
        out_specs=[HBM, HBM, HBM],
        scratch=[
            pltpu.VMEM((length, total // 2), F32),
            pltpu.VMEM((state, length), F32),
            pltpu.VMEM((1, 128), F32),
            dma((STEPS // 2 + 2,)),
        ],
        aliases={0: 0},
    )
    return loss[0, :1], grad_values, grad_b.T, grad_c.T


def solution(mesh):
    rows = P(("groups", "seq"), None)
    in_specs = (rows, rows, rows, rows, P(), P(), rows, P("groups"))
    out_specs = (P("groups"), rows, rows, rows)
    return jax.shard_map(local, mesh=mesh, in_specs=in_specs, out_specs=out_specs, check_vma=False)
```

time: 54.7 us -> 50.1 us (0.916)
  local copies, waits for them, and re-layouts: 3.28 us -> 0 us
    ppermute x4, waiting for transfers between devices: 5.65 us -> 1.62 us  [swap(): return lax.ppermute(x, 'seq', [(i, i ^ 1) for i in range(devices)])]
    ppermute x2, waiting for transfers between devices: 0.01 us -> 3.41 us  [shift(): lax.ppermute(x, 'seq', [(i, i + by) for i in range(devices) if 0 <= i + b...]
    unnamed x12 -> x0, local copies, waits for them, and re-layouts: 3.28 us -> none
    pallas_call x9 -> x12, Pallas kernels: 19.8 us -> 19.3 us  [call(): pl.pallas_call(kernel, out_shape=outs, in_specs=in_specs or [VMEM] * len(...]
  transfers between devices with their start and end apart: 11 -> 11, of which waited for: 5 -> 4; matrix products, arithmetic and copies ran while one was open for 0% -> 0% of each run, Pallas kernels for 13% -> 24%
where the time goes in v5:
time: 50.1 us; the launch traced here: 49.8 us
  starting transfers between devices  23.5 us (47%)
  Pallas kernels  19.3 us (39%)
  waiting for transfers between devices  6.17 us (12%)
  between operations  0.76 us (2%)
    pallas_call x12, Pallas kernels, call(): pl.pallas_call(kernel, out_shape=outs, in_specs=in_specs or [VMEM] * len(...  19.3 us
    ppermute x2, starting transfers between devices, turn(): lax.ppermute(x, 'seq', [(i, (i + by) % devices) for i in range(devices)])  8.55 us
    ppermute x2, starting transfers between devices, shift(): lax.ppermute(x, 'seq', [(i, i + by) for i in range(devices) if 0 <= i + b...  8.12 us
    ppermute x3, starting transfers between devices, far_squares(): lines.append(lax.ppermute(line, 'seq', pairs))  5.9 us
    ppermute x2, waiting for transfers between devices, shift(): lax.ppermute(x, 'seq', [(i, i + by) for i in range(devices) if 0 <= i + b...  3.41 us
    ppermute x4, waiting for transfers between devices, swap(): return lax.ppermute(x, 'seq', [(i, i ^ 1) for i in range(devices)])  1.62 us
    ppermute x3, waiting for transfers between devices, far_squares(): lines.append(lax.ppermute(line, 'seq', pairs))  1.14 us
  transfers between devices with their start and end apart: 11, of which 4 were waited for; matrix products, arithmetic and copies ran while one was open for 0% of the time, Pallas kernels for 24%

profile of v5, /device:TPU:0, one launch (start us, length us, event | category | flops | bytes accessed | tf_op | source)
XLA Modules:
  0.0 49.8 jit_solution(8029388524060588452)
XLA Ops:
  0.6 4.1 %shard_map.111 = (bf16[512,1024]{1,0:T(8,128)(2,1)S(1)}, f32[66,8,128]{2,1,0:T(8,128)S(1)}, bf16[96,512]{1,0:T(8,128)(2,1)S(1)}, bf16[96,512]{1,0:T(8,128)(2,1)S...) custom-call(s32[16]{0:T(128)} %lengths_hbm.1, ...), custom_call_target="tpu_custom_call" | custom-call | bytes 10641728 | tf_op jit(solution)/shard_map/pallas_call | solution.py:386
  4.7 0.5 %collective-permute-start = (f32[66,8,128]{2,1,0:T(8,128)S(1)}, f32[66,8,128]{2,1,0:T(8,128)S(1)}, u32[]{:S(2)}, u32[]{:S(2)}) collective-permute-start(f32[66,8,128]{2,1,0:T(8,128)S(1)} %get-tuple-element.61.send_ref), channel_id=1, source_target_pairs={{0,1},{1,0},{2,3},{3,2},{4,5},{5,4},{6,7},{7,6},{8,9},{9,8},{10,11... | collective-permute-start | bytes 811016 | tf_op jit(solution)/shard_map/ppermute | solution.py:403
  5.3 1.3 %shard_map.112 = (bf16[512,1024]{1,0:T(8,128)(2,1)S(1)}, f32[66,8,128]{2,1,0:T(8,128)S(1)}) custom-call(bf16[96,512]{1,0:T(8,128)(2,1)S(1)} %get-tuple-element.55.f3_ref, bf16[96,512]{1,0:T(8,128)(2,1)S(1)} %get-tuple-element.56.s3_ref, bf16[64,512]{1,0:T(8,128)(2,1)S(1)} %get-tuple-element.57.bm_ref, f32[8,2048]{1,0:T(8,128)S(1)} %get-tuple-element.58.rows_ref, ...), custom_call_target="tpu_custom_call" | custom-call | bytes 3743744 | tf_op jit(solution)/shard_map/pallas_call | solution.py:386
  6.6 0.0 collective-permute-done.got_ref
  6.6 0.1 shard_map.113
  6.7 4.6 %collective-permute-start.1 = (f32[66,8,128]{2,1,0:T(8,128)S(1)}, f32[66,8,128]{2,1,0:T(8,128)S(1)}, u32[]{:S(2)}, u32[]{:S(2)}) collective-permute-start(f32[66,8,128]{2,1,0:T(8,128)S(1)} %get-tuple-element.63), channel_id=1, source_target_pairs={{0,2},{1,3},{2,4},{3,5},{4,6},{5,7},{6,8},{7,9},{8,10},{9,11},{10,... | collective-permute-start | bytes 811016 | tf_op jit(solution)/shard_map/ppermute | solution.py:407
  11.3 3.5 %collective-permute-start.2 = (f32[65,8,128]{2,1,0:T(8,128)S(1)}, f32[65,8,128]{2,1,0:T(8,128)S(1)}, u32[]{:S(2)}, u32[]{:S(2)}) collective-permute-start(f32[65,8,128]{2,1,0:T(8,128)S(1)} %get-tuple-element.64), channel_id=1, source_target_pairs={{0,4},{1,5},{2,6},{3,7},{4,8},{5,9},{6,10},{7,11},{8,12},{9,13},{1... | collective-permute-start | bytes 798728 | tf_op jit(solution)/shard_map/ppermute | solution.py:407
  14.8 2.4 %shard_map.115 = (f32[512,2048]{1,0:T(8,128)S(1)}, bf16[512,512]{1,0:T(8,128)(2,1)S(1)}) custom-call(bf16[512,1024]{1,0:T(8,128)(2,1)S(1)} %get-tuple-element.66.xf_ref.x_ref, bf16[512,1024]{1,0:T(8,128)(2,1)S(1)} %get-tuple-element.67.xo_ref.x_ref, bf16[512,2048]{1,0:T(8,128)(2,1)S(1)} %get-tuple-element.59.v_ref, ...), custom_call_target="tpu_custom_call" | custom-call | flops 1073741824 | bytes 11321344 | tf_op jit(solution)/shard_map/pallas_call | solution.py:386
  17.2 3.4 %collective-permute-done.2.two_ref = f32[65,8,128]{2,1,0:T(8,128)S(1)} collective-permute-done((f32[65,8,128]{2,1,0:T(8,128)S(1)}, f32[65,8,128]{2,1,0:T(8,128)S(1)}, u32[]{:S(2)}, u32[]{:S(2)}) %collective-permute-start.2) | collective-permute-done | bytes 266272 | tf_op jit(solution)/shard_map/ppermute | solution.py:407
  20.6 0.0 collective-permute-done.1.one_ref
  20.6 0.1 shard_map.114
  20.7 0.1 collective-permute-start.3
  20.8 1.2 %shard_map.116 = (f32[512,1024]{1,0:T(8,128)S(1)}, bf16[512,1024]{1,0:T(8,128)(2,1)S(1)}, f32[66,8,128]{2,1,0:T(8,128)S(1)}) custom-call(f32[512,2048]{1,0:T(8,128)S(1)} %get-tuple-element.75.base_ref, bf16[96,512]{1,0:T(8,128)(2,1)S(1)} %get-tuple-element.71.enter3_ref, f32[8,2048]{1,0:T(8,128)S(1)} %get-tuple-element.58.rows_ref, ...), custom_call_target="tpu_custom_call" | custom-call | bytes 8105984 | tf_op jit(solution)/shard_map/pallas_call | solution.py:386
  22.0 0.3 collective-permute-done.3.state_ref.other_ref
  22.3 1.2 %shard_map.117 = (f32[512,1024]{1,0:T(8,128)S(1)}, bf16[512,1024]{1,0:T(8,128)(2,1)S(1)}, f32[66,8,128]{2,1,0:T(8,128)S(1)}) custom-call(f32[512,2048]{1,0:T(8,128)S(1)} %get-tuple-element.75.base_ref, bf16[96,512]{1,0:T(8,128)(2,1)S(1)} %get-tuple-element.71.enter3_ref, f32[8,2048]{1,0:T(8,128)S(1)} %get-tuple-element.58.rows_ref, ...), custom_call_target="tpu_custom_call" | custom-call | bytes 8376320 | tf_op jit(solution)/shard_map/pallas_call | solution.py:386
  23.5 0.3 collective-permute-start.4
  23.8 1.3 %collective-permute-done.4.got_ref = f32[66,8,128]{2,1,0:T(8,128)S(1)} collective-permute-done((f32[66,8,128]{2,1,0:T(8,128)S(1)}, f32[66,8,128]{2,1,0:T(8,128)S(1)}, u32[]{:S(2)}, u32[]{:S(2)}) %collective-permute-start.4) | collective-permute-done | bytes 270368 | tf_op jit(solution)/shard_map/ppermute | solution.py:403
  25.2 0.1 shard_map.118
  25.2 8.1 %collective-permute-start.5 = (f32[66,8,128]{2,1,0:T(8,128)S(1)}, f32[66,8,128]{2,1,0:T(8,128)S(1)}, u32[]{:S(2)}, u32[]{:S(2)}) collective-permute-start(f32[66,8,128]{2,1,0:T(8,128)S(1)} %get-tuple-element.82), channel_id=1, source_target_pairs={{0,14},{1,15},{2,0},{3,1},{4,2},{5,3},{6,4},{7,5},{8,6},{9,7},{10,... | collective-permute-start | bytes 811016 | tf_op jit(solution)/shard_map/ppermute | solution.py:413
  33.3 0.4 collective-permute-start.6
  33.8 0.0 collective-permute-start.7
  33.8 2.9 %collective-permute-start.8 = (f32[8,128]{1,0:T(8,128)S(1)}, f32[8,128]{1,0:T(8,128)S(1)}, u32[]{:S(2)}, u32[]{:S(2)}) collective-permute-start(f32[8,128]{1,0:T(8,128)S(1)} %get-tuple-element.81.line_ref), channel_id=1, source_target_pairs={{0,6},{1,5},{2,8},{3,7},{4,10},{5,9},{6,12},{7,11},{8,14},{9,13},{... | collective-permute-start | bytes 12296 | tf_op jit(solution)/shard_map/ppermute | solution.py:477
  36.7 3.0 %collective-permute-start.9 = (f32[8,128]{1,0:T(8,128)S(1)}, f32[8,128]{1,0:T(8,128)S(1)}, u32[]{:S(2)}, u32[]{:S(2)}) collective-permute-start(f32[8,128]{1,0:T(8,128)S(1)} %get-tuple-element.81.line_ref), channel_id=1, source_target_pairs={{0,2},{2,4},{4,6},{6,8},{8,10},{10,12},{12,14},{14,0},{16,18},{18,... | collective-permute-start | bytes 12296 | tf_op jit(solution)/shard_map/ppermute | solution.py:477
  39.7 4.6 %shard_map.120 = (f32[512,1024]{1,0:T(8,128)S(1)}, f32[512,1024]{1,0:T(8,128)S(1)}, f32[64,512]{1,0:T(8,128)S(1)}, f32[64,512]{1,0:T(8,128)}) custom-call(f32[512,1024]{1,0:T(8,128)S(1)} %get-tuple-element.85.mmf_ref, f32[512,1024]{1,0:T(8,128)S(1)} %get-tuple-element.86.mmo_ref, bf16[512,1024]{1,0:T(8,128)(2,1)S(1)} %get-tuple-element.87.yf_ref, ...), custom_call_target="tpu_custom_call" | custom-call | flops 2147483648 | bytes 14213120 | tf_op jit(solution)/shard_map/pallas_call | solution.py:386
  44.3 1.1 %collective-permute-done.7.refs_0_ = f32[8,128]{1,0:T(8,128)S(1)} collective-permute-done((f32[8,128]{1,0:T(8,128)S(1)}, f32[8,128]{1,0:T(8,128)S(1)}, u32[]{:S(2)}, u32[]{:S(2)}) %collective-permute-start.7) | collective-permute-done | bytes 4128 | tf_op jit(solution)/shard_map/ppermute | solution.py:477
  45.4 0.0 collective-permute-done.8.refs_1_
  45.4 0.0 collective-permute-done.9.refs_2_
  45.4 0.0 collective-permute-done.6.two_ref
  45.4 0.0 collective-permute-done.5.one_ref
  45.4 0.1 shard_map.119
  45.5 0.1 collective-permute-start.10
  45.6 2.2 %shard_map.121 = (f32[512,2048]{1,0:T(8,128)}, f32[512,128]{1,0:T(8,128)S(1)}) custom-call(f32[512,1024]{1,0:T(8,128)S(1)} %get-tuple-element.95.g_ref, bf16[512,1024]{1,0:T(8,128)(2,1)S(1)} %get-tuple-element.67.xo_ref.x_ref, bf16[96,512]{1,0:T(8,128)(2,1)S(1)} %get-tuple-element.90.sf3_ref, f32[8,2048]{1,0:T(8,128)S(1)} %get-tuple-element.58.rows_ref, ...), custom_call_target="tpu_custom_call" | custom-call | bytes 8097792 | tf_op jit(solution)/shard_map/pallas_call | solution.py:386
  47.8 0.0 collective-permute-done.10.other_ref
  47.8 2.0 %shard_map.122 = (f32[512,2048]{1,0:T(8,128)}, f32[64,512]{1,0:T(8,128)}, f32[1,128]{1,0:T(1,128)}) custom-call(f32[512,2048]{1,0:T(8,128)} %get-tuple-element.97._gv_in, f32[512,1024]{1,0:T(8,128)S(1)} %get-tuple-element.98.g_ref, bf16[512,1024]{1,0:T(8,128)(2,1)S(1)} %get-tuple-element.66.xf_ref.x_ref, ...), custom_call_target="tpu_custom_call", output_to_operand_aliasing={{0}: (0, {})} | custom-call | bytes 12837376 | tf_op jit(solution)/shard_map/pallas_call | solution.py:386
Async XLA Ops:
  4.7 1.9 %collective-permute-start = (f32[66,8,128]{2,1,0:T(8,128)S(1)}, f32[66,8,128]{2,1,0:T(8,128)S(1)}, u32[]{:S(2)}, u32[]{:S(2)}) collective-permute-start(f32[66,8,128]{2,1,0:T(8,128)S(1)} %get-tuple-element.61.send_ref), channel_id=1, source_target_pairs={{0,1},{1,0},{2,3},{3,2},{4,5},{5,4},{6,7},{7,6},{8,9},{9,8},{10,11... | collective-permute-start | bytes 811016 | tf_op jit(solution)/shard_map/ppermute | solution.py:403
  6.7 14.0 %collective-permute-start.1 = (f32[66,8,128]{2,1,0:T(8,128)S(1)}, f32[66,8,128]{2,1,0:T(8,128)S(1)}, u32[]{:S(2)}, u32[]{:S(2)}) collective-permute-start(f32[66,8,128]{2,1,0:T(8,128)S(1)} %get-tuple-element.63), channel_id=1, source_target_pairs={{0,2},{1,3},{2,4},{3,5},{4,6},{5,7},{6,8},{7,9},{8,10},{9,11},{10,... | collective-permute-start | bytes 811016 | tf_op jit(solution)/shard_map/ppermute | solution.py:407
  11.3 9.3 %collective-permute-start.2 = (f32[65,8,128]{2,1,0:T(8,128)S(1)}, f32[65,8,128]{2,1,0:T(8,128)S(1)}, u32[]{:S(2)}, u32[]{:S(2)}) collective-permute-start(f32[65,8,128]{2,1,0:T(8,128)S(1)} %get-tuple-element.64), channel_id=1, source_target_pairs={{0,4},{1,5},{2,6},{3,7},{4,8},{5,9},{6,10},{7,11},{8,12},{9,13},{1... | collective-permute-start | bytes 798728 | tf_op jit(solution)/shard_map/ppermute | solution.py:407
  20.7 1.6 %collective-permute-start.3 = (f32[65,8,128]{2,1,0:T(8,128)S(1)}, f32[65,8,128]{2,1,0:T(8,128)S(1)}, u32[]{:S(2)}, u32[]{:S(2)}) collective-permute-start(f32[65,8,128]{2,1,0:T(8,128)S(1)} %get-tuple-element.79), channel_id=1, source_target_pairs={{0,1},{1,0},{2,3},{3,2},{4,5},{5,4},{6,7},{7,6},{8,9},{9,8},{10,11... | collective-permute-start | bytes 798728 | tf_op jit(solution)/shard_map/ppermute | solution.py:403
  23.5 1.6 %collective-permute-start.4 = (f32[66,8,128]{2,1,0:T(8,128)S(1)}, f32[66,8,128]{2,1,0:T(8,128)S(1)}, u32[]{:S(2)}, u32[]{:S(2)}) collective-permute-start(f32[66,8,128]{2,1,0:T(8,128)S(1)} %get-tuple-element.80.send_ref), channel_id=1, source_target_pairs={{0,1},{1,0},{2,3},{3,2},{4,5},{5,4},{6,7},{7,6},{8,9},{9,8},{10,11... | collective-permute-start | bytes 811016 | tf_op jit(solution)/shard_map/ppermute | solution.py:403
  25.2 20.2 %collective-permute-start.5 = (f32[66,8,128]{2,1,0:T(8,128)S(1)}, f32[66,8,128]{2,1,0:T(8,128)S(1)}, u32[]{:S(2)}, u32[]{:S(2)}) collective-permute-start(f32[66,8,128]{2,1,0:T(8,128)S(1)} %get-tuple-element.82), channel_id=1, source_target_pairs={{0,14},{1,15},{2,0},{3,1},{4,2},{5,3},{6,4},{7,5},{8,6},{9,7},{10,... | collective-permute-start | bytes 811016 | tf_op jit(solution)/shard_map/ppermute | solution.py:413
  33.3 12.1 %collective-permute-start.6 = (f32[65,8,128]{2,1,0:T(8,128)S(1)}, f32[65,8,128]{2,1,0:T(8,128)S(1)}, u32[]{:S(2)}, u32[]{:S(2)}) collective-permute-start(f32[65,8,128]{2,1,0:T(8,128)S(1)} %get-tuple-element.83), channel_id=1, source_target_pairs={{0,12},{1,13},{2,14},{3,15},{4,0},{5,1},{6,2},{7,3},{8,4},{9,5},{1... | collective-permute-start | bytes 798728 | tf_op jit(solution)/shard_map/ppermute | solution.py:413
  33.8 11.6 %collective-permute-start.7 = (f32[8,128]{1,0:T(8,128)S(1)}, f32[8,128]{1,0:T(8,128)S(1)}, u32[]{:S(2)}, u32[]{:S(2)}) collective-permute-start(f32[8,128]{1,0:T(8,128)S(1)} %get-tuple-element.81.line_ref), channel_id=1, source_target_pairs={{0,10},{1,9},{2,12},{3,11},{4,14},{5,13},{6,0},{7,15},{8,2},{9,1},... | collective-permute-start | bytes 12296 | tf_op jit(solution)/shard_map/ppermute | solution.py:477
  33.8 11.6 %collective-permute-start.8 = (f32[8,128]{1,0:T(8,128)S(1)}, f32[8,128]{1,0:T(8,128)S(1)}, u32[]{:S(2)}, u32[]{:S(2)}) collective-permute-start(f32[8,128]{1,0:T(8,128)S(1)} %get-tuple-element.81.line_ref), channel_id=1, source_target_pairs={{0,6},{1,5},{2,8},{3,7},{4,10},{5,9},{6,12},{7,11},{8,14},{9,13},{... | collective-permute-start | bytes 12296 | tf_op jit(solution)/shard_map/ppermute | solution.py:477
  36.7 8.7 %collective-permute-start.9 = (f32[8,128]{1,0:T(8,128)S(1)}, f32[8,128]{1,0:T(8,128)S(1)}, u32[]{:S(2)}, u32[]{:S(2)}) collective-permute-start(f32[8,128]{1,0:T(8,128)S(1)} %get-tuple-element.81.line_ref), channel_id=1, source_target_pairs={{0,2},{2,4},{4,6},{6,8},{8,10},{10,12},{12,14},{14,0},{16,18},{18,... | collective-permute-start | bytes 12296 | tf_op jit(solution)/shard_map/ppermute | solution.py:477
  45.5 2.3 %collective-permute-start.10 = (f32[65,8,128]{2,1,0:T(8,128)S(1)}, f32[65,8,128]{2,1,0:T(8,128)S(1)}, u32[]{:S(2)}, u32[]{:S(2)}) collective-permute-start(f32[65,8,128]{2,1,0:T(8,128)S(1)} %get-tuple-element.101), channel_id=1, source_target_pairs={{0,1},{1,0},{2,3},{3,2},{4,5},{5,4},{6,7},{7,6},{8,9},{9,8},{10,11... | collective-permute-start | bytes 798728 | tf_op jit(solution)/shard_map/ppermute | solution.py:403

commit v6 on v5

--- a/solution.py
+++ b/solution.py
@@ -216,7 +216,22 @@
     )
 
 
-def inner_kernel(xf_ref, xo_ref, v_ref, teach_ref, b_ref, c_ref, enter3_ref, rows_ref, ids_ref, base_ref, st_ref):
+def inner_kernel(
+    xf_ref,
+    xo_ref,
+    v_ref,
+    teach_ref,
+    b_ref,
+    c_ref,
+    enter3_ref,
+    sf3_ref,
+    rows_ref,
+    ids_ref,
+    base_ref,
+    st_ref,
+    enter_ref,
+    sf_ref,
+):
     length, total = base_ref.shape
     width = total // STEPS
     heads = enter3_ref.shape[0] // 3
@@ -229,7 +244,10 @@
         rel = slice(j * width, (j + 1) * width)
         a = j % (STEPS // 2)
         x_ref = xf_ref if j < STEPS // 2 else xo_ref
-        enter = dot_tn(enter3_ref[...], expander(heads, total // heads, width, j))
+        spread = expander(heads, total // heads, width, j)
+        enter = dot_tn(enter3_ref[...], spread)
+        enter_ref[:, rel] = enter
+        sf_ref[:, rel] = dot_tn(sf3_ref[...], spread)
         base_ref[:, rel] = (
             enter * dot(s, x_ref[:, a * width : (a + 1) * width])
             + rows_ref[3:4, rel] * v_ref[:, rel].astype(F32)
@@ -237,18 +255,17 @@
         )
 
 
-def mismatch_kernel(first, base_ref, enter3_ref, rows_ref, cm_ref, state_ref, *refs):
+def mismatch_kernel(first, base_ref, enter_ref, rows_ref, cm_ref, state_ref, *refs):
     more, (mm_ref, y_ref, message_ref) = refs[:-3], refs[-3:]
     length, total = base_ref.shape
     width = total // STEPS
-    heads = enter3_ref.shape[0] // 3
     cm = cm_ref[...]
     sums = jnp.zeros((8, width), F32)
     for a in range(STEPS // 2):
         j = first + a
         rel = slice(j * width, (j + 1) * width)
         part = slice(a * width, (a + 1) * width)
-        enter = dot_tn(enter3_ref[...], expander(heads, total // heads, width, j))
+        enter = enter_ref[:, rel]
         state = split2(get_half(a, cm.shape[0], state_ref, width) * rows_ref[0:1, rel])
         mm = base_ref[:, rel] + enter * dot_tn(twice(cm), state)
         mm_ref[:, part] = mm
@@ -272,7 +289,7 @@
     xf_ref,
     xo_ref,
     st_ref,
-    sf3_ref,
+    sf_ref,
     rows_ref,
     b_ref,
     c_ref,
@@ -289,7 +306,6 @@
 ):
     length, half = mmf_ref.shape
     width = 2 * half // STEPS
-    heads = sf3_ref.shape[0] // 3
     n = b_ref.shape[0]
     acc = jnp.zeros((2 * n, length), F32)
     for j in range(STEPS):
@@ -301,8 +317,7 @@
             (mmf_ref, yf_ref, other_ref, gf_ref) if far else (mmo_ref, yo_ref, mine_ref, go_ref)
         )
         y = y_ref[:, part]
-        sf = dot_tn(sf3_ref[...], expander(heads, 2 * half // heads, width, j))
-        g_ref[:, part] = rows_ref[3:4, rel] * mm_ref[:, part] + sf * dot(st_ref[...], y)
+        g_ref[:, part] = rows_ref[3:4, rel] * mm_ref[:, part] + sf_ref[:, rel] * dot(st_ref[...], y)
         acc = acc + dot_nt(split2(get_half(a, n, state_ref, width) * rows_ref[0:1, rel]), y)
     pair[...] = dot_nt(yf_ref[...], xf_ref[...])
     pair[...] += dot_nt(yo_ref[...], xo_ref[...])
@@ -318,10 +333,9 @@
     copy.wait()
 
 
-def finish_half(first, g_ref, x_ref, sf3_ref, rows_ref, bm_ref, state_ref, gv_hbm, gv, sems):
+def finish_half(first, g_ref, x_ref, sf_ref, rows_ref, bm_ref, state_ref, gv_hbm, gv, sems):
     half = g_ref.shape[1]
     width = 2 * half // STEPS
-    heads = sf3_ref.shape[0] // 3
     bm2 = twice(bm_ref[...])
     copies = []
     acc = jnp.zeros((g_ref.shape[0], bm2.shape[0]), F32)
@@ -329,17 +343,16 @@
         j = first + a
         rel = slice(j * width, (j + 1) * width)
         part = slice(a * width, (a + 1) * width)
-        sf = dot_tn(sf3_ref[...], expander(heads, 2 * half // heads, width, j))
         adjoint = split2(get_half(a, bm_ref.shape[0], state_ref, width) * rows_ref[1:2, rel])
-        gv[:, part] = g_ref[:, part] + sf * dot_tn(bm2, adjoint)
+        gv[:, part] = g_ref[:, part] + sf_ref[:, rel] * dot_tn(bm2, adjoint)
         copies.append(pltpu.make_async_copy(gv.at[:, part], gv_hbm.at[:, span_of(j, width)], sems.at[a]))
         copies[a].start()
         acc = acc + dot_nt(x_ref[:, part], adjoint)
     return acc, copies
 
 
-def finish_own_kernel(g_ref, x_ref, sf3_ref, rows_ref, bm_ref, mine_ref, gv_hbm, acc_ref, gv, sems):
-    acc, copies = finish_half(STEPS // 2, g_ref, x_ref, sf3_ref, rows_ref, bm_ref, mine_ref, gv_hbm, gv, sems)
+def finish_own_kernel(g_ref, x_ref, sf_ref, rows_ref, bm_ref, mine_ref, gv_hbm, acc_ref, gv, sems):
+    acc, copies = finish_half(STEPS // 2, g_ref, x_ref, sf_ref, rows_ref, bm_ref, mine_ref, gv_hbm, gv, sems)
     acc_ref[...] = acc
     for copy in copies:
         copy.wait()
@@ -350,7 +363,7 @@
     _gv_in,
     g_ref,
     x_ref,
-    sf3_ref,
+    sf_ref,
     rows_ref,
     bm_ref,
     ids_ref,
@@ -372,7 +385,7 @@
     half = STEPS // 2
     out_loss = pltpu.make_async_copy(loss, loss_hbm, sems.at[half])
     out_loss.start()
-    acc, copies = finish_half(0, g_ref, x_ref, sf3_ref, rows_ref, bm_ref, other_ref, gv_hbm, gv, sems)
+    acc, copies = finish_half(0, g_ref, x_ref, sf_ref, rows_ref, bm_ref, other_ref, gv_hbm, gv, sems)
     acc = acc + acc_ref[...]
     gb[...] = gb_part_ref[...] + (acc[:, :n] + acc[:, n:]).T * ids_ref[2:3, :]
     out_gb = pltpu.make_async_copy(gb, gb_hbm, sems.at[half + 1])
@@ -576,20 +589,20 @@
     x_own, keep = call(prepare_own_kernel, [f3, s3, bm, rows, v], [part16, half])
     inner = call(
         inner_kernel,
-        [x_far, x_own, v, teach, b, c, enter3, rows, ids],
-        [out(length, total), out(length, length, dtype=BF16)],
+        [x_far, x_own, v, teach, b, c, enter3, sf3, rows, ids],
+        [out(length, total), out(length, length, dtype=BF16), out(length, total), out(length, total)],
         square,
     )
-    mine, other, (base, score_t) = carry(keep, send, groups, devices, 1, inner)
+    mine, other, (base, score_t, enter, sf) = carry(keep, send, groups, devices, 1, inner)
     mm_own, y_own, keep = call(
-        functools.partial(mismatch_kernel, STEPS // 2), [base, enter3, rows, cm, mine], [part, part16, half]
+        functools.partial(mismatch_kernel, STEPS // 2), [base, enter, rows, cm, mine], [part, part16, half]
     )
     mm_far, y_far, send = call(
-        functools.partial(mismatch_kernel, 0), [base, enter3, rows, cm, other, keep], [part, part16, half]
+        functools.partial(mismatch_kernel, 0), [base, enter, rows, cm, other, keep], [part, part16, half]
     )
     pairs = call(
         pair_kernel,
-        [mm_far, mm_own, y_far, y_own, x_far, x_own, score_t, sf3, rows, b, c, ids, other, mine],
+        [mm_far, mm_own, y_far, y_own, x_far, x_own, score_t, sf, rows, b, c, ids, other, mine],
         [part, part, out(state, length), out(state, length)],
         2 * square,
         out_specs=[VMEM, VMEM, VMEM, HBM],
@@ -598,7 +611,7 @@
     mine, other, (g_far, g_own, gb_part, grad_c) = carry(keep, send, groups, devices, -1, pairs)
     grad_values, acc = call(
         finish_own_kernel,
-        [g_own, x_own, sf3, rows, bm, mine],
+        [g_own, x_own, sf, rows, bm, mine],
         [out(length, total), out(length, 2 * state)],
         out_specs=[HBM, VMEM],
         scratch=[pltpu.VMEM((length, total // 2), F32), dma((STEPS // 2,))],
@@ -606,7 +619,7 @@
     scale = 1.0 / (devices * length * total)
     grad_values, grad_b, loss = call(
         functools.partial(finish_kernel, scale),
-        [grad_values, g_far, x_far, sf3, rows, bm, ids, gb_part, acc, mine, other],
+        [grad_values, g_far, x_far, sf, rows, bm, ids, gb_part, acc, mine, other],
         [out(length, total), out(state, length), out(1, 128)],
         in_specs=[HBM] + [VMEM] * 10,
         out_specs=[HBM, HBM, HBM],

time: 50.1 us -> 49.2 us (0.982)
  Pallas kernels: 19.3 us -> 18.6 us
    pallas_call x12, Pallas kernels: 19.3 us -> 18.6 us  [call(): pl.pallas_call(kernel, out_shape=outs, in_specs=in_specs or [VMEM] * len(...]
    ppermute x2, waiting for transfers between devices: 3.41 us -> 2.8 us  [shift(): lax.ppermute(x, 'seq', [(i, i + by) for i in range(devices) if 0 <= i + b...]
  transfers between devices with their start and end apart: 11 -> 11, of which waited for: 4 -> 4; matrix products, arithmetic and copies ran while one was open for 0% -> 0% of each run, Pallas kernels for 24% -> 23%
where the time goes in v6:
time: 49.2 us; the launch traced here: 48.8 us
  starting transfers between devices  23.5 us (48%)
  Pallas kernels  18.6 us (38%)
  waiting for transfers between devices  6.04 us (12%)
  between operations  0.76 us (2%)
    pallas_call x12, Pallas kernels, call(): pl.pallas_call(kernel, out_shape=outs, in_specs=in_specs or [VMEM] * len(...  18.6 us
    ppermute x2, starting transfers between devices, turn(): lax.ppermute(x, 'seq', [(i, (i + by) % devices) for i in range(devices)])  8.55 us
    ppermute x2, starting transfers between devices, shift(): lax.ppermute(x, 'seq', [(i, i + by) for i in range(devices) if 0 <= i + b...  8.12 us
    ppermute x3, starting transfers between devices, far_squares(): lines.append(lax.ppermute(line, 'seq', pairs))  5.95 us
    ppermute x2, waiting for transfers between devices, shift(): lax.ppermute(x, 'seq', [(i, i + by) for i in range(devices) if 0 <= i + b...  2.8 us
    ppermute x4, waiting for transfers between devices, swap(): return lax.ppermute(x, 'seq', [(i, i ^ 1) for i in range(devices)])  1.91 us
    ppermute x3, waiting for transfers between devices, far_squares(): lines.append(lax.ppermute(line, 'seq', pairs))  1.32 us
  transfers between devices with their start and end apart: 11, of which 4 were waited for; matrix products, arithmetic and copies ran while one was open for 0% of the time, Pallas kernels for 23%

profile of v6, /device:TPU:0, one launch (start us, length us, event | category | flops | bytes accessed | tf_op | source)
XLA Modules:
  0.0 48.8 jit_solution(2671135873183243332)
XLA Ops:
  0.6 4.1 %shard_map.111 = (bf16[512,1024]{1,0:T(8,128)(2,1)S(1)}, f32[66,8,128]{2,1,0:T(8,128)S(1)}, bf16[96,512]{1,0:T(8,128)(2,1)S(1)}, bf16[96,512]{1,0:T(8,128)(2,1)S...) custom-call(s32[16]{0:T(128)} %lengths_hbm.1, ...), custom_call_target="tpu_custom_call" | custom-call | bytes 10641728 | tf_op jit(solution)/shard_map/pallas_call | solution.py:399
  4.7 0.5 %collective-permute-start = (f32[66,8,128]{2,1,0:T(8,128)S(1)}, f32[66,8,128]{2,1,0:T(8,128)S(1)}, u32[]{:S(2)}, u32[]{:S(2)}) collective-permute-start(f32[66,8,128]{2,1,0:T(8,128)S(1)} %get-tuple-element.65.send_ref), channel_id=1, source_target_pairs={{0,1},{1,0},{2,3},{3,2},{4,5},{5,4},{6,7},{7,6},{8,9},{9,8},{10,11... | collective-permute-start | bytes 811016 | tf_op jit(solution)/shard_map/ppermute | solution.py:416
  5.3 1.3 %shard_map.112 = (bf16[512,1024]{1,0:T(8,128)(2,1)S(1)}, f32[66,8,128]{2,1,0:T(8,128)S(1)}) custom-call(bf16[96,512]{1,0:T(8,128)(2,1)S(1)} %get-tuple-element.59.f3_ref, bf16[96,512]{1,0:T(8,128)(2,1)S(1)} %get-tuple-element.60.s3_ref, bf16[64,512]{1,0:T(8,128)(2,1)S(1)} %get-tuple-element.61.bm_ref, f32[8,2048]{1,0:T(8,128)S(1)} %get-tuple-element.62.rows_ref, ...), custom_call_target="tpu_custom_call" | custom-call | bytes 3743744 | tf_op jit(solution)/shard_map/pallas_call | solution.py:399
  6.6 0.0 collective-permute-done.got_ref
  6.6 0.1 shard_map.113
  6.7 4.6 %collective-permute-start.1 = (f32[66,8,128]{2,1,0:T(8,128)S(1)}, f32[66,8,128]{2,1,0:T(8,128)S(1)}, u32[]{:S(2)}, u32[]{:S(2)}) collective-permute-start(f32[66,8,128]{2,1,0:T(8,128)S(1)} %get-tuple-element.67), channel_id=1, source_target_pairs={{0,2},{1,3},{2,4},{3,5},{4,6},{5,7},{6,8},{7,9},{8,10},{9,11},{10,... | collective-permute-start | bytes 811016 | tf_op jit(solution)/shard_map/ppermute | solution.py:420
  11.3 3.5 %collective-permute-start.2 = (f32[65,8,128]{2,1,0:T(8,128)S(1)}, f32[65,8,128]{2,1,0:T(8,128)S(1)}, u32[]{:S(2)}, u32[]{:S(2)}) collective-permute-start(f32[65,8,128]{2,1,0:T(8,128)S(1)} %get-tuple-element.68), channel_id=1, source_target_pairs={{0,4},{1,5},{2,6},{3,7},{4,8},{5,9},{6,10},{7,11},{8,12},{9,13},{1... | collective-permute-start | bytes 798728 | tf_op jit(solution)/shard_map/ppermute | solution.py:420
  14.8 3.0 %shard_map.115 = (f32[512,2048]{1,0:T(8,128)S(1)}, bf16[512,512]{1,0:T(8,128)(2,1)S(1)}, f32[512,2048]{1,0:T(8,128)S(1)}, f32[512,2048]{1,0:T(8,128)S(1)}) custom-call(bf16[512,1024]{1,0:T(8,128)(2,1)S(1)} %get-tuple-element.70.xf_ref.x_ref, bf16[512,1024]{1,0:T(8,128)(2,1)S(1)} %get-tuple-element.71.xo_ref.x_ref, ...), custom_call_target="tpu_custom_call" | custom-call | flops 1073741824 | bytes 19808256 | tf_op jit(solution)/shard_map/pallas_call | solution.py:399
  17.8 2.8 %collective-permute-done.2.two_ref = f32[65,8,128]{2,1,0:T(8,128)S(1)} collective-permute-done((f32[65,8,128]{2,1,0:T(8,128)S(1)}, f32[65,8,128]{2,1,0:T(8,128)S(1)}, u32[]{:S(2)}, u32[]{:S(2)}) %collective-permute-start.2) | collective-permute-done | bytes 266272 | tf_op jit(solution)/shard_map/ppermute | solution.py:420
  20.6 0.0 collective-permute-done.1.one_ref
  20.6 0.1 shard_map.114
  20.7 0.1 collective-permute-start.3
  20.8 1.0 %shard_map.116 = (f32[512,1024]{1,0:T(8,128)S(1)}, bf16[512,1024]{1,0:T(8,128)(2,1)S(1)}, f32[66,8,128]{2,1,0:T(8,128)S(1)}) custom-call(f32[512,2048]{1,0:T(8,128)S(1)} %get-tuple-element.82.base_ref, f32[512,2048]{1,0:T(8,128)S(1)} %get-tuple-element.83.enter_ref, f32[8,2048]{1,0:T(8,128)S(1)} %get-tuple-element.62.rows_ref, ...), custom_call_target="tpu_custom_call" | custom-call | bytes 12201984 | tf_op jit(solution)/shard_map/pallas_call | solution.py:399
  21.8 0.5 %collective-permute-done.3.state_ref.other_ref = f32[65,8,128]{2,1,0:T(8,128)S(1)} collective-permute-done((f32[65,8,128]{2,1,0:T(8,128)S(1)}, f32[65,8,128]{2,1,0:T(8,128)S(1)}, u32[]{:S(2)}, u32[]{:S(2)}) %collective-permute-start.3) | collective-permute-done | bytes 266272 | tf_op jit(solution)/shard_map/ppermute | solution.py:416
  22.3 1.0 %shard_map.117 = (f32[512,1024]{1,0:T(8,128)S(1)}, bf16[512,1024]{1,0:T(8,128)(2,1)S(1)}, f32[66,8,128]{2,1,0:T(8,128)S(1)}) custom-call(f32[512,2048]{1,0:T(8,128)S(1)} %get-tuple-element.82.base_ref, f32[512,2048]{1,0:T(8,128)S(1)} %get-tuple-element.83.enter_ref, f32[8,2048]{1,0:T(8,128)S(1)} %get-tuple-element.62.rows_ref, ...), custom_call_target="tpu_custom_call" | custom-call | bytes 12472320 | tf_op jit(solution)/shard_map/pallas_call | solution.py:399
  23.3 0.2 collective-permute-start.4
  23.5 1.4 %collective-permute-done.4.got_ref = f32[66,8,128]{2,1,0:T(8,128)S(1)} collective-permute-done((f32[66,8,128]{2,1,0:T(8,128)S(1)}, f32[66,8,128]{2,1,0:T(8,128)S(1)}, u32[]{:S(2)}, u32[]{:S(2)}) %collective-permute-start.4) | collective-permute-done | bytes 270368 | tf_op jit(solution)/shard_map/ppermute | solution.py:416
  25.0 8.1 %collective-permute-start.5 = (f32[66,8,128]{2,1,0:T(8,128)S(1)}, f32[66,8,128]{2,1,0:T(8,128)S(1)}, u32[]{:S(2)}, u32[]{:S(2)}) collective-permute-start(f32[66,8,128]{2,1,0:T(8,128)S(1)} %get-tuple-element.90), channel_id=1, source_target_pairs={{0,14},{1,15},{2,0},{3,1},{4,2},{5,3},{6,4},{7,5},{8,6},{9,7},{10,... | collective-permute-start | bytes 811016 | tf_op jit(solution)/shard_map/ppermute | solution.py:426
  33.1 0.4 collective-permute-start.6
  33.5 2.1 %collective-permute-start.9 = (f32[8,128]{1,0:T(8,128)S(1)}, f32[8,128]{1,0:T(8,128)S(1)}, u32[]{:S(2)}, u32[]{:S(2)}) collective-permute-start(f32[8,128]{1,0:T(8,128)S(1)} %get-tuple-element.89.line_ref), channel_id=1, source_target_pairs={{0,2},{2,4},{4,6},{6,8},{8,10},{10,12},{12,14},{14,0},{16,18},{18,... | collective-permute-start | bytes 12296 | tf_op jit(solution)/shard_map/ppermute | solution.py:490
  35.6 0.3 collective-permute-start.8
  35.9 3.6 %collective-permute-start.7 = (f32[8,128]{1,0:T(8,128)S(1)}, f32[8,128]{1,0:T(8,128)S(1)}, u32[]{:S(2)}, u32[]{:S(2)}) collective-permute-start(f32[8,128]{1,0:T(8,128)S(1)} %get-tuple-element.89.line_ref), channel_id=1, source_target_pairs={{0,10},{1,9},{2,12},{3,11},{4,14},{5,13},{6,0},{7,15},{8,2},{9,1},... | collective-permute-start | bytes 12296 | tf_op jit(solution)/shard_map/ppermute | solution.py:490
  39.5 4.2 %shard_map.120 = (f32[512,1024]{1,0:T(8,128)S(1)}, f32[512,1024]{1,0:T(8,128)S(1)}, f32[64,512]{1,0:T(8,128)S(1)}, f32[64,512]{1,0:T(8,128)}) custom-call(f32[512,1024]{1,0:T(8,128)S(1)} %get-tuple-element.93.mmf_ref, f32[512,1024]{1,0:T(8,128)S(1)} %get-tuple-element.94.mmo_ref, bf16[512,1024]{1,0:T(8,128)(2,1)S(1)} %get-tuple-element.95.yf_ref, ...), custom_call_target="tpu_custom_call" | custom-call | flops 2147483648 | bytes 18309120 | tf_op jit(solution)/shard_map/pallas_call | solution.py:399
  43.7 0.0 collective-permute-done.9.refs_2_
  43.7 1.3 %collective-permute-done.8.refs_1_ = f32[8,128]{1,0:T(8,128)S(1)} collective-permute-done((f32[8,128]{1,0:T(8,128)S(1)}, f32[8,128]{1,0:T(8,128)S(1)}, u32[]{:S(2)}, u32[]{:S(2)}) %collective-permute-start.8) | collective-permute-done | bytes 4128 | tf_op jit(solution)/shard_map/ppermute | solution.py:490
  45.0 0.0 collective-permute-done.7.refs_0_
  45.1 0.0 collective-permute-done.6.two_ref
  45.1 0.0 collective-permute-done.5.one_ref
  45.1 0.1 shard_map.119
  45.1 0.1 collective-permute-start.10
  45.2 1.9 %shard_map.121 = (f32[512,2048]{1,0:T(8,128)}, f32[512,128]{1,0:T(8,128)S(1)}) custom-call(f32[512,1024]{1,0:T(8,128)S(1)} %get-tuple-element.103.g_ref, bf16[512,1024]{1,0:T(8,128)(2,1)S(1)} %get-tuple-element.71.xo_ref.x_ref, f32[512,2048]{1,0:T(8,128)S(1)} %get-tuple-element.98.sf_ref, f32[8,2048]{1,0:T(8,128)S(1)} %get-tuple-element.62.rows_ref, ...), custom_call_target="tpu_custom_call" | custom-call | bytes 12193792 | tf_op jit(solution)/shard_map/pallas_call | solution.py:399
  47.1 0.0 collective-permute-done.10.other_ref
  47.1 1.7 %shard_map.122 = (f32[512,2048]{1,0:T(8,128)}, f32[64,512]{1,0:T(8,128)}, f32[1,128]{1,0:T(1,128)}) custom-call(f32[512,2048]{1,0:T(8,128)} %get-tuple-element.105._gv_in, f32[512,1024]{1,0:T(8,128)S(1)} %get-tuple-element.106.g_ref, bf16[512,1024]{1,0:T(8,128)(2,1)S(1)} %get-tuple-element.70.xf_ref.x_ref, ...), custom_call_target="tpu_custom_call", output_to_operand_aliasing={{0}: (0, {})} | custom-call | bytes 16933376 | tf_op jit(solution)/shard_map/pallas_call | solution.py:399
  (1 shorter events, 0.0 us)
Async XLA Ops:
  4.7 1.9 %collective-permute-start = (f32[66,8,128]{2,1,0:T(8,128)S(1)}, f32[66,8,128]{2,1,0:T(8,128)S(1)}, u32[]{:S(2)}, u32[]{:S(2)}) collective-permute-start(f32[66,8,128]{2,1,0:T(8,128)S(1)} %get-tuple-element.65.send_ref), channel_id=1, source_target_pairs={{0,1},{1,0},{2,3},{3,2},{4,5},{5,4},{6,7},{7,6},{8,9},{9,8},{10,11... | collective-permute-start | bytes 811016 | tf_op jit(solution)/shard_map/ppermute | solution.py:416
  6.7 14.0 %collective-permute-start.1 = (f32[66,8,128]{2,1,0:T(8,128)S(1)}, f32[66,8,128]{2,1,0:T(8,128)S(1)}, u32[]{:S(2)}, u32[]{:S(2)}) collective-permute-start(f32[66,8,128]{2,1,0:T(8,128)S(1)} %get-tuple-element.67), channel_id=1, source_target_pairs={{0,2},{1,3},{2,4},{3,5},{4,6},{5,7},{6,8},{7,9},{8,10},{9,11},{10,... | collective-permute-start | bytes 811016 | tf_op jit(solution)/shard_map/ppermute | solution.py:420
  11.3 9.3 %collective-permute-start.2 = (f32[65,8,128]{2,1,0:T(8,128)S(1)}, f32[65,8,128]{2,1,0:T(8,128)S(1)}, u32[]{:S(2)}, u32[]{:S(2)}) collective-permute-start(f32[65,8,128]{2,1,0:T(8,128)S(1)} %get-tuple-element.68), channel_id=1, source_target_pairs={{0,4},{1,5},{2,6},{3,7},{4,8},{5,9},{6,10},{7,11},{8,12},{9,13},{1... | collective-permute-start | bytes 798728 | tf_op jit(solution)/shard_map/ppermute | solution.py:420
  20.7 1.6 %collective-permute-start.3 = (f32[65,8,128]{2,1,0:T(8,128)S(1)}, f32[65,8,128]{2,1,0:T(8,128)S(1)}, u32[]{:S(2)}, u32[]{:S(2)}) collective-permute-start(f32[65,8,128]{2,1,0:T(8,128)S(1)} %get-tuple-element.87), channel_id=1, source_target_pairs={{0,1},{1,0},{2,3},{3,2},{4,5},{5,4},{6,7},{7,6},{8,9},{9,8},{10,11... | collective-permute-start | bytes 798728 | tf_op jit(solution)/shard_map/ppermute | solution.py:416
  23.3 1.6 %collective-permute-start.4 = (f32[66,8,128]{2,1,0:T(8,128)S(1)}, f32[66,8,128]{2,1,0:T(8,128)S(1)}, u32[]{:S(2)}, u32[]{:S(2)}) collective-permute-start(f32[66,8,128]{2,1,0:T(8,128)S(1)} %get-tuple-element.88.send_ref), channel_id=1, source_target_pairs={{0,1},{1,0},{2,3},{3,2},{4,5},{5,4},{6,7},{7,6},{8,9},{9,8},{10,11... | collective-permute-start | bytes 811016 | tf_op jit(solution)/shard_map/ppermute | solution.py:416
  25.0 20.1 %collective-permute-start.5 = (f32[66,8,128]{2,1,0:T(8,128)S(1)}, f32[66,8,128]{2,1,0:T(8,128)S(1)}, u32[]{:S(2)}, u32[]{:S(2)}) collective-permute-start(f32[66,8,128]{2,1,0:T(8,128)S(1)} %get-tuple-element.90), channel_id=1, source_target_pairs={{0,14},{1,15},{2,0},{3,1},{4,2},{5,3},{6,4},{7,5},{8,6},{9,7},{10,... | collective-permute-start | bytes 811016 | tf_op jit(solution)/shard_map/ppermute | solution.py:426
  33.1 12.0 %collective-permute-start.6 = (f32[65,8,128]{2,1,0:T(8,128)S(1)}, f32[65,8,128]{2,1,0:T(8,128)S(1)}, u32[]{:S(2)}, u32[]{:S(2)}) collective-permute-start(f32[65,8,128]{2,1,0:T(8,128)S(1)} %get-tuple-element.91), channel_id=1, source_target_pairs={{0,12},{1,13},{2,14},{3,15},{4,0},{5,1},{6,2},{7,3},{8,4},{9,5},{1... | collective-permute-start | bytes 798728 | tf_op jit(solution)/shard_map/ppermute | solution.py:426
  33.5 10.2 %collective-permute-start.9 = (f32[8,128]{1,0:T(8,128)S(1)}, f32[8,128]{1,0:T(8,128)S(1)}, u32[]{:S(2)}, u32[]{:S(2)}) collective-permute-start(f32[8,128]{1,0:T(8,128)S(1)} %get-tuple-element.89.line_ref), channel_id=1, source_target_pairs={{0,2},{2,4},{4,6},{6,8},{8,10},{10,12},{12,14},{14,0},{16,18},{18,... | collective-permute-start | bytes 12296 | tf_op jit(solution)/shard_map/ppermute | solution.py:490
  35.6 9.4 %collective-permute-start.8 = (f32[8,128]{1,0:T(8,128)S(1)}, f32[8,128]{1,0:T(8,128)S(1)}, u32[]{:S(2)}, u32[]{:S(2)}) collective-permute-start(f32[8,128]{1,0:T(8,128)S(1)} %get-tuple-element.89.line_ref), channel_id=1, source_target_pairs={{0,6},{1,5},{2,8},{3,7},{4,10},{5,9},{6,12},{7,11},{8,14},{9,13},{... | collective-permute-start | bytes 12296 | tf_op jit(solution)/shard_map/ppermute | solution.py:490
  35.9 9.1 %collective-permute-start.7 = (f32[8,128]{1,0:T(8,128)S(1)}, f32[8,128]{1,0:T(8,128)S(1)}, u32[]{:S(2)}, u32[]{:S(2)}) collective-permute-start(f32[8,128]{1,0:T(8,128)S(1)} %get-tuple-element.89.line_ref), channel_id=1, source_target_pairs={{0,10},{1,9},{2,12},{3,11},{4,14},{5,13},{6,0},{7,15},{8,2},{9,1},... | collective-permute-start | bytes 12296 | tf_op jit(solution)/shard_map/ppermute | solution.py:490
  45.1 2.0 %collective-permute-start.10 = (f32[65,8,128]{2,1,0:T(8,128)S(1)}, f32[65,8,128]{2,1,0:T(8,128)S(1)}, u32[]{:S(2)}, u32[]{:S(2)}) collective-permute-start(f32[65,8,128]{2,1,0:T(8,128)S(1)} %get-tuple-element.109), channel_id=1, source_target_pairs={{0,1},{1,0},{2,3},{3,2},{4,5},{5,4},{6,7},{7,6},{8,9},{9,8},{10,11... | collective-permute-start | bytes 798728 | tf_op jit(solution)/shard_map/ppermute | solution.py:416

commit v7 on v6

--- a/solution.py
+++ b/solution.py
@@ -111,9 +111,8 @@
         scaled = (dot_tn(s3, spread) * v_ref[:, rel].astype(F32)).astype(BF16).astype(F32)
         x = dot_tn(f3, spread) * scaled
         hi = x.astype(BF16)
-        lo = (x - hi.astype(F32)).astype(BF16)
         x_ref[:, a * width : (a + 1) * width] = hi
-        state = (dot(bm, hi) + dot(bm, lo)) * rows_ref[1:2, rel]
+        state = dot(bm, hi) * rows_ref[1:2, rel]
         put_half(a, message_ref, state, rows_ref[2:3, rel])
     message_ref[message_ref.shape[0] - 1] = jnp.zeros((8, 128), F32)
 
@@ -227,14 +226,20 @@
     sf3_ref,
     rows_ref,
     ids_ref,
+    bm_ref,
+    cm_ref,
     base_ref,
     st_ref,
     enter_ref,
     sf_ref,
+    bm2_ref,
+    cm2_ref,
 ):
     length, total = base_ref.shape
     width = total // STEPS
     heads = enter3_ref.shape[0] // 3
+    bm2_ref[...] = twice(bm_ref[...].astype(F32)).T.astype(BF16)
+    cm2_ref[...] = twice(cm_ref[...].astype(F32)).T.astype(BF16)
     same = same_doc(ids_ref)
     down = iota((length, length), 0)
     along = iota((length, length), 1)
@@ -255,7 +260,7 @@
         )
 
 
-def mismatch_kernel(first, base_ref, enter_ref, rows_ref, cm_ref, state_ref, *refs):
+def mismatch_kernel(first, base_ref, enter_ref, rows_ref, cm_ref, cm2_ref, state_ref, *refs):
     more, (mm_ref, y_ref, message_ref) = refs[:-3], refs[-3:]
     length, total = base_ref.shape
     width = total // STEPS
@@ -267,7 +272,7 @@
         part = slice(a * width, (a + 1) * width)
         enter = enter_ref[:, rel]
         state = split2(get_half(a, cm.shape[0], state_ref, width) * rows_ref[0:1, rel])
-        mm = base_ref[:, rel] + enter * dot_tn(twice(cm), state)
+        mm = base_ref[:, rel] + enter * dot(cm2_ref[...], state)
         mm_ref[:, part] = mm
         y = (enter * mm).astype(BF16)
         y_ref[:, part] = y
@@ -333,26 +338,26 @@
     copy.wait()
 
 
-def finish_half(first, g_ref, x_ref, sf_ref, rows_ref, bm_ref, state_ref, gv_hbm, gv, sems):
+def finish_half(first, g_ref, x_ref, sf_ref, rows_ref, bm2_ref, state_ref, gv_hbm, gv, sems):
     half = g_ref.shape[1]
     width = 2 * half // STEPS
-    bm2 = twice(bm_ref[...])
+    n = bm2_ref.shape[1] // 2
     copies = []
-    acc = jnp.zeros((g_ref.shape[0], bm2.shape[0]), F32)
+    acc = jnp.zeros(bm2_ref.shape, F32)
     for a in range(STEPS // 2):
         j = first + a
         rel = slice(j * width, (j + 1) * width)
         part = slice(a * width, (a + 1) * width)
-        adjoint = split2(get_half(a, bm_ref.shape[0], state_ref, width) * rows_ref[1:2, rel])
-        gv[:, part] = g_ref[:, part] + sf_ref[:, rel] * dot_tn(bm2, adjoint)
+        adjoint = split2(get_half(a, n, state_ref, width) * rows_ref[1:2, rel])
+        gv[:, part] = g_ref[:, part] + sf_ref[:, rel] * dot(bm2_ref[...], adjoint)
         copies.append(pltpu.make_async_copy(gv.at[:, part], gv_hbm.at[:, span_of(j, width)], sems.at[a]))
         copies[a].start()
         acc = acc + dot_nt(x_ref[:, part], adjoint)
     return acc, copies
 
 
-def finish_own_kernel(g_ref, x_ref, sf_ref, rows_ref, bm_ref, mine_ref, gv_hbm, acc_ref, gv, sems):
-    acc, copies = finish_half(STEPS // 2, g_ref, x_ref, sf_ref, rows_ref, bm_ref, mine_ref, gv_hbm, gv, sems)
+def finish_own_kernel(g_ref, x_ref, sf_ref, rows_ref, bm2_ref, mine_ref, gv_hbm, acc_ref, gv, sems):
+    acc, copies = finish_half(STEPS // 2, g_ref, x_ref, sf_ref, rows_ref, bm2_ref, mine_ref, gv_hbm, gv, sems)
     acc_ref[...] = acc
     for copy in copies:
         copy.wait()
@@ -365,7 +370,7 @@
     x_ref,
     sf_ref,
     rows_ref,
-    bm_ref,
+    bm2_ref,
     ids_ref,
     gb_part_ref,
     acc_ref,
@@ -379,13 +384,13 @@
     loss,
     sems,
 ):
-    n = bm_ref.shape[0]
+    n = bm2_ref.shape[1] // 2
     last = mine_ref.shape[0] - 1
     loss[...] = jnp.broadcast_to(jnp.sum(mine_ref[last] + other_ref[last]) * scale, (1, 128))
     half = STEPS // 2
     out_loss = pltpu.make_async_copy(loss, loss_hbm, sems.at[half])
     out_loss.start()
-    acc, copies = finish_half(0, g_ref, x_ref, sf_ref, rows_ref, bm_ref, other_ref, gv_hbm, gv, sems)
+    acc, copies = finish_half(0, g_ref, x_ref, sf_ref, rows_ref, bm2_ref, other_ref, gv_hbm, gv, sems)
     acc = acc + acc_ref[...]
     gb[...] = gb_part_ref[...] + (acc[:, :n] + acc[:, n:]).T * ids_ref[2:3, :]
     out_gb = pltpu.make_async_copy(gb, gb_hbm, sems.at[half + 1])
@@ -543,6 +548,7 @@
     dma = pltpu.SemaphoreType.DMA
     wide = out(length, total, dtype=BF16)
     part = out(length, total // 2)
+    doubled = out(length, 2 * state, dtype=BF16)
     part16 = out(length, total // 2, dtype=BF16)
     x_far, send, enter3, sf3, f3, s3, rows, bm, cm, ids, v, teach, b, c = call(
         prepare_kernel,
@@ -589,16 +595,23 @@
     x_own, keep = call(prepare_own_kernel, [f3, s3, bm, rows, v], [part16, half])
     inner = call(
         inner_kernel,
-        [x_far, x_own, v, teach, b, c, enter3, sf3, rows, ids],
-        [out(length, total), out(length, length, dtype=BF16), out(length, total), out(length, total)],
+        [x_far, x_own, v, teach, b, c, enter3, sf3, rows, ids, bm, cm],
+        [
+            out(length, total),
+            out(length, length, dtype=BF16),
+            out(length, total),
+            out(length, total),
+            doubled,
+            doubled,
+        ],
         square,
     )
-    mine, other, (base, score_t, enter, sf) = carry(keep, send, groups, devices, 1, inner)
+    mine, other, (base, score_t, enter, sf, bm2, cm2) = carry(keep, send, groups, devices, 1, inner)
     mm_own, y_own, keep = call(
-        functools.partial(mismatch_kernel, STEPS // 2), [base, enter, rows, cm, mine], [part, part16, half]
+        functools.partial(mismatch_kernel, STEPS // 2), [base, enter, rows, cm, cm2, mine], [part, part16, half]
     )
     mm_far, y_far, send = call(
-        functools.partial(mismatch_kernel, 0), [base, enter, rows, cm, other, keep], [part, part16, half]
+        functools.partial(mismatch_kernel, 0), [base, enter, rows, cm, cm2, other, keep], [part, part16, half]
     )
     pairs = call(
         pair_kernel,
@@ -611,7 +624,7 @@
     mine, other, (g_far, g_own, gb_part, grad_c) = carry(keep, send, groups, devices, -1, pairs)
     grad_values, acc = call(
         finish_own_kernel,
-        [g_own, x_own, sf, rows, bm, mine],
+        [g_own, x_own, sf, rows, bm2, mine],
         [out(length, total), out(length, 2 * state)],
         out_specs=[HBM, VMEM],
         scratch=[pltpu.VMEM((length, total // 2), F32), dma((STEPS // 2,))],
@@ -619,7 +632,7 @@
     scale = 1.0 / (devices * length * total)
     grad_values, grad_b, loss = call(
         functools.partial(finish_kernel, scale),
-        [grad_values, g_far, x_far, sf, rows, bm, ids, gb_part, acc, mine, other],
+        [grad_values, g_far, x_far, sf, rows, bm2, ids, gb_part, acc, mine, other],
         [out(length, total), out(state, length), out(1, 128)],
         in_specs=[HBM] + [VMEM] * 10,
         out_specs=[HBM, HBM, HBM],

time: 49.2 us -> 48.5 us (0.986)
  Pallas kernels: 18.6 us -> 17.5 us
    pallas_call x12, Pallas kernels: 18.6 us -> 17.5 us  [call(): pl.pallas_call(kernel, out_shape=outs, in_specs=in_specs or [VMEM] * len(...]
  transfers between devices with their start and end apart: 11 -> 11, of which waited for: 4 -> 5; matrix products, arithmetic and copies ran while one was open for 0% -> 0% of each run, Pallas kernels for 23% -> 23%
where the time goes in v7:
time: 48.5 us; the launch traced here: 48.2 us
  starting transfers between devices  23.7 us (49%)
  Pallas kernels  17.5 us (36%)
  waiting for transfers between devices  6.28 us (13%)
  between operations  0.76 us (2%)
    pallas_call x12, Pallas kernels, call(): pl.pallas_call(kernel, out_shape=outs, in_specs=in_specs or [VMEM] * len(...  17.5 us
    ppermute x2, starting transfers between devices, turn(): lax.ppermute(x, 'seq', [(i, (i + by) % devices) for i in range(devices)])  8.55 us
    ppermute x2, starting transfers between devices, shift(): lax.ppermute(x, 'seq', [(i, i + by) for i in range(devices) if 0 <= i + b...  8.3 us
    ppermute x3, starting transfers between devices, far_squares(): lines.append(lax.ppermute(line, 'seq', pairs))  5.95 us
    ppermute x2, waiting for transfers between devices, shift(): lax.ppermute(x, 'seq', [(i, i + by) for i in range(devices) if 0 <= i + b...  2.74 us
    ppermute x4, waiting for transfers between devices, swap(): return lax.ppermute(x, 'seq', [(i, i ^ 1) for i in range(devices)])  2.13 us
    ppermute x3, waiting for transfers between devices, far_squares(): lines.append(lax.ppermute(line, 'seq', pairs))  1.4 us
  transfers between devices with their start and end apart: 11, of which 5 were waited for; matrix products, arithmetic and copies ran while one was open for 0% of the time, Pallas kernels for 23%

profile of v7, /device:TPU:0, one launch (start us, length us, event | category | flops | bytes accessed | tf_op | source)
XLA Modules:
  0.0 48.2 jit_solution(11546269436388004270)
XLA Ops:
  0.6 3.8 %shard_map.111 = (bf16[512,1024]{1,0:T(8,128)(2,1)S(1)}, f32[66,8,128]{2,1,0:T(8,128)S(1)}, bf16[96,512]{1,0:T(8,128)(2,1)S(1)}, bf16[96,512]{1,0:T(8,128)(2,1)S...) custom-call(s32[16]{0:T(128)} %lengths_hbm.1, ...), custom_call_target="tpu_custom_call" | custom-call | bytes 10641728 | tf_op jit(solution)/shard_map/pallas_call | solution.py:404
  4.5 0.5 %collective-permute-start = (f32[66,8,128]{2,1,0:T(8,128)S(1)}, f32[66,8,128]{2,1,0:T(8,128)S(1)}, u32[]{:S(2)}, u32[]{:S(2)}) collective-permute-start(f32[66,8,128]{2,1,0:T(8,128)S(1)} %get-tuple-element.69.send_ref), channel_id=1, source_target_pairs={{0,1},{1,0},{2,3},{3,2},{4,5},{5,4},{6,7},{7,6},{8,9},{9,8},{10,11... | collective-permute-start | bytes 811016 | tf_op jit(solution)/shard_map/ppermute | solution.py:421
  5.0 1.0 %shard_map.112 = (bf16[512,1024]{1,0:T(8,128)(2,1)S(1)}, f32[66,8,128]{2,1,0:T(8,128)S(1)}) custom-call(bf16[96,512]{1,0:T(8,128)(2,1)S(1)} %get-tuple-element.63.f3_ref, bf16[96,512]{1,0:T(8,128)(2,1)S(1)} %get-tuple-element.64.s3_ref, bf16[64,512]{1,0:T(8,128)(2,1)S(1)} %get-tuple-element.65.bm_ref, f32[8,2048]{1,0:T(8,128)S(1)} %get-tuple-element.66.rows_ref, ...), custom_call_target="tpu_custom_call" | custom-call | bytes 3743744 | tf_op jit(solution)/shard_map/pallas_call | solution.py:404
  6.0 0.1 collective-permute-done.got_ref
  6.2 4.8 %collective-permute-start.1 = (f32[66,8,128]{2,1,0:T(8,128)S(1)}, f32[66,8,128]{2,1,0:T(8,128)S(1)}, u32[]{:S(2)}, u32[]{:S(2)}) collective-permute-start(f32[66,8,128]{2,1,0:T(8,128)S(1)} %get-tuple-element.71), channel_id=1, source_target_pairs={{0,2},{1,3},{2,4},{3,5},{4,6},{5,7},{6,8},{7,9},{8,10},{9,11},{10,... | collective-permute-start | bytes 811016 | tf_op jit(solution)/shard_map/ppermute | solution.py:425
  11.0 3.5 %collective-permute-start.2 = (f32[65,8,128]{2,1,0:T(8,128)S(1)}, f32[65,8,128]{2,1,0:T(8,128)S(1)}, u32[]{:S(2)}, u32[]{:S(2)}) collective-permute-start(f32[65,8,128]{2,1,0:T(8,128)S(1)} %get-tuple-element.72), channel_id=1, source_target_pairs={{0,4},{1,5},{2,6},{3,7},{4,8},{5,9},{6,10},{7,11},{8,12},{9,13},{1... | collective-permute-start | bytes 798728 | tf_op jit(solution)/shard_map/ppermute | solution.py:425
  14.5 2.9 %shard_map.115 = (f32[512,2048]{1,0:T(8,128)S(1)}, bf16[512,512]{1,0:T(8,128)(2,1)S(1)}, f32[512,2048]{1,0:T(8,128)S(1)}, f32[512,2048]{1,0:T(8,128)S(1)}, bf16[...) custom-call(bf16[512,1024]{1,0:T(8,128)(2,1)S(1)} %get-tuple-element.74.xf_ref.x_ref, ...), custom_call_target="tpu_custom_call" | custom-call | flops 1073741824 | bytes 20201472 | tf_op jit(solution)/shard_map/pallas_call | solution.py:404
  17.4 2.7 %collective-permute-done.2.two_ref = f32[65,8,128]{2,1,0:T(8,128)S(1)} collective-permute-done((f32[65,8,128]{2,1,0:T(8,128)S(1)}, f32[65,8,128]{2,1,0:T(8,128)S(1)}, u32[]{:S(2)}, u32[]{:S(2)}) %collective-permute-start.2) | collective-permute-done | bytes 266272 | tf_op jit(solution)/shard_map/ppermute | solution.py:425
  20.1 0.0 collective-permute-done.1.one_ref
  20.1 0.1 shard_map.114
  20.2 0.1 collective-permute-start.3
  20.3 0.9 %shard_map.116 = (f32[512,1024]{1,0:T(8,128)S(1)}, bf16[512,1024]{1,0:T(8,128)(2,1)S(1)}, f32[66,8,128]{2,1,0:T(8,128)S(1)}) custom-call(f32[512,2048]{1,0:T(8,128)S(1)} %get-tuple-element.89.base_ref, f32[512,2048]{1,0:T(8,128)S(1)} %get-tuple-element.90.enter_ref, f32[8,2048]{1,0:T(8,128)S(1)} %get-tuple-element.66.rows_ref, ...), custom_call_target="tpu_custom_call" | custom-call | bytes 12333056 | tf_op jit(solution)/shard_map/pallas_call | solution.py:404
  21.2 0.6 %collective-permute-done.3.state_ref.other_ref = f32[65,8,128]{2,1,0:T(8,128)S(1)} collective-permute-done((f32[65,8,128]{2,1,0:T(8,128)S(1)}, f32[65,8,128]{2,1,0:T(8,128)S(1)}, u32[]{:S(2)}, u32[]{:S(2)}) %collective-permute-start.3) | collective-permute-done | bytes 266272 | tf_op jit(solution)/shard_map/ppermute | solution.py:421
  21.8 0.9 %shard_map.117 = (f32[512,1024]{1,0:T(8,128)S(1)}, bf16[512,1024]{1,0:T(8,128)(2,1)S(1)}, f32[66,8,128]{2,1,0:T(8,128)S(1)}) custom-call(f32[512,2048]{1,0:T(8,128)S(1)} %get-tuple-element.89.base_ref, f32[512,2048]{1,0:T(8,128)S(1)} %get-tuple-element.90.enter_ref, f32[8,2048]{1,0:T(8,128)S(1)} %get-tuple-element.66.rows_ref, ...), custom_call_target="tpu_custom_call" | custom-call | bytes 12603392 | tf_op jit(solution)/shard_map/pallas_call | solution.py:404
  22.8 0.2 collective-permute-start.4
  23.0 1.4 %collective-permute-done.4.got_ref = f32[66,8,128]{2,1,0:T(8,128)S(1)} collective-permute-done((f32[66,8,128]{2,1,0:T(8,128)S(1)}, f32[66,8,128]{2,1,0:T(8,128)S(1)}, u32[]{:S(2)}, u32[]{:S(2)}) %collective-permute-start.4) | collective-permute-done | bytes 270368 | tf_op jit(solution)/shard_map/ppermute | solution.py:421
  24.4 8.1 %collective-permute-start.5 = (f32[66,8,128]{2,1,0:T(8,128)S(1)}, f32[66,8,128]{2,1,0:T(8,128)S(1)}, u32[]{:S(2)}, u32[]{:S(2)}) collective-permute-start(f32[66,8,128]{2,1,0:T(8,128)S(1)} %get-tuple-element.97), channel_id=1, source_target_pairs={{0,14},{1,15},{2,0},{3,1},{4,2},{5,3},{6,4},{7,5},{8,6},{9,7},{10,... | collective-permute-start | bytes 811016 | tf_op jit(solution)/shard_map/ppermute | solution.py:431
  32.5 0.4 collective-permute-start.6
  33.0 2.1 %collective-permute-start.9 = (f32[8,128]{1,0:T(8,128)S(1)}, f32[8,128]{1,0:T(8,128)S(1)}, u32[]{:S(2)}, u32[]{:S(2)}) collective-permute-start(f32[8,128]{1,0:T(8,128)S(1)} %get-tuple-element.96.line_ref), channel_id=1, source_target_pairs={{0,2},{2,4},{4,6},{6,8},{8,10},{10,12},{12,14},{14,0},{16,18},{18,... | collective-permute-start | bytes 12296 | tf_op jit(solution)/shard_map/ppermute | solution.py:495
  35.1 0.3 collective-permute-start.8
  35.4 3.6 %collective-permute-start.7 = (f32[8,128]{1,0:T(8,128)S(1)}, f32[8,128]{1,0:T(8,128)S(1)}, u32[]{:S(2)}, u32[]{:S(2)}) collective-permute-start(f32[8,128]{1,0:T(8,128)S(1)} %get-tuple-element.96.line_ref), channel_id=1, source_target_pairs={{0,10},{1,9},{2,12},{3,11},{4,14},{5,13},{6,0},{7,15},{8,2},{9,1},... | collective-permute-start | bytes 12296 | tf_op jit(solution)/shard_map/ppermute | solution.py:495
  38.9 4.1 %shard_map.120 = (f32[512,1024]{1,0:T(8,128)S(1)}, f32[512,1024]{1,0:T(8,128)S(1)}, f32[64,512]{1,0:T(8,128)S(1)}, f32[64,512]{1,0:T(8,128)}) custom-call(f32[512,1024]{1,0:T(8,128)S(1)} %get-tuple-element.100.mmf_ref, f32[512,1024]{1,0:T(8,128)S(1)} %get-tuple-element.101.mmo_ref, bf16[512,1024]{1,0:T(8,128)(2,1)S(1)} %get-tuple-element.102.yf_ref, ...), custom_call_target="tpu_custom_call" | custom-call | flops 2147483648 | bytes 18309120 | tf_op jit(solution)/shard_map/pallas_call | solution.py:404
  43.1 0.0 collective-permute-done.9.refs_2_
  43.1 1.4 %collective-permute-done.8.refs_1_ = f32[8,128]{1,0:T(8,128)S(1)} collective-permute-done((f32[8,128]{1,0:T(8,128)S(1)}, f32[8,128]{1,0:T(8,128)S(1)}, u32[]{:S(2)}, u32[]{:S(2)}) %collective-permute-start.8) | collective-permute-done | bytes 4128 | tf_op jit(solution)/shard_map/ppermute | solution.py:495
  44.5 0.0 collective-permute-done.7.refs_0_
  44.5 0.0 collective-permute-done.6.two_ref
  44.5 0.0 collective-permute-done.5.one_ref
  44.5 0.1 shard_map.119
  44.6 0.1 collective-permute-start.10
  44.7 1.9 %shard_map.121 = (f32[512,2048]{1,0:T(8,128)}, f32[512,128]{1,0:T(8,128)S(1)}) custom-call(f32[512,1024]{1,0:T(8,128)S(1)} %get-tuple-element.110.g_ref, bf16[512,1024]{1,0:T(8,128)(2,1)S(1)} %get-tuple-element.75.xo_ref.x_ref, f32[512,2048]{1,0:T(8,128)S(1)} %get-tuple-element.105.sf_ref, f32[8,2048]{1,0:T(8,128)S(1)} %get-tuple-element.66.rows_ref, ...), custom_call_target="tpu_custom_call" | custom-call | bytes 12259328 | tf_op jit(solution)/shard_map/pallas_call | solution.py:404
  46.5 0.0 collective-permute-done.10.other_ref
  46.5 1.7 %shard_map.122 = (f32[512,2048]{1,0:T(8,128)}, f32[64,512]{1,0:T(8,128)}, f32[1,128]{1,0:T(1,128)}) custom-call(f32[512,2048]{1,0:T(8,128)} %get-tuple-element.113._gv_in, f32[512,1024]{1,0:T(8,128)S(1)} %get-tuple-element.114.g_ref, bf16[512,1024]{1,0:T(8,128)(2,1)S(1)} %get-tuple-element.74.xf_ref.x_ref, ...), custom_call_target="tpu_custom_call", output_to_operand_aliasing={{0}: (0, {})} | custom-call | bytes 16998912 | tf_op jit(solution)/shard_map/pallas_call | solution.py:404
  (2 shorter events, 0.1 us)
Async XLA Ops:
  4.5 1.7 %collective-permute-start = (f32[66,8,128]{2,1,0:T(8,128)S(1)}, f32[66,8,128]{2,1,0:T(8,128)S(1)}, u32[]{:S(2)}, u32[]{:S(2)}) collective-permute-start(f32[66,8,128]{2,1,0:T(8,128)S(1)} %get-tuple-element.69.send_ref), channel_id=1, source_target_pairs={{0,1},{1,0},{2,3},{3,2},{4,5},{5,4},{6,7},{7,6},{8,9},{9,8},{10,11... | collective-permute-start | bytes 811016 | tf_op jit(solution)/shard_map/ppermute | solution.py:421
  6.2 13.9 %collective-permute-start.1 = (f32[66,8,128]{2,1,0:T(8,128)S(1)}, f32[66,8,128]{2,1,0:T(8,128)S(1)}, u32[]{:S(2)}, u32[]{:S(2)}) collective-permute-start(f32[66,8,128]{2,1,0:T(8,128)S(1)} %get-tuple-element.71), channel_id=1, source_target_pairs={{0,2},{1,3},{2,4},{3,5},{4,6},{5,7},{6,8},{7,9},{8,10},{9,11},{10,... | collective-permute-start | bytes 811016 | tf_op jit(solution)/shard_map/ppermute | solution.py:425
  11.0 9.1 %collective-permute-start.2 = (f32[65,8,128]{2,1,0:T(8,128)S(1)}, f32[65,8,128]{2,1,0:T(8,128)S(1)}, u32[]{:S(2)}, u32[]{:S(2)}) collective-permute-start(f32[65,8,128]{2,1,0:T(8,128)S(1)} %get-tuple-element.72), channel_id=1, source_target_pairs={{0,4},{1,5},{2,6},{3,7},{4,8},{5,9},{6,10},{7,11},{8,12},{9,13},{1... | collective-permute-start | bytes 798728 | tf_op jit(solution)/shard_map/ppermute | solution.py:425
  20.2 1.6 %collective-permute-start.3 = (f32[65,8,128]{2,1,0:T(8,128)S(1)}, f32[65,8,128]{2,1,0:T(8,128)S(1)}, u32[]{:S(2)}, u32[]{:S(2)}) collective-permute-start(f32[65,8,128]{2,1,0:T(8,128)S(1)} %get-tuple-element.94), channel_id=1, source_target_pairs={{0,1},{1,0},{2,3},{3,2},{4,5},{5,4},{6,7},{7,6},{8,9},{9,8},{10,11... | collective-permute-start | bytes 798728 | tf_op jit(solution)/shard_map/ppermute | solution.py:421
  22.8 1.6 %collective-permute-start.4 = (f32[66,8,128]{2,1,0:T(8,128)S(1)}, f32[66,8,128]{2,1,0:T(8,128)S(1)}, u32[]{:S(2)}, u32[]{:S(2)}) collective-permute-start(f32[66,8,128]{2,1,0:T(8,128)S(1)} %get-tuple-element.95.send_ref), channel_id=1, source_target_pairs={{0,1},{1,0},{2,3},{3,2},{4,5},{5,4},{6,7},{7,6},{8,9},{9,8},{10,11... | collective-permute-start | bytes 811016 | tf_op jit(solution)/shard_map/ppermute | solution.py:421
  24.4 20.1 %collective-permute-start.5 = (f32[66,8,128]{2,1,0:T(8,128)S(1)}, f32[66,8,128]{2,1,0:T(8,128)S(1)}, u32[]{:S(2)}, u32[]{:S(2)}) collective-permute-start(f32[66,8,128]{2,1,0:T(8,128)S(1)} %get-tuple-element.97), channel_id=1, source_target_pairs={{0,14},{1,15},{2,0},{3,1},{4,2},{5,3},{6,4},{7,5},{8,6},{9,7},{10,... | collective-permute-start | bytes 811016 | tf_op jit(solution)/shard_map/ppermute | solution.py:431
  32.5 12.0 %collective-permute-start.6 = (f32[65,8,128]{2,1,0:T(8,128)S(1)}, f32[65,8,128]{2,1,0:T(8,128)S(1)}, u32[]{:S(2)}, u32[]{:S(2)}) collective-permute-start(f32[65,8,128]{2,1,0:T(8,128)S(1)} %get-tuple-element.98), channel_id=1, source_target_pairs={{0,12},{1,13},{2,14},{3,15},{4,0},{5,1},{6,2},{7,3},{8,4},{9,5},{1... | collective-permute-start | bytes 798728 | tf_op jit(solution)/shard_map/ppermute | solution.py:431
  33.0 10.1 %collective-permute-start.9 = (f32[8,128]{1,0:T(8,128)S(1)}, f32[8,128]{1,0:T(8,128)S(1)}, u32[]{:S(2)}, u32[]{:S(2)}) collective-permute-start(f32[8,128]{1,0:T(8,128)S(1)} %get-tuple-element.96.line_ref), channel_id=1, source_target_pairs={{0,2},{2,4},{4,6},{6,8},{8,10},{10,12},{12,14},{14,0},{16,18},{18,... | collective-permute-start | bytes 12296 | tf_op jit(solution)/shard_map/ppermute | solution.py:495
  35.1 9.4 %collective-permute-start.8 = (f32[8,128]{1,0:T(8,128)S(1)}, f32[8,128]{1,0:T(8,128)S(1)}, u32[]{:S(2)}, u32[]{:S(2)}) collective-permute-start(f32[8,128]{1,0:T(8,128)S(1)} %get-tuple-element.96.line_ref), channel_id=1, source_target_pairs={{0,6},{1,5},{2,8},{3,7},{4,10},{5,9},{6,12},{7,11},{8,14},{9,13},{... | collective-permute-start | bytes 12296 | tf_op jit(solution)/shard_map/ppermute | solution.py:495
  35.4 9.1 %collective-permute-start.7 = (f32[8,128]{1,0:T(8,128)S(1)}, f32[8,128]{1,0:T(8,128)S(1)}, u32[]{:S(2)}, u32[]{:S(2)}) collective-permute-start(f32[8,128]{1,0:T(8,128)S(1)} %get-tuple-element.96.line_ref), channel_id=1, source_target_pairs={{0,10},{1,9},{2,12},{3,11},{4,14},{5,13},{6,0},{7,15},{8,2},{9,1},... | collective-permute-start | bytes 12296 | tf_op jit(solution)/shard_map/ppermute | solution.py:495
  44.6 1.9 %collective-permute-start.10 = (f32[65,8,128]{2,1,0:T(8,128)S(1)}, f32[65,8,128]{2,1,0:T(8,128)S(1)}, u32[]{:S(2)}, u32[]{:S(2)}) collective-permute-start(f32[65,8,128]{2,1,0:T(8,128)S(1)} %get-tuple-element.117), channel_id=1, source_target_pairs={{0,1},{1,0},{2,3},{3,2},{4,5},{5,4},{6,7},{7,6},{8,9},{9,8},{10,11... | collective-permute-start | bytes 798728 | tf_op jit(solution)/shard_map/ppermute | solution.py:421

commit v8 on v7

--- a/solution.py
+++ b/solution.py
@@ -9,7 +9,7 @@
 F32 = jnp.float32
 BF16 = jnp.bfloat16
 PAD = 8
-STEPS = 4
+STEPS = 2
 LIMIT = 24 << 20
 HBM = pl.BlockSpec(memory_space=pltpu.MemorySpace.HBM)
 VMEM = pl.BlockSpec(memory_space=pltpu.MemorySpace.VMEM)

time: 48.5 us -> 47.8 us (0.986)
  Pallas kernels: 17.5 us -> 16.6 us
    pallas_call x12, Pallas kernels: 17.5 us -> 16.6 us  [call(): pl.pallas_call(kernel, out_shape=outs, in_specs=in_specs or [VMEM] * len(...]
where the time goes in v8:
time: 47.8 us; the launch traced here: 47.5 us
  starting transfers between devices  23.7 us (50%)
  Pallas kernels  16.6 us (35%)
  waiting for transfers between devices  6.46 us (14%)
  between operations  0.76 us (2%)
    pallas_call x12, Pallas kernels, call(): pl.pallas_call(kernel, out_shape=outs, in_specs=in_specs or [VMEM] * len(...  16.6 us
    ppermute x2, starting transfers between devices, turn(): lax.ppermute(x, 'seq', [(i, (i + by) % devices) for i in range(devices)])  8.55 us
    ppermute x2, starting transfers between devices, shift(): lax.ppermute(x, 'seq', [(i, i + by) for i in range(devices) if 0 <= i + b...  8.29 us
    ppermute x3, starting transfers between devices, far_squares(): lines.append(lax.ppermute(line, 'seq', pairs))  5.95 us
    ppermute x2, waiting for transfers between devices, shift(): lax.ppermute(x, 'seq', [(i, i + by) for i in range(devices) if 0 <= i + b...  2.71 us
    ppermute x4, waiting for transfers between devices, swap(): return lax.ppermute(x, 'seq', [(i, i ^ 1) for i in range(devices)])  2.4 us
    ppermute x3, waiting for transfers between devices, far_squares(): lines.append(lax.ppermute(line, 'seq', pairs))  1.35 us
  transfers between devices with their start and end apart: 11, of which 5 were waited for; matrix products, arithmetic and copies ran while one was open for 0% of the time, Pallas kernels for 23%

profile of v8, /device:TPU:0, one launch (start us, length us, event | category | flops | bytes accessed | tf_op | source)
XLA Modules:
  0.0 47.5 jit_solution(5828120517234948935)
XLA Ops:
  0.6 2.6 %shard_map.111 = (bf16[512,1024]{1,0:T(8,128)(2,1)S(1)}, f32[66,8,128]{2,1,0:T(8,128)S(1)}, bf16[96,512]{1,0:T(8,128)(2,1)S(1)}, bf16[96,512]{1,0:T(8,128)(2,1)S...) custom-call(s32[16]{0:T(128)} %lengths_hbm.1, ...), custom_call_target="tpu_custom_call" | custom-call | bytes 10641728 | tf_op jit(solution)/shard_map/pallas_call | solution.py:404
  3.3 0.5 %collective-permute-start = (f32[66,8,128]{2,1,0:T(8,128)S(1)}, f32[66,8,128]{2,1,0:T(8,128)S(1)}, u32[]{:S(2)}, u32[]{:S(2)}) collective-permute-start(f32[66,8,128]{2,1,0:T(8,128)S(1)} %get-tuple-element.69.send_ref), channel_id=1, source_target_pairs={{0,1},{1,0},{2,3},{3,2},{4,5},{5,4},{6,7},{7,6},{8,9},{9,8},{10,11... | collective-permute-start | bytes 811016 | tf_op jit(solution)/shard_map/ppermute | solution.py:421
  3.8 0.9 %shard_map.112 = (bf16[512,1024]{1,0:T(8,128)(2,1)S(1)}, f32[66,8,128]{2,1,0:T(8,128)S(1)}) custom-call(bf16[96,512]{1,0:T(8,128)(2,1)S(1)} %get-tuple-element.63.f3_ref, bf16[96,512]{1,0:T(8,128)(2,1)S(1)} %get-tuple-element.64.s3_ref, bf16[64,512]{1,0:T(8,128)(2,1)S(1)} %get-tuple-element.65.bm_ref, f32[8,2048]{1,0:T(8,128)S(1)} %get-tuple-element.66.rows_ref, ...), custom_call_target="tpu_custom_call" | custom-call | bytes 3743744 | tf_op jit(solution)/shard_map/pallas_call | solution.py:404
  4.7 0.3 collective-permute-done.got_ref
  5.0 4.8 %collective-permute-start.1 = (f32[66,8,128]{2,1,0:T(8,128)S(1)}, f32[66,8,128]{2,1,0:T(8,128)S(1)}, u32[]{:S(2)}, u32[]{:S(2)}) collective-permute-start(f32[66,8,128]{2,1,0:T(8,128)S(1)} %get-tuple-element.71), channel_id=1, source_target_pairs={{0,2},{1,3},{2,4},{3,5},{4,6},{5,7},{6,8},{7,9},{8,10},{9,11},{10,... | collective-permute-start | bytes 811016 | tf_op jit(solution)/shard_map/ppermute | solution.py:425
  9.9 3.5 %collective-permute-start.2 = (f32[65,8,128]{2,1,0:T(8,128)S(1)}, f32[65,8,128]{2,1,0:T(8,128)S(1)}, u32[]{:S(2)}, u32[]{:S(2)}) collective-permute-start(f32[65,8,128]{2,1,0:T(8,128)S(1)} %get-tuple-element.72), channel_id=1, source_target_pairs={{0,4},{1,5},{2,6},{3,7},{4,8},{5,9},{6,10},{7,11},{8,12},{9,13},{1... | collective-permute-start | bytes 798728 | tf_op jit(solution)/shard_map/ppermute | solution.py:425
  13.3 2.9 %shard_map.115 = (f32[512,2048]{1,0:T(8,128)S(1)}, bf16[512,512]{1,0:T(8,128)(2,1)S(1)}, f32[512,2048]{1,0:T(8,128)S(1)}, f32[512,2048]{1,0:T(8,128)S(1)}, bf16[...) custom-call(bf16[512,1024]{1,0:T(8,128)(2,1)S(1)} %get-tuple-element.74.xf_ref.x_ref, ...), custom_call_target="tpu_custom_call" | custom-call | flops 1073741824 | bytes 20201472 | tf_op jit(solution)/shard_map/pallas_call | solution.py:404
  16.3 2.7 %collective-permute-done.2.two_ref = f32[65,8,128]{2,1,0:T(8,128)S(1)} collective-permute-done((f32[65,8,128]{2,1,0:T(8,128)S(1)}, f32[65,8,128]{2,1,0:T(8,128)S(1)}, u32[]{:S(2)}, u32[]{:S(2)}) %collective-permute-start.2) | collective-permute-done | bytes 266272 | tf_op jit(solution)/shard_map/ppermute | solution.py:425
  19.0 0.0 collective-permute-done.1.one_ref
  19.0 0.1 shard_map.114
  19.1 0.1 collective-permute-start.3
  19.1 0.8 %shard_map.116 = (f32[512,1024]{1,0:T(8,128)S(1)}, bf16[512,1024]{1,0:T(8,128)(2,1)S(1)}, f32[66,8,128]{2,1,0:T(8,128)S(1)}) custom-call(f32[512,2048]{1,0:T(8,128)S(1)} %get-tuple-element.89.base_ref, f32[512,2048]{1,0:T(8,128)S(1)} %get-tuple-element.90.enter_ref, f32[8,2048]{1,0:T(8,128)S(1)} %get-tuple-element.66.rows_ref, ...), custom_call_target="tpu_custom_call" | custom-call | bytes 12333056 | tf_op jit(solution)/shard_map/pallas_call | solution.py:404
  20.0 0.7 %collective-permute-done.3.state_ref.other_ref = f32[65,8,128]{2,1,0:T(8,128)S(1)} collective-permute-done((f32[65,8,128]{2,1,0:T(8,128)S(1)}, f32[65,8,128]{2,1,0:T(8,128)S(1)}, u32[]{:S(2)}, u32[]{:S(2)}) %collective-permute-start.3) | collective-permute-done | bytes 266272 | tf_op jit(solution)/shard_map/ppermute | solution.py:421
  20.7 0.8 %shard_map.117 = (f32[512,1024]{1,0:T(8,128)S(1)}, bf16[512,1024]{1,0:T(8,128)(2,1)S(1)}, f32[66,8,128]{2,1,0:T(8,128)S(1)}) custom-call(f32[512,2048]{1,0:T(8,128)S(1)} %get-tuple-element.89.base_ref, f32[512,2048]{1,0:T(8,128)S(1)} %get-tuple-element.90.enter_ref, f32[8,2048]{1,0:T(8,128)S(1)} %get-tuple-element.66.rows_ref, ...), custom_call_target="tpu_custom_call" | custom-call | bytes 12603392 | tf_op jit(solution)/shard_map/pallas_call | solution.py:404
  21.5 0.2 collective-permute-start.4
  21.7 1.4 %collective-permute-done.4.got_ref = f32[66,8,128]{2,1,0:T(8,128)S(1)} collective-permute-done((f32[66,8,128]{2,1,0:T(8,128)S(1)}, f32[66,8,128]{2,1,0:T(8,128)S(1)}, u32[]{:S(2)}, u32[]{:S(2)}) %collective-permute-start.4) | collective-permute-done | bytes 270368 | tf_op jit(solution)/shard_map/ppermute | solution.py:421
  23.1 8.1 %collective-permute-start.5 = (f32[66,8,128]{2,1,0:T(8,128)S(1)}, f32[66,8,128]{2,1,0:T(8,128)S(1)}, u32[]{:S(2)}, u32[]{:S(2)}) collective-permute-start(f32[66,8,128]{2,1,0:T(8,128)S(1)} %get-tuple-element.97), channel_id=1, source_target_pairs={{0,14},{1,15},{2,0},{3,1},{4,2},{5,3},{6,4},{7,5},{8,6},{9,7},{10,... | collective-permute-start | bytes 811016 | tf_op jit(solution)/shard_map/ppermute | solution.py:431
  31.2 0.4 collective-permute-start.6
  31.7 2.1 %collective-permute-start.9 = (f32[8,128]{1,0:T(8,128)S(1)}, f32[8,128]{1,0:T(8,128)S(1)}, u32[]{:S(2)}, u32[]{:S(2)}) collective-permute-start(f32[8,128]{1,0:T(8,128)S(1)} %get-tuple-element.96.line_ref), channel_id=1, source_target_pairs={{0,2},{2,4},{4,6},{6,8},{8,10},{10,12},{12,14},{14,0},{16,18},{18,... | collective-permute-start | bytes 12296 | tf_op jit(solution)/shard_map/ppermute | solution.py:495
  33.8 0.3 collective-permute-start.8
  34.1 3.6 %collective-permute-start.7 = (f32[8,128]{1,0:T(8,128)S(1)}, f32[8,128]{1,0:T(8,128)S(1)}, u32[]{:S(2)}, u32[]{:S(2)}) collective-permute-start(f32[8,128]{1,0:T(8,128)S(1)} %get-tuple-element.96.line_ref), channel_id=1, source_target_pairs={{0,10},{1,9},{2,12},{3,11},{4,14},{5,13},{6,0},{7,15},{8,2},{9,1},... | collective-permute-start | bytes 12296 | tf_op jit(solution)/shard_map/ppermute | solution.py:495
  37.7 4.2 %shard_map.120 = (f32[512,1024]{1,0:T(8,128)S(1)}, f32[512,1024]{1,0:T(8,128)S(1)}, f32[64,512]{1,0:T(8,128)S(1)}, f32[64,512]{1,0:T(8,128)}) custom-call(f32[512,1024]{1,0:T(8,128)S(1)} %get-tuple-element.100.mmf_ref, f32[512,1024]{1,0:T(8,128)S(1)} %get-tuple-element.101.mmo_ref, bf16[512,1024]{1,0:T(8,128)(2,1)S(1)} %get-tuple-element.102.yf_ref, ...), custom_call_target="tpu_custom_call" | custom-call | flops 2147483648 | bytes 18309120 | tf_op jit(solution)/shard_map/pallas_call | solution.py:404
  41.9 0.0 collective-permute-done.9.refs_2_
  41.9 1.3 %collective-permute-done.8.refs_1_ = f32[8,128]{1,0:T(8,128)S(1)} collective-permute-done((f32[8,128]{1,0:T(8,128)S(1)}, f32[8,128]{1,0:T(8,128)S(1)}, u32[]{:S(2)}, u32[]{:S(2)}) %collective-permute-start.8) | collective-permute-done | bytes 4128 | tf_op jit(solution)/shard_map/ppermute | solution.py:495
  43.2 0.0 collective-permute-done.7.refs_0_
  43.2 0.0 collective-permute-done.6.two_ref
  43.2 0.0 collective-permute-done.5.one_ref
  43.2 0.1 shard_map.119
  43.3 0.1 collective-permute-start.10
  43.4 1.9 %shard_map.121 = (f32[512,2048]{1,0:T(8,128)}, f32[512,128]{1,0:T(8,128)S(1)}) custom-call(f32[512,1024]{1,0:T(8,128)S(1)} %get-tuple-element.110.g_ref, bf16[512,1024]{1,0:T(8,128)(2,1)S(1)} %get-tuple-element.75.xo_ref.x_ref, f32[512,2048]{1,0:T(8,128)S(1)} %get-tuple-element.105.sf_ref, f32[8,2048]{1,0:T(8,128)S(1)} %get-tuple-element.66.rows_ref, ...), custom_call_target="tpu_custom_call" | custom-call | bytes 12259328 | tf_op jit(solution)/shard_map/pallas_call | solution.py:404
  45.3 0.0 collective-permute-done.10.other_ref
  45.3 2.1 %shard_map.122 = (f32[512,2048]{1,0:T(8,128)}, f32[64,512]{1,0:T(8,128)}, f32[1,128]{1,0:T(1,128)}) custom-call(f32[512,2048]{1,0:T(8,128)} %get-tuple-element.113._gv_in, f32[512,1024]{1,0:T(8,128)S(1)} %get-tuple-element.114.g_ref, bf16[512,1024]{1,0:T(8,128)(2,1)S(1)} %get-tuple-element.74.xf_ref.x_ref, ...), custom_call_target="tpu_custom_call", output_to_operand_aliasing={{0}: (0, {})} | custom-call | bytes 16998912 | tf_op jit(solution)/shard_map/pallas_call | solution.py:404
  (2 shorter events, 0.1 us)
Async XLA Ops:
  3.3 1.7 %collective-permute-start = (f32[66,8,128]{2,1,0:T(8,128)S(1)}, f32[66,8,128]{2,1,0:T(8,128)S(1)}, u32[]{:S(2)}, u32[]{:S(2)}) collective-permute-start(f32[66,8,128]{2,1,0:T(8,128)S(1)} %get-tuple-element.69.send_ref), channel_id=1, source_target_pairs={{0,1},{1,0},{2,3},{3,2},{4,5},{5,4},{6,7},{7,6},{8,9},{9,8},{10,11... | collective-permute-start | bytes 811016 | tf_op jit(solution)/shard_map/ppermute | solution.py:421
  5.0 13.9 %collective-permute-start.1 = (f32[66,8,128]{2,1,0:T(8,128)S(1)}, f32[66,8,128]{2,1,0:T(8,128)S(1)}, u32[]{:S(2)}, u32[]{:S(2)}) collective-permute-start(f32[66,8,128]{2,1,0:T(8,128)S(1)} %get-tuple-element.71), channel_id=1, source_target_pairs={{0,2},{1,3},{2,4},{3,5},{4,6},{5,7},{6,8},{7,9},{8,10},{9,11},{10,... | collective-permute-start | bytes 811016 | tf_op jit(solution)/shard_map/ppermute | solution.py:425
  9.9 9.1 %collective-permute-start.2 = (f32[65,8,128]{2,1,0:T(8,128)S(1)}, f32[65,8,128]{2,1,0:T(8,128)S(1)}, u32[]{:S(2)}, u32[]{:S(2)}) collective-permute-start(f32[65,8,128]{2,1,0:T(8,128)S(1)} %get-tuple-element.72), channel_id=1, source_target_pairs={{0,4},{1,5},{2,6},{3,7},{4,8},{5,9},{6,10},{7,11},{8,12},{9,13},{1... | collective-permute-start | bytes 798728 | tf_op jit(solution)/shard_map/ppermute | solution.py:425
  19.1 1.6 %collective-permute-start.3 = (f32[65,8,128]{2,1,0:T(8,128)S(1)}, f32[65,8,128]{2,1,0:T(8,128)S(1)}, u32[]{:S(2)}, u32[]{:S(2)}) collective-permute-start(f32[65,8,128]{2,1,0:T(8,128)S(1)} %get-tuple-element.94), channel_id=1, source_target_pairs={{0,1},{1,0},{2,3},{3,2},{4,5},{5,4},{6,7},{7,6},{8,9},{9,8},{10,11... | collective-permute-start | bytes 798728 | tf_op jit(solution)/shard_map/ppermute | solution.py:421
  21.5 1.6 %collective-permute-start.4 = (f32[66,8,128]{2,1,0:T(8,128)S(1)}, f32[66,8,128]{2,1,0:T(8,128)S(1)}, u32[]{:S(2)}, u32[]{:S(2)}) collective-permute-start(f32[66,8,128]{2,1,0:T(8,128)S(1)} %get-tuple-element.95.send_ref), channel_id=1, source_target_pairs={{0,1},{1,0},{2,3},{3,2},{4,5},{5,4},{6,7},{7,6},{8,9},{9,8},{10,11... | collective-permute-start | bytes 811016 | tf_op jit(solution)/shard_map/ppermute | solution.py:421
  23.1 20.1 %collective-permute-start.5 = (f32[66,8,128]{2,1,0:T(8,128)S(1)}, f32[66,8,128]{2,1,0:T(8,128)S(1)}, u32[]{:S(2)}, u32[]{:S(2)}) collective-permute-start(f32[66,8,128]{2,1,0:T(8,128)S(1)} %get-tuple-element.97), channel_id=1, source_target_pairs={{0,14},{1,15},{2,0},{3,1},{4,2},{5,3},{6,4},{7,5},{8,6},{9,7},{10,... | collective-permute-start | bytes 811016 | tf_op jit(solution)/shard_map/ppermute | solution.py:431
  31.2 12.0 %collective-permute-start.6 = (f32[65,8,128]{2,1,0:T(8,128)S(1)}, f32[65,8,128]{2,1,0:T(8,128)S(1)}, u32[]{:S(2)}, u32[]{:S(2)}) collective-permute-start(f32[65,8,128]{2,1,0:T(8,128)S(1)} %get-tuple-element.98), channel_id=1, source_target_pairs={{0,12},{1,13},{2,14},{3,15},{4,0},{5,1},{6,2},{7,3},{8,4},{9,5},{1... | collective-permute-start | bytes 798728 | tf_op jit(solution)/shard_map/ppermute | solution.py:431
  31.7 10.2 %collective-permute-start.9 = (f32[8,128]{1,0:T(8,128)S(1)}, f32[8,128]{1,0:T(8,128)S(1)}, u32[]{:S(2)}, u32[]{:S(2)}) collective-permute-start(f32[8,128]{1,0:T(8,128)S(1)} %get-tuple-element.96.line_ref), channel_id=1, source_target_pairs={{0,2},{2,4},{4,6},{6,8},{8,10},{10,12},{12,14},{14,0},{16,18},{18,... | collective-permute-start | bytes 12296 | tf_op jit(solution)/shard_map/ppermute | solution.py:495
  33.8 9.4 %collective-permute-start.8 = (f32[8,128]{1,0:T(8,128)S(1)}, f32[8,128]{1,0:T(8,128)S(1)}, u32[]{:S(2)}, u32[]{:S(2)}) collective-permute-start(f32[8,128]{1,0:T(8,128)S(1)} %get-tuple-element.96.line_ref), channel_id=1, source_target_pairs={{0,6},{1,5},{2,8},{3,7},{4,10},{5,9},{6,12},{7,11},{8,14},{9,13},{... | collective-permute-start | bytes 12296 | tf_op jit(solution)/shard_map/ppermute | solution.py:495
  34.1 9.1 %collective-permute-start.7 = (f32[8,128]{1,0:T(8,128)S(1)}, f32[8,128]{1,0:T(8,128)S(1)}, u32[]{:S(2)}, u32[]{:S(2)}) collective-permute-start(f32[8,128]{1,0:T(8,128)S(1)} %get-tuple-element.96.line_ref), channel_id=1, source_target_pairs={{0,10},{1,9},{2,12},{3,11},{4,14},{5,13},{6,0},{7,15},{8,2},{9,1},... | collective-permute-start | bytes 12296 | tf_op jit(solution)/shard_map/ppermute | solution.py:495
  43.3 2.0 %collective-permute-start.10 = (f32[65,8,128]{2,1,0:T(8,128)S(1)}, f32[65,8,128]{2,1,0:T(8,128)S(1)}, u32[]{:S(2)}, u32[]{:S(2)}) collective-permute-start(f32[65,8,128]{2,1,0:T(8,128)S(1)} %get-tuple-element.117), channel_id=1, source_target_pairs={{0,1},{1,0},{2,3},{3,2},{4,5},{5,4},{6,7},{7,6},{8,9},{9,8},{10,11... | collective-permute-start | bytes 798728 | tf_op jit(solution)/shard_map/ppermute | solution.py:421

commit v9 on v8

--- a/solution.py
+++ b/solution.py
@@ -10,6 +10,7 @@
 BF16 = jnp.bfloat16
 PAD = 8
 STEPS = 2
+PIECES = 2
 LIMIT = 24 << 20
 HBM = pl.BlockSpec(memory_space=pltpu.MemorySpace.HBM)
 VMEM = pl.BlockSpec(memory_space=pltpu.MemorySpace.VMEM)
@@ -341,18 +342,24 @@
 def finish_half(first, g_ref, x_ref, sf_ref, rows_ref, bm2_ref, state_ref, gv_hbm, gv, sems):
     half = g_ref.shape[1]
     width = 2 * half // STEPS
+    piece = width // PIECES
     n = bm2_ref.shape[1] // 2
     copies = []
     acc = jnp.zeros(bm2_ref.shape, F32)
     for a in range(STEPS // 2):
         j = first + a
         rel = slice(j * width, (j + 1) * width)
-        part = slice(a * width, (a + 1) * width)
         adjoint = split2(get_half(a, n, state_ref, width) * rows_ref[1:2, rel])
-        gv[:, part] = g_ref[:, part] + sf_ref[:, rel] * dot(bm2_ref[...], adjoint)
-        copies.append(pltpu.make_async_copy(gv.at[:, part], gv_hbm.at[:, span_of(j, width)], sems.at[a]))
-        copies[a].start()
-        acc = acc + dot_nt(x_ref[:, part], adjoint)
+        for k in range(PIECES):
+            part = slice(a * width + k * piece, a * width + (k + 1) * piece)
+            near = slice(j * width + k * piece, j * width + (k + 1) * piece)
+            gv[:, part] = g_ref[:, part] + sf_ref[:, near] * dot(
+                bm2_ref[...], adjoint[:, k * piece : (k + 1) * piece]
+            )
+            place = pl.ds(pl.multiple_of(chunk_of(j) * width + k * piece, piece), piece)
+            copies.append(pltpu.make_async_copy(gv.at[:, part], gv_hbm.at[:, place], sems.at[a * PIECES + k]))
+            copies[-1].start()
+        acc = acc + dot_nt(x_ref[:, a * width : (a + 1) * width], adjoint)
     return acc, copies
 
 
@@ -387,7 +394,7 @@
     n = bm2_ref.shape[1] // 2
     last = mine_ref.shape[0] - 1
     loss[...] = jnp.broadcast_to(jnp.sum(mine_ref[last] + other_ref[last]) * scale, (1, 128))
-    half = STEPS // 2
+    half = STEPS // 2 * PIECES
     out_loss = pltpu.make_async_copy(loss, loss_hbm, sems.at[half])
     out_loss.start()
     acc, copies = finish_half(0, g_ref, x_ref, sf_ref, rows_ref, bm2_ref, other_ref, gv_hbm, gv, sems)
@@ -627,7 +634,7 @@
         [g_own, x_own, sf, rows, bm2, mine],
         [out(length, total), out(length, 2 * state)],
         out_specs=[HBM, VMEM],
-        scratch=[pltpu.VMEM((length, total // 2), F32), dma((STEPS // 2,))],
+        scratch=[pltpu.VMEM((length, total // 2), F32), dma((STEPS // 2 * PIECES,))],
     )
     scale = 1.0 / (devices * length * total)
     grad_values, grad_b, loss = call(
@@ -640,7 +647,7 @@
             pltpu.VMEM((length, total // 2), F32),
             pltpu.VMEM((state, length), F32),
             pltpu.VMEM((1, 128), F32),
-            dma((STEPS // 2 + 2,)),
+            dma((STEPS // 2 * PIECES + 2,)),
         ],
         aliases={0: 0},
     )

time: 47.8 us -> 47.5 us (level)
  no operation moved by 1% of the time
where the time goes in v9:
time: 47.5 us; the launch traced here: 47.2 us
  starting transfers between devices  23.7 us (50%)
  Pallas kernels  16.3 us (34%)
  waiting for transfers between devices  6.46 us (14%)
  between operations  0.76 us (2%)
    pallas_call x12, Pallas kernels, call(): pl.pallas_call(kernel, out_shape=outs, in_specs=in_specs or [VMEM] * len(...  16.3 us
    ppermute x2, starting transfers between devices, turn(): lax.ppermute(x, 'seq', [(i, (i + by) % devices) for i in range(devices)])  8.55 us
    ppermute x2, starting transfers between devices, shift(): lax.ppermute(x, 'seq', [(i, i + by) for i in range(devices) if 0 <= i + b...  8.29 us
    ppermute x3, starting transfers between devices, far_squares(): lines.append(lax.ppermute(line, 'seq', pairs))  5.95 us
    ppermute x2, waiting for transfers between devices, shift(): lax.ppermute(x, 'seq', [(i, i + by) for i in range(devices) if 0 <= i + b...  2.71 us
    ppermute x4, waiting for transfers between devices, swap(): return lax.ppermute(x, 'seq', [(i, i ^ 1) for i in range(devices)])  2.4 us
    ppermute x3, waiting for transfers between devices, far_squares(): lines.append(lax.ppermute(line, 'seq', pairs))  1.35 us
  transfers between devices with their start and end apart: 11, of which 5 were waited for; matrix products, arithmetic and copies ran while one was open for 0% of the time, Pallas kernels for 23%

profile of v9, /device:TPU:0, one launch (start us, length us, event | category | flops | bytes accessed | tf_op | source)
XLA Modules:
  0.0 47.2 jit_solution(17817313778113228214)
XLA Ops:
  0.6 2.6 %shard_map.111 = (bf16[512,1024]{1,0:T(8,128)(2,1)S(1)}, f32[66,8,128]{2,1,0:T(8,128)S(1)}, bf16[96,512]{1,0:T(8,128)(2,1)S(1)}, bf16[96,512]{1,0:T(8,128)(2,1)S...) custom-call(s32[16]{0:T(128)} %lengths_hbm.1, ...), custom_call_target="tpu_custom_call" | custom-call | bytes 10641728 | tf_op jit(solution)/shard_map/pallas_call | solution.py:411
  3.3 0.5 %collective-permute-start = (f32[66,8,128]{2,1,0:T(8,128)S(1)}, f32[66,8,128]{2,1,0:T(8,128)S(1)}, u32[]{:S(2)}, u32[]{:S(2)}) collective-permute-start(f32[66,8,128]{2,1,0:T(8,128)S(1)} %get-tuple-element.69.send_ref), channel_id=1, source_target_pairs={{0,1},{1,0},{2,3},{3,2},{4,5},{5,4},{6,7},{7,6},{8,9},{9,8},{10,11... | collective-permute-start | bytes 811016 | tf_op jit(solution)/shard_map/ppermute | solution.py:428
  3.8 0.9 %shard_map.112 = (bf16[512,1024]{1,0:T(8,128)(2,1)S(1)}, f32[66,8,128]{2,1,0:T(8,128)S(1)}) custom-call(bf16[96,512]{1,0:T(8,128)(2,1)S(1)} %get-tuple-element.63.f3_ref, bf16[96,512]{1,0:T(8,128)(2,1)S(1)} %get-tuple-element.64.s3_ref, bf16[64,512]{1,0:T(8,128)(2,1)S(1)} %get-tuple-element.65.bm_ref, f32[8,2048]{1,0:T(8,128)S(1)} %get-tuple-element.66.rows_ref, ...), custom_call_target="tpu_custom_call" | custom-call | bytes 3743744 | tf_op jit(solution)/shard_map/pallas_call | solution.py:411
  4.7 0.3 collective-permute-done.got_ref
  5.0 4.8 %collective-permute-start.1 = (f32[66,8,128]{2,1,0:T(8,128)S(1)}, f32[66,8,128]{2,1,0:T(8,128)S(1)}, u32[]{:S(2)}, u32[]{:S(2)}) collective-permute-start(f32[66,8,128]{2,1,0:T(8,128)S(1)} %get-tuple-element.71), channel_id=1, source_target_pairs={{0,2},{1,3},{2,4},{3,5},{4,6},{5,7},{6,8},{7,9},{8,10},{9,11},{10,... | collective-permute-start | bytes 811016 | tf_op jit(solution)/shard_map/ppermute | solution.py:432
  9.9 3.5 %collective-permute-start.2 = (f32[65,8,128]{2,1,0:T(8,128)S(1)}, f32[65,8,128]{2,1,0:T(8,128)S(1)}, u32[]{:S(2)}, u32[]{:S(2)}) collective-permute-start(f32[65,8,128]{2,1,0:T(8,128)S(1)} %get-tuple-element.72), channel_id=1, source_target_pairs={{0,4},{1,5},{2,6},{3,7},{4,8},{5,9},{6,10},{7,11},{8,12},{9,13},{1... | collective-permute-start | bytes 798728 | tf_op jit(solution)/shard_map/ppermute | solution.py:432
  13.3 2.9 %shard_map.115 = (f32[512,2048]{1,0:T(8,128)S(1)}, bf16[512,512]{1,0:T(8,128)(2,1)S(1)}, f32[512,2048]{1,0:T(8,128)S(1)}, f32[512,2048]{1,0:T(8,128)S(1)}, bf16[...) custom-call(bf16[512,1024]{1,0:T(8,128)(2,1)S(1)} %get-tuple-element.74.xf_ref.x_ref, ...), custom_call_target="tpu_custom_call" | custom-call | flops 1073741824 | bytes 20201472 | tf_op jit(solution)/shard_map/pallas_call | solution.py:411
  16.3 2.7 %collective-permute-done.2.two_ref = f32[65,8,128]{2,1,0:T(8,128)S(1)} collective-permute-done((f32[65,8,128]{2,1,0:T(8,128)S(1)}, f32[65,8,128]{2,1,0:T(8,128)S(1)}, u32[]{:S(2)}, u32[]{:S(2)}) %collective-permute-start.2) | collective-permute-done | bytes 266272 | tf_op jit(solution)/shard_map/ppermute | solution.py:432
  19.0 0.0 collective-permute-done.1.one_ref
  19.0 0.1 shard_map.114
  19.1 0.1 collective-permute-start.3
  19.1 0.8 %shard_map.116 = (f32[512,1024]{1,0:T(8,128)S(1)}, bf16[512,1024]{1,0:T(8,128)(2,1)S(1)}, f32[66,8,128]{2,1,0:T(8,128)S(1)}) custom-call(f32[512,2048]{1,0:T(8,128)S(1)} %get-tuple-element.89.base_ref, f32[512,2048]{1,0:T(8,128)S(1)} %get-tuple-element.90.enter_ref, f32[8,2048]{1,0:T(8,128)S(1)} %get-tuple-element.66.rows_ref, ...), custom_call_target="tpu_custom_call" | custom-call | bytes 12333056 | tf_op jit(solution)/shard_map/pallas_call | solution.py:411
  20.0 0.7 %collective-permute-done.3.state_ref.other_ref = f32[65,8,128]{2,1,0:T(8,128)S(1)} collective-permute-done((f32[65,8,128]{2,1,0:T(8,128)S(1)}, f32[65,8,128]{2,1,0:T(8,128)S(1)}, u32[]{:S(2)}, u32[]{:S(2)}) %collective-permute-start.3) | collective-permute-done | bytes 266272 | tf_op jit(solution)/shard_map/ppermute | solution.py:428
  20.7 0.8 %shard_map.117 = (f32[512,1024]{1,0:T(8,128)S(1)}, bf16[512,1024]{1,0:T(8,128)(2,1)S(1)}, f32[66,8,128]{2,1,0:T(8,128)S(1)}) custom-call(f32[512,2048]{1,0:T(8,128)S(1)} %get-tuple-element.89.base_ref, f32[512,2048]{1,0:T(8,128)S(1)} %get-tuple-element.90.enter_ref, f32[8,2048]{1,0:T(8,128)S(1)} %get-tuple-element.66.rows_ref, ...), custom_call_target="tpu_custom_call" | custom-call | bytes 12603392 | tf_op jit(solution)/shard_map/pallas_call | solution.py:411
  21.5 0.2 collective-permute-start.4
  21.7 1.4 %collective-permute-done.4.got_ref = f32[66,8,128]{2,1,0:T(8,128)S(1)} collective-permute-done((f32[66,8,128]{2,1,0:T(8,128)S(1)}, f32[66,8,128]{2,1,0:T(8,128)S(1)}, u32[]{:S(2)}, u32[]{:S(2)}) %collective-permute-start.4) | collective-permute-done | bytes 270368 | tf_op jit(solution)/shard_map/ppermute | solution.py:428
  23.1 8.1 %collective-permute-start.5 = (f32[66,8,128]{2,1,0:T(8,128)S(1)}, f32[66,8,128]{2,1,0:T(8,128)S(1)}, u32[]{:S(2)}, u32[]{:S(2)}) collective-permute-start(f32[66,8,128]{2,1,0:T(8,128)S(1)} %get-tuple-element.97), channel_id=1, source_target_pairs={{0,14},{1,15},{2,0},{3,1},{4,2},{5,3},{6,4},{7,5},{8,6},{9,7},{10,... | collective-permute-start | bytes 811016 | tf_op jit(solution)/shard_map/ppermute | solution.py:438
  31.2 0.4 collective-permute-start.6
  31.7 2.1 %collective-permute-start.9 = (f32[8,128]{1,0:T(8,128)S(1)}, f32[8,128]{1,0:T(8,128)S(1)}, u32[]{:S(2)}, u32[]{:S(2)}) collective-permute-start(f32[8,128]{1,0:T(8,128)S(1)} %get-tuple-element.96.line_ref), channel_id=1, source_target_pairs={{0,2},{2,4},{4,6},{6,8},{8,10},{10,12},{12,14},{14,0},{16,18},{18,... | collective-permute-start | bytes 12296 | tf_op jit(solution)/shard_map/ppermute | solution.py:502
  33.8 0.3 collective-permute-start.8
  34.1 3.6 %collective-permute-start.7 = (f32[8,128]{1,0:T(8,128)S(1)}, f32[8,128]{1,0:T(8,128)S(1)}, u32[]{:S(2)}, u32[]{:S(2)}) collective-permute-start(f32[8,128]{1,0:T(8,128)S(1)} %get-tuple-element.96.line_ref), channel_id=1, source_target_pairs={{0,10},{1,9},{2,12},{3,11},{4,14},{5,13},{6,0},{7,15},{8,2},{9,1},... | collective-permute-start | bytes 12296 | tf_op jit(solution)/shard_map/ppermute | solution.py:502
  37.7 4.2 %shard_map.120 = (f32[512,1024]{1,0:T(8,128)S(1)}, f32[512,1024]{1,0:T(8,128)S(1)}, f32[64,512]{1,0:T(8,128)S(1)}, f32[64,512]{1,0:T(8,128)}) custom-call(f32[512,1024]{1,0:T(8,128)S(1)} %get-tuple-element.100.mmf_ref, f32[512,1024]{1,0:T(8,128)S(1)} %get-tuple-element.101.mmo_ref, bf16[512,1024]{1,0:T(8,128)(2,1)S(1)} %get-tuple-element.102.yf_ref, ...), custom_call_target="tpu_custom_call" | custom-call | flops 2147483648 | bytes 18309120 | tf_op jit(solution)/shard_map/pallas_call | solution.py:411
  41.9 0.0 collective-permute-done.9.refs_2_
  41.9 1.3 %collective-permute-done.8.refs_1_ = f32[8,128]{1,0:T(8,128)S(1)} collective-permute-done((f32[8,128]{1,0:T(8,128)S(1)}, f32[8,128]{1,0:T(8,128)S(1)}, u32[]{:S(2)}, u32[]{:S(2)}) %collective-permute-start.8) | collective-permute-done | bytes 4128 | tf_op jit(solution)/shard_map/ppermute | solution.py:502
  43.2 0.0 collective-permute-done.7.refs_0_
  43.2 0.0 collective-permute-done.6.two_ref
  43.2 0.0 collective-permute-done.5.one_ref
  43.2 0.1 shard_map.119
  43.3 0.1 collective-permute-start.10
  43.4 1.8 %shard_map.121 = (f32[512,2048]{1,0:T(8,128)}, f32[512,128]{1,0:T(8,128)S(1)}) custom-call(f32[512,1024]{1,0:T(8,128)S(1)} %get-tuple-element.110.g_ref, bf16[512,1024]{1,0:T(8,128)(2,1)S(1)} %get-tuple-element.75.xo_ref.x_ref, f32[512,2048]{1,0:T(8,128)S(1)} %get-tuple-element.105.sf_ref, f32[8,2048]{1,0:T(8,128)S(1)} %get-tuple-element.66.rows_ref, ...), custom_call_target="tpu_custom_call" | custom-call | bytes 12259328 | tf_op jit(solution)/shard_map/pallas_call | solution.py:411
  45.2 0.0 collective-permute-done.10.other_ref
  45.2 1.9 %shard_map.122 = (f32[512,2048]{1,0:T(8,128)}, f32[64,512]{1,0:T(8,128)}, f32[1,128]{1,0:T(1,128)}) custom-call(f32[512,2048]{1,0:T(8,128)} %get-tuple-element.113._gv_in, f32[512,1024]{1,0:T(8,128)S(1)} %get-tuple-element.114.g_ref, bf16[512,1024]{1,0:T(8,128)(2,1)S(1)} %get-tuple-element.74.xf_ref.x_ref, ...), custom_call_target="tpu_custom_call", output_to_operand_aliasing={{0}: (0, {})} | custom-call | bytes 16998912 | tf_op jit(solution)/shard_map/pallas_call | solution.py:411
  (2 shorter events, 0.1 us)
Async XLA Ops:
  3.3 1.7 %collective-permute-start = (f32[66,8,128]{2,1,0:T(8,128)S(1)}, f32[66,8,128]{2,1,0:T(8,128)S(1)}, u32[]{:S(2)}, u32[]{:S(2)}) collective-permute-start(f32[66,8,128]{2,1,0:T(8,128)S(1)} %get-tuple-element.69.send_ref), channel_id=1, source_target_pairs={{0,1},{1,0},{2,3},{3,2},{4,5},{5,4},{6,7},{7,6},{8,9},{9,8},{10,11... | collective-permute-start | bytes 811016 | tf_op jit(solution)/shard_map/ppermute | solution.py:428
  5.0 13.9 %collective-permute-start.1 = (f32[66,8,128]{2,1,0:T(8,128)S(1)}, f32[66,8,128]{2,1,0:T(8,128)S(1)}, u32[]{:S(2)}, u32[]{:S(2)}) collective-permute-start(f32[66,8,128]{2,1,0:T(8,128)S(1)} %get-tuple-element.71), channel_id=1, source_target_pairs={{0,2},{1,3},{2,4},{3,5},{4,6},{5,7},{6,8},{7,9},{8,10},{9,11},{10,... | collective-permute-start | bytes 811016 | tf_op jit(solution)/shard_map/ppermute | solution.py:432
  9.9 9.1 %collective-permute-start.2 = (f32[65,8,128]{2,1,0:T(8,128)S(1)}, f32[65,8,128]{2,1,0:T(8,128)S(1)}, u32[]{:S(2)}, u32[]{:S(2)}) collective-permute-start(f32[65,8,128]{2,1,0:T(8,128)S(1)} %get-tuple-element.72), channel_id=1, source_target_pairs={{0,4},{1,5},{2,6},{3,7},{4,8},{5,9},{6,10},{7,11},{8,12},{9,13},{1... | collective-permute-start | bytes 798728 | tf_op jit(solution)/shard_map/ppermute | solution.py:432
  19.1 1.6 %collective-permute-start.3 = (f32[65,8,128]{2,1,0:T(8,128)S(1)}, f32[65,8,128]{2,1,0:T(8,128)S(1)}, u32[]{:S(2)}, u32[]{:S(2)}) collective-permute-start(f32[65,8,128]{2,1,0:T(8,128)S(1)} %get-tuple-element.94), channel_id=1, source_target_pairs={{0,1},{1,0},{2,3},{3,2},{4,5},{5,4},{6,7},{7,6},{8,9},{9,8},{10,11... | collective-permute-start | bytes 798728 | tf_op jit(solution)/shard_map/ppermute | solution.py:428
  21.5 1.6 %collective-permute-start.4 = (f32[66,8,128]{2,1,0:T(8,128)S(1)}, f32[66,8,128]{2,1,0:T(8,128)S(1)}, u32[]{:S(2)}, u32[]{:S(2)}) collective-permute-start(f32[66,8,128]{2,1,0:T(8,128)S(1)} %get-tuple-element.95.send_ref), channel_id=1, source_target_pairs={{0,1},{1,0},{2,3},{3,2},{4,5},{5,4},{6,7},{7,6},{8,9},{9,8},{10,11... | collective-permute-start | bytes 811016 | tf_op jit(solution)/shard_map/ppermute | solution.py:428
  23.1 20.1 %collective-permute-start.5 = (f32[66,8,128]{2,1,0:T(8,128)S(1)}, f32[66,8,128]{2,1,0:T(8,128)S(1)}, u32[]{:S(2)}, u32[]{:S(2)}) collective-permute-start(f32[66,8,128]{2,1,0:T(8,128)S(1)} %get-tuple-element.97), channel_id=1, source_target_pairs={{0,14},{1,15},{2,0},{3,1},{4,2},{5,3},{6,4},{7,5},{8,6},{9,7},{10,... | collective-permute-start | bytes 811016 | tf_op jit(solution)/shard_map/ppermute | solution.py:438
  31.2 12.0 %collective-permute-start.6 = (f32[65,8,128]{2,1,0:T(8,128)S(1)}, f32[65,8,128]{2,1,0:T(8,128)S(1)}, u32[]{:S(2)}, u32[]{:S(2)}) collective-permute-start(f32[65,8,128]{2,1,0:T(8,128)S(1)} %get-tuple-element.98), channel_id=1, source_target_pairs={{0,12},{1,13},{2,14},{3,15},{4,0},{5,1},{6,2},{7,3},{8,4},{9,5},{1... | collective-permute-start | bytes 798728 | tf_op jit(solution)/shard_map/ppermute | solution.py:438
  31.7 10.2 %collective-permute-start.9 = (f32[8,128]{1,0:T(8,128)S(1)}, f32[8,128]{1,0:T(8,128)S(1)}, u32[]{:S(2)}, u32[]{:S(2)}) collective-permute-start(f32[8,128]{1,0:T(8,128)S(1)} %get-tuple-element.96.line_ref), channel_id=1, source_target_pairs={{0,2},{2,4},{4,6},{6,8},{8,10},{10,12},{12,14},{14,0},{16,18},{18,... | collective-permute-start | bytes 12296 | tf_op jit(solution)/shard_map/ppermute | solution.py:502
  33.8 9.4 %collective-permute-start.8 = (f32[8,128]{1,0:T(8,128)S(1)}, f32[8,128]{1,0:T(8,128)S(1)}, u32[]{:S(2)}, u32[]{:S(2)}) collective-permute-start(f32[8,128]{1,0:T(8,128)S(1)} %get-tuple-element.96.line_ref), channel_id=1, source_target_pairs={{0,6},{1,5},{2,8},{3,7},{4,10},{5,9},{6,12},{7,11},{8,14},{9,13},{... | collective-permute-start | bytes 12296 | tf_op jit(solution)/shard_map/ppermute | solution.py:502
  34.1 9.1 %collective-permute-start.7 = (f32[8,128]{1,0:T(8,128)S(1)}, f32[8,128]{1,0:T(8,128)S(1)}, u32[]{:S(2)}, u32[]{:S(2)}) collective-permute-start(f32[8,128]{1,0:T(8,128)S(1)} %get-tuple-element.96.line_ref), channel_id=1, source_target_pairs={{0,10},{1,9},{2,12},{3,11},{4,14},{5,13},{6,0},{7,15},{8,2},{9,1},... | collective-permute-start | bytes 12296 | tf_op jit(solution)/shard_map/ppermute | solution.py:502
  43.3 1.9 %collective-permute-start.10 = (f32[65,8,128]{2,1,0:T(8,128)S(1)}, f32[65,8,128]{2,1,0:T(8,128)S(1)}, u32[]{:S(2)}, u32[]{:S(2)}) collective-permute-start(f32[65,8,128]{2,1,0:T(8,128)S(1)} %get-tuple-element.117), channel_id=1, source_target_pairs={{0,1},{1,0},{2,3},{3,2},{4,5},{5,4},{6,7},{7,6},{8,9},{9,8},{10,11... | collective-permute-start | bytes 798728 | tf_op jit(solution)/shard_map/ppermute | solution.py:428

commit v10 on v9

--- a/solution.py
+++ b/solution.py
@@ -10,7 +10,7 @@
 BF16 = jnp.bfloat16
 PAD = 8
 STEPS = 2
-PIECES = 2
+PIECES = 4
 LIMIT = 24 << 20
 HBM = pl.BlockSpec(memory_space=pltpu.MemorySpace.HBM)
 VMEM = pl.BlockSpec(memory_space=pltpu.MemorySpace.VMEM)

time: 47.5 us -> 47.2 us (level)
  transfers between devices with their start and end apart: 11 -> 11, of which waited for: 5 -> 5; matrix products, arithmetic and copies ran while one was open for 0% -> 0% of each run, Pallas kernels for 23% -> 22%
where the time goes in v10:
time: 47.2 us; the launch traced here: 46.9 us
  starting transfers between devices  23.7 us (50%)
  Pallas kernels  16 us (34%)
  waiting for transfers between devices  6.46 us (14%)
  between operations  0.76 us (2%)
    pallas_call x12, Pallas kernels, call(): pl.pallas_call(kernel, out_shape=outs, in_specs=in_specs or [VMEM] * len(...  16 us
    ppermute x2, starting transfers between devices, turn(): lax.ppermute(x, 'seq', [(i, (i + by) % devices) for i in range(devices)])  8.55 us
    ppermute x2, starting transfers between devices, shift(): lax.ppermute(x, 'seq', [(i, i + by) for i in range(devices) if 0 <= i + b...  8.29 us
    ppermute x3, starting transfers between devices, far_squares(): lines.append(lax.ppermute(line, 'seq', pairs))  5.95 us
    ppermute x2, waiting for transfers between devices, shift(): lax.ppermute(x, 'seq', [(i, i + by) for i in range(devices) if 0 <= i + b...  2.71 us
    ppermute x4, waiting for transfers between devices, swap(): return lax.ppermute(x, 'seq', [(i, i ^ 1) for i in range(devices)])  2.4 us
    ppermute x3, waiting for transfers between devices, far_squares(): lines.append(lax.ppermute(line, 'seq', pairs))  1.35 us
  transfers between devices with their start and end apart: 11, of which 5 were waited for; matrix products, arithmetic and copies ran while one was open for 0% of the time, Pallas kernels for 22%

profile of v10, /device:TPU:0, one launch (start us, length us, event | category | flops | bytes accessed | tf_op | source)
XLA Modules:
  0.0 46.9 jit_solution(9820593328859554990)
XLA Ops:
  0.6 2.6 %shard_map.111 = (bf16[512,1024]{1,0:T(8,128)(2,1)S(1)}, f32[66,8,128]{2,1,0:T(8,128)S(1)}, bf16[96,512]{1,0:T(8,128)(2,1)S(1)}, bf16[96,512]{1,0:T(8,128)(2,1)S...) custom-call(s32[16]{0:T(128)} %lengths_hbm.1, ...), custom_call_target="tpu_custom_call" | custom-call | bytes 10641728 | tf_op jit(solution)/shard_map/pallas_call | solution.py:411
  3.3 0.5 %collective-permute-start = (f32[66,8,128]{2,1,0:T(8,128)S(1)}, f32[66,8,128]{2,1,0:T(8,128)S(1)}, u32[]{:S(2)}, u32[]{:S(2)}) collective-permute-start(f32[66,8,128]{2,1,0:T(8,128)S(1)} %get-tuple-element.69.send_ref), channel_id=1, source_target_pairs={{0,1},{1,0},{2,3},{3,2},{4,5},{5,4},{6,7},{7,6},{8,9},{9,8},{10,11... | collective-permute-start | bytes 811016 | tf_op jit(solution)/shard_map/ppermute | solution.py:428
  3.8 0.9 %shard_map.112 = (bf16[512,1024]{1,0:T(8,128)(2,1)S(1)}, f32[66,8,128]{2,1,0:T(8,128)S(1)}) custom-call(bf16[96,512]{1,0:T(8,128)(2,1)S(1)} %get-tuple-element.63.f3_ref, bf16[96,512]{1,0:T(8,128)(2,1)S(1)} %get-tuple-element.64.s3_ref, bf16[64,512]{1,0:T(8,128)(2,1)S(1)} %get-tuple-element.65.bm_ref, f32[8,2048]{1,0:T(8,128)S(1)} %get-tuple-element.66.rows_ref, ...), custom_call_target="tpu_custom_call" | custom-call | bytes 3743744 | tf_op jit(solution)/shard_map/pallas_call | solution.py:411
  4.7 0.3 collective-permute-done.got_ref
  5.0 4.8 %collective-permute-start.1 = (f32[66,8,128]{2,1,0:T(8,128)S(1)}, f32[66,8,128]{2,1,0:T(8,128)S(1)}, u32[]{:S(2)}, u32[]{:S(2)}) collective-permute-start(f32[66,8,128]{2,1,0:T(8,128)S(1)} %get-tuple-element.71), channel_id=1, source_target_pairs={{0,2},{1,3},{2,4},{3,5},{4,6},{5,7},{6,8},{7,9},{8,10},{9,11},{10,... | collective-permute-start | bytes 811016 | tf_op jit(solution)/shard_map/ppermute | solution.py:432
  9.9 3.5 %collective-permute-start.2 = (f32[65,8,128]{2,1,0:T(8,128)S(1)}, f32[65,8,128]{2,1,0:T(8,128)S(1)}, u32[]{:S(2)}, u32[]{:S(2)}) collective-permute-start(f32[65,8,128]{2,1,0:T(8,128)S(1)} %get-tuple-element.72), channel_id=1, source_target_pairs={{0,4},{1,5},{2,6},{3,7},{4,8},{5,9},{6,10},{7,11},{8,12},{9,13},{1... | collective-permute-start | bytes 798728 | tf_op jit(solution)/shard_map/ppermute | solution.py:432
  13.3 2.9 %shard_map.115 = (f32[512,2048]{1,0:T(8,128)S(1)}, bf16[512,512]{1,0:T(8,128)(2,1)S(1)}, f32[512,2048]{1,0:T(8,128)S(1)}, f32[512,2048]{1,0:T(8,128)S(1)}, bf16[...) custom-call(bf16[512,1024]{1,0:T(8,128)(2,1)S(1)} %get-tuple-element.74.xf_ref.x_ref, ...), custom_call_target="tpu_custom_call" | custom-call | flops 1073741824 | bytes 20201472 | tf_op jit(solution)/shard_map/pallas_call | solution.py:411
  16.3 2.7 %collective-permute-done.2.two_ref = f32[65,8,128]{2,1,0:T(8,128)S(1)} collective-permute-done((f32[65,8,128]{2,1,0:T(8,128)S(1)}, f32[65,8,128]{2,1,0:T(8,128)S(1)}, u32[]{:S(2)}, u32[]{:S(2)}) %collective-permute-start.2) | collective-permute-done | bytes 266272 | tf_op jit(solution)/shard_map/ppermute | solution.py:432
  19.0 0.0 collective-permute-done.1.one_ref
  19.0 0.1 shard_map.114
  19.1 0.1 collective-permute-start.3
  19.1 0.8 %shard_map.116 = (f32[512,1024]{1,0:T(8,128)S(1)}, bf16[512,1024]{1,0:T(8,128)(2,1)S(1)}, f32[66,8,128]{2,1,0:T(8,128)S(1)}) custom-call(f32[512,2048]{1,0:T(8,128)S(1)} %get-tuple-element.89.base_ref, f32[512,2048]{1,0:T(8,128)S(1)} %get-tuple-element.90.enter_ref, f32[8,2048]{1,0:T(8,128)S(1)} %get-tuple-element.66.rows_ref, ...), custom_call_target="tpu_custom_call" | custom-call | bytes 12333056 | tf_op jit(solution)/shard_map/pallas_call | solution.py:411
  20.0 0.7 %collective-permute-done.3.state_ref.other_ref = f32[65,8,128]{2,1,0:T(8,128)S(1)} collective-permute-done((f32[65,8,128]{2,1,0:T(8,128)S(1)}, f32[65,8,128]{2,1,0:T(8,128)S(1)}, u32[]{:S(2)}, u32[]{:S(2)}) %collective-permute-start.3) | collective-permute-done | bytes 266272 | tf_op jit(solution)/shard_map/ppermute | solution.py:428
  20.7 0.8 %shard_map.117 = (f32[512,1024]{1,0:T(8,128)S(1)}, bf16[512,1024]{1,0:T(8,128)(2,1)S(1)}, f32[66,8,128]{2,1,0:T(8,128)S(1)}) custom-call(f32[512,2048]{1,0:T(8,128)S(1)} %get-tuple-element.89.base_ref, f32[512,2048]{1,0:T(8,128)S(1)} %get-tuple-element.90.enter_ref, f32[8,2048]{1,0:T(8,128)S(1)} %get-tuple-element.66.rows_ref, ...), custom_call_target="tpu_custom_call" | custom-call | bytes 12603392 | tf_op jit(solution)/shard_map/pallas_call | solution.py:411
  21.5 0.2 collective-permute-start.4
  21.7 1.4 %collective-permute-done.4.got_ref = f32[66,8,128]{2,1,0:T(8,128)S(1)} collective-permute-done((f32[66,8,128]{2,1,0:T(8,128)S(1)}, f32[66,8,128]{2,1,0:T(8,128)S(1)}, u32[]{:S(2)}, u32[]{:S(2)}) %collective-permute-start.4) | collective-permute-done | bytes 270368 | tf_op jit(solution)/shard_map/ppermute | solution.py:428
  23.1 8.1 %collective-permute-start.5 = (f32[66,8,128]{2,1,0:T(8,128)S(1)}, f32[66,8,128]{2,1,0:T(8,128)S(1)}, u32[]{:S(2)}, u32[]{:S(2)}) collective-permute-start(f32[66,8,128]{2,1,0:T(8,128)S(1)} %get-tuple-element.97), channel_id=1, source_target_pairs={{0,14},{1,15},{2,0},{3,1},{4,2},{5,3},{6,4},{7,5},{8,6},{9,7},{10,... | collective-permute-start | bytes 811016 | tf_op jit(solution)/shard_map/ppermute | solution.py:438
  31.2 0.4 collective-permute-start.6
  31.7 2.1 %collective-permute-start.9 = (f32[8,128]{1,0:T(8,128)S(1)}, f32[8,128]{1,0:T(8,128)S(1)}, u32[]{:S(2)}, u32[]{:S(2)}) collective-permute-start(f32[8,128]{1,0:T(8,128)S(1)} %get-tuple-element.96.line_ref), channel_id=1, source_target_pairs={{0,2},{2,4},{4,6},{6,8},{8,10},{10,12},{12,14},{14,0},{16,18},{18,... | collective-permute-start | bytes 12296 | tf_op jit(solution)/shard_map/ppermute | solution.py:502
  33.8 0.3 collective-permute-start.8
  34.1 3.6 %collective-permute-start.7 = (f32[8,128]{1,0:T(8,128)S(1)}, f32[8,128]{1,0:T(8,128)S(1)}, u32[]{:S(2)}, u32[]{:S(2)}) collective-permute-start(f32[8,128]{1,0:T(8,128)S(1)} %get-tuple-element.96.line_ref), channel_id=1, source_target_pairs={{0,10},{1,9},{2,12},{3,11},{4,14},{5,13},{6,0},{7,15},{8,2},{9,1},... | collective-permute-start | bytes 12296 | tf_op jit(solution)/shard_map/ppermute | solution.py:502
  37.7 4.2 %shard_map.120 = (f32[512,1024]{1,0:T(8,128)S(1)}, f32[512,1024]{1,0:T(8,128)S(1)}, f32[64,512]{1,0:T(8,128)S(1)}, f32[64,512]{1,0:T(8,128)}) custom-call(f32[512,1024]{1,0:T(8,128)S(1)} %get-tuple-element.100.mmf_ref, f32[512,1024]{1,0:T(8,128)S(1)} %get-tuple-element.101.mmo_ref, bf16[512,1024]{1,0:T(8,128)(2,1)S(1)} %get-tuple-element.102.yf_ref, ...), custom_call_target="tpu_custom_call" | custom-call | flops 2147483648 | bytes 18309120 | tf_op jit(solution)/shard_map/pallas_call | solution.py:411
  41.9 0.0 collective-permute-done.9.refs_2_
  41.9 1.3 %collective-permute-done.8.refs_1_ = f32[8,128]{1,0:T(8,128)S(1)} collective-permute-done((f32[8,128]{1,0:T(8,128)S(1)}, f32[8,128]{1,0:T(8,128)S(1)}, u32[]{:S(2)}, u32[]{:S(2)}) %collective-permute-start.8) | collective-permute-done | bytes 4128 | tf_op jit(solution)/shard_map/ppermute | solution.py:502
  43.2 0.0 collective-permute-done.7.refs_0_
  43.2 0.0 collective-permute-done.6.two_ref
  43.2 0.0 collective-permute-done.5.one_ref
  43.2 0.1 shard_map.119
  43.3 0.1 collective-permute-start.10
  43.4 1.7 %shard_map.121 = (f32[512,2048]{1,0:T(8,128)}, f32[512,128]{1,0:T(8,128)S(1)}) custom-call(f32[512,1024]{1,0:T(8,128)S(1)} %get-tuple-element.110.g_ref, bf16[512,1024]{1,0:T(8,128)(2,1)S(1)} %get-tuple-element.75.xo_ref.x_ref, f32[512,2048]{1,0:T(8,128)S(1)} %get-tuple-element.105.sf_ref, f32[8,2048]{1,0:T(8,128)S(1)} %get-tuple-element.66.rows_ref, ...), custom_call_target="tpu_custom_call" | custom-call | bytes 12259328 | tf_op jit(solution)/shard_map/pallas_call | solution.py:411
  45.1 0.0 collective-permute-done.10.other_ref
  45.1 1.8 %shard_map.122 = (f32[512,2048]{1,0:T(8,128)}, f32[64,512]{1,0:T(8,128)}, f32[1,128]{1,0:T(1,128)}) custom-call(f32[512,2048]{1,0:T(8,128)} %get-tuple-element.113._gv_in, f32[512,1024]{1,0:T(8,128)S(1)} %get-tuple-element.114.g_ref, bf16[512,1024]{1,0:T(8,128)(2,1)S(1)} %get-tuple-element.74.xf_ref.x_ref, ...), custom_call_target="tpu_custom_call", output_to_operand_aliasing={{0}: (0, {})} | custom-call | bytes 16998912 | tf_op jit(solution)/shard_map/pallas_call | solution.py:411
  (2 shorter events, 0.1 us)
Async XLA Ops:
  3.3 1.7 %collective-permute-start = (f32[66,8,128]{2,1,0:T(8,128)S(1)}, f32[66,8,128]{2,1,0:T(8,128)S(1)}, u32[]{:S(2)}, u32[]{:S(2)}) collective-permute-start(f32[66,8,128]{2,1,0:T(8,128)S(1)} %get-tuple-element.69.send_ref), channel_id=1, source_target_pairs={{0,1},{1,0},{2,3},{3,2},{4,5},{5,4},{6,7},{7,6},{8,9},{9,8},{10,11... | collective-permute-start | bytes 811016 | tf_op jit(solution)/shard_map/ppermute | solution.py:428
  5.0 13.9 %collective-permute-start.1 = (f32[66,8,128]{2,1,0:T(8,128)S(1)}, f32[66,8,128]{2,1,0:T(8,128)S(1)}, u32[]{:S(2)}, u32[]{:S(2)}) collective-permute-start(f32[66,8,128]{2,1,0:T(8,128)S(1)} %get-tuple-element.71), channel_id=1, source_target_pairs={{0,2},{1,3},{2,4},{3,5},{4,6},{5,7},{6,8},{7,9},{8,10},{9,11},{10,... | collective-permute-start | bytes 811016 | tf_op jit(solution)/shard_map/ppermute | solution.py:432
  9.9 9.1 %collective-permute-start.2 = (f32[65,8,128]{2,1,0:T(8,128)S(1)}, f32[65,8,128]{2,1,0:T(8,128)S(1)}, u32[]{:S(2)}, u32[]{:S(2)}) collective-permute-start(f32[65,8,128]{2,1,0:T(8,128)S(1)} %get-tuple-element.72), channel_id=1, source_target_pairs={{0,4},{1,5},{2,6},{3,7},{4,8},{5,9},{6,10},{7,11},{8,12},{9,13},{1... | collective-permute-start | bytes 798728 | tf_op jit(solution)/shard_map/ppermute | solution.py:432
  19.1 1.6 %collective-permute-start.3 = (f32[65,8,128]{2,1,0:T(8,128)S(1)}, f32[65,8,128]{2,1,0:T(8,128)S(1)}, u32[]{:S(2)}, u32[]{:S(2)}) collective-permute-start(f32[65,8,128]{2,1,0:T(8,128)S(1)} %get-tuple-element.94), channel_id=1, source_target_pairs={{0,1},{1,0},{2,3},{3,2},{4,5},{5,4},{6,7},{7,6},{8,9},{9,8},{10,11... | collective-permute-start | bytes 798728 | tf_op jit(solution)/shard_map/ppermute | solution.py:428
  21.5 1.6 %collective-permute-start.4 = (f32[66,8,128]{2,1,0:T(8,128)S(1)}, f32[66,8,128]{2,1,0:T(8,128)S(1)}, u32[]{:S(2)}, u32[]{:S(2)}) collective-permute-start(f32[66,8,128]{2,1,0:T(8,128)S(1)} %get-tuple-element.95.send_ref), channel_id=1, source_target_pairs={{0,1},{1,0},{2,3},{3,2},{4,5},{5,4},{6,7},{7,6},{8,9},{9,8},{10,11... | collective-permute-start | bytes 811016 | tf_op jit(solution)/shard_map/ppermute | solution.py:428
  23.1 20.1 %collective-permute-start.5 = (f32[66,8,128]{2,1,0:T(8,128)S(1)}, f32[66,8,128]{2,1,0:T(8,128)S(1)}, u32[]{:S(2)}, u32[]{:S(2)}) collective-permute-start(f32[66,8,128]{2,1,0:T(8,128)S(1)} %get-tuple-element.97), channel_id=1, source_target_pairs={{0,14},{1,15},{2,0},{3,1},{4,2},{5,3},{6,4},{7,5},{8,6},{9,7},{10,... | collective-permute-start | bytes 811016 | tf_op jit(solution)/shard_map/ppermute | solution.py:438
  31.2 12.0 %collective-permute-start.6 = (f32[65,8,128]{2,1,0:T(8,128)S(1)}, f32[65,8,128]{2,1,0:T(8,128)S(1)}, u32[]{:S(2)}, u32[]{:S(2)}) collective-permute-start(f32[65,8,128]{2,1,0:T(8,128)S(1)} %get-tuple-element.98), channel_id=1, source_target_pairs={{0,12},{1,13},{2,14},{3,15},{4,0},{5,1},{6,2},{7,3},{8,4},{9,5},{1... | collective-permute-start | bytes 798728 | tf_op jit(solution)/shard_map/ppermute | solution.py:438
  31.7 10.2 %collective-permute-start.9 = (f32[8,128]{1,0:T(8,128)S(1)}, f32[8,128]{1,0:T(8,128)S(1)}, u32[]{:S(2)}, u32[]{:S(2)}) collective-permute-start(f32[8,128]{1,0:T(8,128)S(1)} %get-tuple-element.96.line_ref), channel_id=1, source_target_pairs={{0,2},{2,4},{4,6},{6,8},{8,10},{10,12},{12,14},{14,0},{16,18},{18,... | collective-permute-start | bytes 12296 | tf_op jit(solution)/shard_map/ppermute | solution.py:502
  33.8 9.4 %collective-permute-start.8 = (f32[8,128]{1,0:T(8,128)S(1)}, f32[8,128]{1,0:T(8,128)S(1)}, u32[]{:S(2)}, u32[]{:S(2)}) collective-permute-start(f32[8,128]{1,0:T(8,128)S(1)} %get-tuple-element.96.line_ref), channel_id=1, source_target_pairs={{0,6},{1,5},{2,8},{3,7},{4,10},{5,9},{6,12},{7,11},{8,14},{9,13},{... | collective-permute-start | bytes 12296 | tf_op jit(solution)/shard_map/ppermute | solution.py:502
  34.1 9.1 %collective-permute-start.7 = (f32[8,128]{1,0:T(8,128)S(1)}, f32[8,128]{1,0:T(8,128)S(1)}, u32[]{:S(2)}, u32[]{:S(2)}) collective-permute-start(f32[8,128]{1,0:T(8,128)S(1)} %get-tuple-element.96.line_ref), channel_id=1, source_target_pairs={{0,10},{1,9},{2,12},{3,11},{4,14},{5,13},{6,0},{7,15},{8,2},{9,1},... | collective-permute-start | bytes 12296 | tf_op jit(solution)/shard_map/ppermute | solution.py:502
  43.3 1.8 %collective-permute-start.10 = (f32[65,8,128]{2,1,0:T(8,128)S(1)}, f32[65,8,128]{2,1,0:T(8,128)S(1)}, u32[]{:S(2)}, u32[]{:S(2)}) collective-permute-start(f32[65,8,128]{2,1,0:T(8,128)S(1)} %get-tuple-element.117), channel_id=1, source_target_pairs={{0,1},{1,0},{2,3},{3,2},{4,5},{5,4},{6,7},{7,6},{8,9},{9,8},{10,11... | collective-permute-start | bytes 798728 | tf_op jit(solution)/shard_map/ppermute | solution.py:428
